TPU v7x, 512 devices: a whole 4x8x8 slice. The times are simulated.
512 devices in a mesh: dom: 128 (over y, z, core), rep: 4 (over x).
Axes of the slice: x: 4, y: 8, z: 8, core: 2. Of those that a mesh axis runs over, the one named last changes fastest.
Arguments:
- feats: bfloat16 [65536, 512], P('dom', 'rep'), may hold values from -6 to 6
- hist_one: bfloat16 [65536, 512], P('dom', 'rep'), may hold values from -6 to 6
- local_val: bfloat16 [65536, 128], P('dom'), may hold values from -0.375 to 0.375
- halo_val: bfloat16 [65536, 128], P('dom'), may hold values from -0.375 to 0.375
- halo_send: int32 [128, 128, 4], P('dom'), may hold values from 0 to 511
- halo_tile: int32 [128, 4], P('dom'), may hold values from 0 to 3, as said below
- tile_type: int32 [128, 4], P('dom'), may hold values from 0 to 7
- w_one: bfloat16 [512, 8, 512], P(None, None, 'rep'), may hold values from -0.25 to 0.25
- w_two: bfloat16 [512, 8, 512], P(None, None, 'rep'), may hold values from -0.25 to 0.25
- grad_out: bfloat16 [65536, 512], P('dom', 'rep'), may hold values from -6 to 6
Outputs:
- hidden_two: bfloat16 [65536, 512], P('dom', 'rep')
- history_one: bfloat16 [65536, 512], P('dom', 'rep')
- grad_w_one: float32 [512, 8, 512], P(None, None, 'rep')
- grad_w_two: float32 [512, 8, 512], P(None, None, 'rep')
Inputs may be any that keep to these rules, and one draw needn't show every extreme that they name: `halo_tile`: for each partition, every one of the 4 halo blocks is read by exactly 1 of its row blocks.
All inputs are finite; a program needn't handle non-finite values.
Results may differ from a plain program's by a relative error of at most 0.013.
Values may be sent and summed in bfloat16 or wider, within the bound.
No kernel may reach another device: no remote copies, remote signals or barrier semaphores. Data moves between devices by JAX's collectives and lax.ppermute only.
A program may use at most 64 MiB of HBM per device.

v0:
```python
import jax
import jax.numpy as jnp
from jax import lax
from jax.sharding import PartitionSpec as P


def slope_silu(value):
    sig = jax.nn.sigmoid(value)
    return sig * (1.0 + value * (1.0 - sig))


def pull_rows(table, send_rows):
    picked = jnp.take(table, send_rows, axis=0)
    landed = lax.all_to_all(picked, "dom", split_axis=0, concat_axis=0, tiled=True)
    return landed.reshape(-1, table.shape[1])


def aggregate(source, halo, local_blocks, halo_blocks, halo_pick):
    rows, tile, _ = local_blocks.shape
    width = source.shape[1]
    src = source.reshape(rows, tile, width)
    halo_tiles = jnp.take(halo.reshape(-1, tile, width), halo_pick, axis=0)
    total = jnp.einsum("jrk,jkc->jrc", local_blocks, src, preferred_element_type=jnp.float32)
    total = total + jnp.einsum(
        "jrk,jkc->jrc", halo_blocks, halo_tiles, preferred_element_type=jnp.float32
    )
    return total.astype(jnp.bfloat16)


def mix_layer(source, halo, local_blocks, halo_blocks, halo_pick):
    whole_source, whole_halo = (
        lax.all_gather(source, "rep", axis=1, tiled=True),
        lax.all_gather(halo, "rep", axis=1, tiled=True),
    )
    return aggregate(whole_source, whole_halo, local_blocks, halo_blocks, halo_pick)


def expert_forward(agg_full, weights, types):
    chosen = jnp.take(weights, types, axis=1)
    return jnp.einsum("jrd,djc->jrc", agg_full, chosen, preferred_element_type=jnp.float32)


def grad_term(agg_full, dz_rows, onehot):
    per_tile = jnp.einsum("jrd,jrc->jdc", agg_full, dz_rows, preferred_element_type=jnp.float32)
    return jnp.einsum("je,jdc->dec", onehot, per_tile)


def shards(
    feats, hist_one, local_val, halo_val, halo_send, halo_tile, tile_type, w_one, w_two, grad_out
):
    tile = local_val.shape[1]
    rows = feats.shape[0] // tile
    cols = feats.shape[1]
    experts = w_one.shape[1]
    local_blocks = local_val.reshape(rows, tile, tile)
    halo_blocks = halo_val.reshape(rows, tile, tile)
    halo_pick = halo_tile[0]
    types = tile_type[0]
    send_rows = halo_send[0]
    halo_first = pull_rows(feats, send_rows)
    agg_one = mix_layer(feats, halo_first, local_blocks, halo_blocks, halo_pick)
    z_one = expert_forward(agg_one, w_one, types)
    h_one = (feats.reshape(rows, tile, cols).astype(jnp.float32) + jax.nn.silu(z_one)).astype(
        jnp.bfloat16
    )
    halo_second = pull_rows(hist_one, send_rows)
    agg_two = mix_layer(h_one.reshape(-1, cols), halo_second, local_blocks, halo_blocks, halo_pick)
    z_two = expert_forward(agg_two, w_two, types)
    h_two = (h_one.astype(jnp.float32) + jax.nn.silu(z_two)).astype(jnp.bfloat16)
    onehot = (types[:, None] == jnp.arange(experts, dtype=jnp.int32)[None, :]).astype(jnp.float32)
    upstream = grad_out.reshape(rows, tile, cols).astype(jnp.float32)
    dz_two = (upstream * slope_silu(z_two)).astype(jnp.bfloat16)
    chosen_two = jnp.take(w_two, types, axis=1)
    partial_back = jnp.einsum(
        "jrc,djc->jrd", dz_two, chosen_two, preferred_element_type=jnp.float32
    )
    own_cols = lax.psum_scatter(
        partial_back.astype(jnp.bfloat16), "rep", scatter_dimension=2, tiled=True
    )
    dh_one = upstream + jnp.einsum(
        "jrk,jrc->jkc", local_blocks, own_cols, preferred_element_type=jnp.float32
    )
    dz_one = (dh_one * slope_silu(z_one)).astype(jnp.bfloat16)
    grad_one, grad_two = lax.psum(
        (grad_term(agg_one, dz_one, onehot), grad_term(agg_two, dz_two, onehot)), "dom"
    )
    return (h_two.reshape(-1, cols), h_one.reshape(-1, cols), grad_one, grad_two)


def solution(mesh):
    in_specs = (
        P("dom", "rep"),
        P("dom", "rep"),
        P("dom", None),
        P("dom", None),
        P("dom", None, None),
        P("dom", None),
        P("dom", None),
        P(None, None, "rep"),
        P(None, None, "rep"),
        P("dom", "rep"),
    )
    out_specs = (P("dom", "rep"), P("dom", "rep"), P(None, None, "rep"), P(None, None, "rep"))
    return jax.shard_map(shards, mesh=mesh, in_specs=in_specs, out_specs=out_specs, check_vma=False)
```

profile of v0, /device:TPU:1, one launch (start us, length us, event | category | flops | bytes accessed | tf_op | source)
XLA Modules:
  0.0 363.9 jit_solution(2959704878794870880)
XLA Ops:
  7.2 0.8 compare_and_fusion.2
  8.0 0.7 compare_select_fusion
  9.0 2.0 gather_fusion.3
  11.0 1.3 gather_fusion
  12.4 0.9 broadcast_select_fusion
  13.3 18.4 %all-to-all-start = ((bf16[128,4,128]{2,1,0:T(4,128)(2,1)}), bf16[128,4,128]{2,1,0:T(4,128)(2,1)S(1)}, u32[]{:S(2)}, u32[]{:S(2)}) async-start(bf16[128,4,128]{2,1,0:T(4,128)(2,1)} %get-tuple-element.10), calls=%async_computation | async-start | bytes 262144 | tf_op jit(solution)/shard_map/all_to_all | solution.py:14
  31.8 12.6 %all_gather.12 = bf16[512,512]{1,0:T(8,128)(2,1)} all-gather(bf16[512,128]{1,0:T(8,128)(2,1)S(1)} %copy-done.2), channel_id=1, replica_groups=mesh['dom'=128,'rep'=4] {'rep'}, dimensions={1}, use_global_device_ids=true | all-gather | bytes 655360 | tf_op jit(solution)/shard_map/all_gather | solution.py:32
  44.4 2.9 gather_fusion.5
  47.3 2.9 gather_fusion.2
  50.3 1.5 select_bitcast_fusion
  52.1 16.2 %all-to-all-start.1 = ((bf16[128,4,128]{2,1,0:T(4,128)(2,1)}), bf16[128,4,128]{2,1,0:T(4,128)(2,1)S(1)}, u32[]{:S(2)}, u32[]{:S(2)}) async-start(bf16[128,4,128]{2,1,0:T(4,128)(2,1)} %get-tuple-element.9), calls=%async_computation.1 | async-start | bytes 262144 | tf_op jit(solution)/shard_map/all_to_all | solution.py:14
  68.4 11.6 %all_gather.13 = bf16[512,512]{1,0:T(8,128)(2,1)S(1)} all-gather(bf16[512,128]{1,0:T(8,128)(2,1)S(1)} %bitcast.82), channel_id=1, replica_groups=mesh['dom'=128,'rep'=4] {'rep'}, dimensions={1}, use_global_device_ids=true | all-gather | bytes 655360 | tf_op jit(solution)/shard_map/all_gather | solution.py:33
  80.0 0.5 all-to-all-done.1
  80.5 12.5 %all_gather.15 = bf16[512,512]{1,0:T(8,128)(2,1)} all-gather(bf16[512,128]{1,0:T(8,128)(2,1)S(1)} %bitcast.83), channel_id=1, replica_groups=mesh['dom'=128,'rep'=4] {'rep'}, dimensions={1}, use_global_device_ids=true | all-gather | bytes 655360 | tf_op jit(solution)/shard_map/all_gather | solution.py:33
  93.0 0.6 gather_fusion.1
  93.6 1.6 gather_fusion.4
  95.3 0.4 fusion.2
  95.7 0.6 copy-done.8
  96.6 11.1 %all_gather.14 = bf16[512,512]{1,0:T(8,128)(2,1)S(1)} all-gather(bf16[512,128]{1,0:T(8,128)(2,1)S(1)} %bitcast.89), channel_id=1, replica_groups=mesh['dom'=128,'rep'=4] {'rep'}, dimensions={1}, use_global_device_ids=true | all-gather | bytes 655360 | tf_op jit(solution)/shard_map/all_gather | solution.py:32
  108.1 0.4 fusion.1
  108.8 1.1 add_convert_fusion
  109.9 1.3 convolution_convert_fusion
  111.5 0.9 copy.77
  112.4 1.3 fusion.38
  113.8 1.9 convolution_bitcast_fusion
  115.7 26.3 %reduce-scatter.4.cloned.1.call-done = bf16[128,512]{1,0:T(8,128)(2,1)} async-done(((bf16[512,512]{1,0:T(8,128)(2,1)}), bf16[128,512]{1,0:T(8,128)(2,1)}) %reduce-scatter.4.cloned.1.call-update) | async-done | bytes 131088
  141.9 0.9 reshape.147
  142.9 0.5 fusion.6
  143.4 1.9 convolution_bitcast_fusion.1
  145.3 207.2 %all-reduce.3.cloned.1.call-done = (f32[512,8,128]{2,1,0:T(8,128)}, f32[512,8,128]{2,1,0:T(8,128)}) async-done(((f32[512,8,128]{2,1,0:T(8,128)}, f32[512,8,128]{2,1,0:T(8,128)}), (f32[512,8,128]{2,1,0:T(8,128)}, f32[512,8,128]{2,1,0:T(8,128)})) %all-reduce.3.cloned.1.call-update) | async-done | bytes 4194320 | tf_op jit(solution)/shard_map/psum | solution.py:84
  352.6 3.2 copy.80
  355.8 1.3 copy.81
  (50 shorter events, 2.1 us)
Async XLA Ops:
  7.2 37.2 %copy-start = (bf16[512,8,128]{2,1,0:T(8,128)(2,1)S(1)}, bf16[512,8,128]{2,1,0:T(8,128)(2,1)}, u32[]{:S(2)}) copy-start(bf16[512,8,128]{2,1,0:T(8,128)(2,1)} %param.24) | copy-start | bytes 3145732
  7.2 3.9 %copy-start.2 = (bf16[512,128]{1,0:T(8,128)(2,1)S(1)}, bf16[512,128]{1,0:T(8,128)(2,1)}, u32[]{:S(2)}) copy-start(bf16[512,128]{1,0:T(8,128)(2,1)} %param.16) | copy-start | bytes 393220
  7.2 24.6 %copy-start.15 = (s32[1,4]{1,0:T(1,128)S(1)}, s32[1,4]{1,0:T(1,128)}, u32[]{:S(2)}) copy-start(s32[1,4]{1,0:T(1,128)} %param.21) | copy-start | bytes 52
  7.2 24.6 %copy-start.13 = (s32[1,4]{1,0:T(1,128)S(1)}, s32[1,4]{1,0:T(1,128)}, u32[]{:S(2)}) copy-start(s32[1,4]{1,0:T(1,128)} %param.22) | copy-start | bytes 52
  13.3 38.8 %all-to-all-start = ((bf16[128,4,128]{2,1,0:T(4,128)(2,1)}), bf16[128,4,128]{2,1,0:T(4,128)(2,1)S(1)}, u32[]{:S(2)}, u32[]{:S(2)}) async-start(bf16[128,4,128]{2,1,0:T(4,128)(2,1)} %get-tuple-element.10), calls=%async_computation | async-start | bytes 262144 | tf_op jit(solution)/shard_map/all_to_all | solution.py:14
  44.4 3.0 copy-start.1
  50.3 1.5 copy-start.3
  50.3 1.5 copy-start.10
  52.1 43.2 %copy-start.9 = (bf16[512,128]{1,0:T(8,128)(2,1)S(1)}, bf16[512,128]{1,0:T(8,128)(2,1)}, u32[]{:S(2)}) copy-start(bf16[512,128]{1,0:T(8,128)(2,1)} %param.19) | copy-start | bytes 393220
  52.1 28.4 %all-to-all-start.1 = ((bf16[128,4,128]{2,1,0:T(4,128)(2,1)}), bf16[128,4,128]{2,1,0:T(4,128)(2,1)S(1)}, u32[]{:S(2)}, u32[]{:S(2)}) async-start(bf16[128,4,128]{2,1,0:T(4,128)(2,1)} %get-tuple-element.9), calls=%async_computation.1 | async-start | bytes 262144 | tf_op jit(solution)/shard_map/all_to_all | solution.py:14
  68.3 73.6 %reduce-scatter.4.cloned.1.call-start = ((), (), s32[]{:S(2)}) async-start(), calls=%async_computation.3 | async-start | bytes 655360
  95.2 1.0 copy-start.8
  95.6 1.0 copy-start.6
  95.7 12.1 %copy-start.11 = (bf16[512,128]{1,0:T(8,128)(2,1)S(1)}, bf16[512,128]{1,0:T(8,128)(2,1)}, u32[]{:S(2)}) copy-start(bf16[512,128]{1,0:T(8,128)(2,1)} %param.18) | copy-start | bytes 393220
  96.6 11.9 %copy-start.12 = (bf16[4,128,128]{2,1,0:T(8,128)(2,1)}, bf16[4,128,128]{2,1,0:T(8,128)(2,1)S(1)}, u32[]{:S(2)}) copy-start(bf16[4,128,128]{2,1,0:T(8,128)(2,1)S(1)} %get-tuple-element.13) | copy-start | bytes 393220
  107.7 1.0 copy-start.5
  108.1 1.8 copy-start.14
  112.4 30.5 %copy-start.7 = (bf16[4,128,512]{2,1,0:T(8,128)(2,1)S(1)}, bf16[4,128,512]{2,1,0:T(8,128)(2,1)}, u32[]{:S(2)}) copy-start(bf16[4,128,512]{2,1,0:T(8,128)(2,1)} %copy-done.6) | copy-start | bytes 1572868
  112.4 240.2 %all-reduce.3.cloned.1.call-start = ((), (), s32[]{:S(2)}) async-start(), calls=%async_computation.4 | async-start | bytes 8388608 | tf_op jit(solution)/shard_map/psum | solution.py:84
  352.6 3.2 copy-start.4
Sparse Core Ops, SparseCore 0:
  112.5 29.4 reduce-scatter.3
  145.9 206.6 all-reduce.2
where the time goes:
time: 366 us; the launch traced here: 364 us
  waiting for transfers between devices  234 us (64%)
  blocking collectives  47.8 us (13%)
  starting transfers between devices  34.7 us (9%)
  local copies, waits for them, and re-layouts  19.3 us (5%)
  between operations  14.4 us (4%)
  matrix products  9.73 us (3%)
  other arithmetic  3.91 us (1%)
    psum x1, waiting for transfers between devices, shards(): lax.psum((grad_term(agg_one, dz_one, onehot), grad_term(agg_two, dz_two,...  207 us
    all_to_all x2, starting transfers between devices, pull_rows(): lax.all_to_all(picked, 'dom', split_axis=0, concat_axis=0, tiled=True)  34.6 us
    unnamed x3, waiting for transfers between devices  26.3 us
    all_gather x2, blocking collectives, mix_layer(): lax.all_gather(halo, 'rep', axis=1, tiled=True)  24.1 us
    all_gather x2, blocking collectives, mix_layer(): lax.all_gather(source, 'rep', axis=1, tiled=True)  23.6 us
    unnamed x37, local copies, waits for them, and re-layouts  7.58 us
  transfers between devices with their start and end apart: 4, of which 3 were waited for; matrix products, arithmetic and copies ran while one was open for 3% of the time, Pallas kernels for 0%

commit v1 on v0

v1 whole, which is shorter than its diff:
```python
import jax
import jax.numpy as jnp
import numpy as np
from jax import lax
from jax.sharding import Mesh, PartitionSpec as P

DOM = ("y", "z", "c")
BF = jnp.bfloat16
F32 = jnp.float32


def slope_silu(value):
    sig = jax.nn.sigmoid(value)
    return sig * (1.0 + value * (1.0 - sig))


def dot(spec, a, b):
    return jnp.einsum(spec, a, b, preferred_element_type=F32)


def spread_rep(rows):
    copies = jnp.broadcast_to(rows[None], (4,) + rows.shape)
    return lax.all_to_all(copies, "rep", split_axis=0, concat_axis=0, tiled=True)


def shards(
    feats, hist_one, local_val, halo_val, halo_send, halo_tile, tile_type, w_one, w_two, grad_out
):
    tile = local_val.shape[1]
    rows = feats.shape[0] // tile
    cols = feats.shape[1]
    width, experts, _ = w_one.shape
    reps = width // cols
    parts, cap = halo_send.shape[1], halo_send.shape[2]
    nodes = feats.shape[0]
    local_blocks = local_val.reshape(rows, tile, tile)
    halo_blocks = halo_val.reshape(rows, tile, tile)
    halo_pick = halo_tile[0]
    types = tile_type[0]
    send_rows = halo_send[0]
    code = jnp.broadcast_to(types.astype(F32)[:, None, None], (rows, 4, 128)).reshape(16, 128)
    all_types = lax.all_gather(code, DOM, axis=0, tiled=False)[:, ::4, 0]

    index = jnp.stack([send_rows, send_rows + nodes], axis=1).reshape(-1)
    pick = (index[:, None] == jnp.arange(2 * nodes, dtype=jnp.int32)[None, :]).astype(BF)
    table = jnp.concatenate([feats, hist_one], axis=0)
    picked = dot("ab,bc->ac", pick, table).astype(BF).reshape(parts, 2 * cap, cols)
    landed = lax.all_to_all(picked, DOM, split_axis=0, concat_axis=0, tiled=True)
    landed = landed.reshape(rows, 2 * tile, cols)
    order = np.zeros((2, tile, 2 * tile), np.float32)
    for t in range(2):
        for k in range(tile):
            order[t, k, (k // cap) * 2 * cap + t * cap + k % cap] = 1.0
    wide = dot("jrk,tkm->tjrm", halo_blocks, jnp.asarray(order, BF)).astype(BF)
    halo = jnp.take(landed, halo_pick, axis=0)

    source = feats.reshape(rows, tile, cols)
    agg_own = (dot("jrk,jkc->jrc", local_blocks, source) + dot("jrk,jkc->jrc", wide[0], halo)).astype(BF)
    agg_one = spread_rep(agg_own.reshape(nodes, cols)).reshape(reps, rows, tile, cols)
    pick_one = jnp.take(w_one, types, axis=1).reshape(reps, cols, rows, cols)
    z_one = dot("qjrd,qdjc->jrc", agg_one, pick_one)
    h_one = (source.astype(F32) + jax.nn.silu(z_one)).astype(BF)

    agg_own = (dot("jrk,jkc->jrc", local_blocks, h_one) + dot("jrk,jkc->jrc", wide[1], halo)).astype(BF)
    agg_two = spread_rep(agg_own.reshape(nodes, cols)).reshape(reps, rows, tile, cols)
    pick_two = jnp.take(w_two, types, axis=1).reshape(reps, cols, rows, cols)
    z_two = dot("qjrd,qdjc->jrc", agg_two, pick_two)
    h_two = (h_one.astype(F32) + jax.nn.silu(z_two)).astype(BF)
    upstream = grad_out.reshape(rows, tile, cols).astype(F32)
    dz_two = (upstream * slope_silu(z_two)).astype(BF)
    partial_back = dot("jrc,qdjc->qjrd", dz_two, pick_two).astype(BF).reshape(reps, nodes, cols)
    partial_back = lax.all_to_all(partial_back, "rep", split_axis=0, concat_axis=0, tiled=True)
    dagg = jnp.sum(partial_back.astype(F32), axis=0).astype(BF).reshape(rows, tile, cols)
    dh_one = upstream + dot("jrk,jrc->jkc", local_blocks, dagg)
    dz_one = (dh_one * slope_silu(z_one)).astype(BF)

    half = parts // 2
    own = width // half
    tiles = []
    for agg, dz in ((agg_one, dz_one), (agg_two, dz_two)):
        part = dot("qjrd,jrc->jqdc", agg, dz).astype(BF)
        tiles.append(part.reshape(rows, half, own, cols).transpose(1, 0, 2, 3))
    sent = jnp.concatenate(tiles, axis=0)
    got = lax.all_to_all(sent, DOM, split_axis=0, concat_axis=0, tiled=True)
    onehot = (
        all_types[:, :, None] == jnp.arange(experts, dtype=F32)[None, None, :]
    ).astype(BF)
    mine = dot("pje,pjdc->dec", onehot, got).astype(BF).reshape(own * experts, cols)

    copies = jnp.broadcast_to(mine[None], (half,) + mine.shape)
    same = lax.all_to_all(copies, ("y", "z"), split_axis=0, concat_axis=0, tiled=True)
    other = lax.ppermute(same, "c", [(0, 1), (1, 0)])
    core = lax.axis_index("c")
    even = jnp.where(core == 0, same, other)
    odd = jnp.where(core == 0, other, same)
    both = jnp.stack([even, odd], axis=1).reshape(2, width, experts, cols).astype(F32)
    return (h_two.reshape(-1, cols), h_one.reshape(-1, cols), both[0], both[1])


def solution(mesh):
    fine = Mesh(mesh.devices.reshape(8, 8, 2, 4), ("y", "z", "c", "rep"))
    in_specs = (
        P(DOM, "rep"),
        P(DOM, "rep"),
        P(DOM, None),
        P(DOM, None),
        P(DOM, None, None),
        P(DOM, None),
        P(DOM, None),
        P(None, None, "rep"),
        P(None, None, "rep"),
        P(DOM, "rep"),
    )
    out_specs = (P(DOM, "rep"), P(DOM, "rep"), P(None, None, "rep"), P(None, None, "rep"))
    return jax.shard_map(shards, mesh=fine, in_specs=in_specs, out_specs=out_specs, check_vma=False)
```

time: 366 us -> 409 us (1.12)
  blocking collectives: 47.8 us -> 308 us
  waiting for transfers between devices: 234 us -> 20.2 us
  starting transfers between devices: 34.7 us -> 47.8 us
  between operations: 14.4 us -> 1.66 us
  local copies, waits for them, and re-layouts: 19.3 us -> 14.5 us
    unnamed x0 -> x1, blocking collectives: none -> 267 us
    psum x1 -> x0, waiting for transfers between devices: 207 us -> none  [shards(): lax.psum((grad_term(agg_one, dz_one, onehot), grad_term(agg_two, dz_two,...]
    all_gather x4 -> x0, blocking collectives: 47.8 us -> none  [the longest x2 24.1 us: mix_layer(): lax.all_gather(halo, 'rep', axis=1, tiled=True)]
    all_to_all x0 -> x2, blocking collectives: none -> 40.2 us  [the longest x1 30.9 us: shards(): lax.all_to_all(copies, ('y', 'z'), split_axis=0, concat_axis=0, tiled=True)]
    unnamed x3 -> x0, waiting for transfers between devices: 26.3 us -> none
    all_to_all x2 -> x4, waiting for transfers between devices: 0.53 us -> 18 us  [the longest x1 6.32 us: shards(): lax.all_to_all(partial_back, 'rep', split_axis=0, concat_axis=0, tiled=True)]
    ppermute x0 -> x1, starting transfers between devices: none -> 7.6 us  [shards(): other = lax.ppermute(same, 'c', [(0, 1), (1, 0)])]
    unnamed x37 -> x21, local copies, waits for them, and re-layouts: 7.58 us -> 1.6 us
  transfers between devices with their start and end apart: 4 -> 5, of which waited for: 3 -> 4; matrix products, arithmetic and copies ran while one was open for 3% -> 3% of each run, Pallas kernels for 0% -> 0%
where the time goes in v1:
time: 409 us; the launch traced here: 408 us
  blocking collectives  308 us (75%)
  starting transfers between devices  47.8 us (12%)
  waiting for transfers between devices  20.2 us (5%)
  local copies, waits for them, and re-layouts  14.5 us (4%)
  matrix products  11 us (3%)
  other arithmetic  5.12 us (1%)
    unnamed x1, blocking collectives  267 us
    all_to_all x1, blocking collectives, shards(): lax.all_to_all(copies, ('y', 'z'), split_axis=0, concat_axis=0, tiled=True)  30.9 us
    all_to_all x1, starting transfers between devices, shards(): lax.all_to_all(picked, DOM, split_axis=0, concat_axis=0, tiled=True)  18.4 us
    all_to_all x1, starting transfers between devices, shards(): got = lax.all_to_all(sent, DOM, split_axis=0, concat_axis=0, tiled=True)  14 us
    dot_general x12, matrix products, dot(): return jnp.einsum(spec, a, b, preferred_element_type=F32)  11 us
    all_to_all x1, blocking collectives, spread_rep(): lax.all_to_all(copies, 'rep', split_axis=0, concat_axis=0, tiled=True)  9.33 us
  transfers between devices with their start and end apart: 5, of which 4 were waited for; matrix products, arithmetic and copies ran while one was open for 3% of the time, Pallas kernels for 0%

profile of v1, /device:TPU:1, one launch (start us, length us, event | category | flops | bytes accessed | tf_op | source)
XLA Modules:
  0.0 407.9 jit_solution(5974419423795127033)
XLA Ops:
  0.7 0.8 broadcast_add_fusion
  1.4 0.7 pad_add_fusion
  2.5 2.5 fusion.5
  5.0 18.4 %all-to-all-start = ((bf16[128,8,128]{2,1,0:T(8,128)(2,1)}), bf16[128,8,128]{2,1,0:T(8,128)(2,1)S(1)}, u32[]{:S(2)}, u32[]{:S(2)}) async-start(bf16[128,8,128]{2,1,0:T(8,128)(2,1)} %fusion.5), calls=%async_computation | async-start | bytes 524288 | tf_op jit(solution)/shard_map/all_to_all | solution.py:48
  23.5 2.9 gather_fusion.2
  26.5 2.9 gather_fusion.1
  29.4 1.1 fusion.43
  30.5 1.3 fusion.2
  31.8 5.9 %all-to-all-done = bf16[128,8,128]{2,1,0:T(8,128)(2,1)S(1)} async-done(((bf16[128,8,128]{2,1,0:T(8,128)(2,1)}), bf16[128,8,128]{2,1,0:T(8,128)(2,1)S(1)}, u32[]{:S(2)}, u32[]{:S(2)}) %all-to-all-start) | async-done | bytes 262176 | tf_op jit(solution)/shard_map/all_to_all | solution.py:48
  37.6 0.6 gather_fusion
  38.6 0.9 broadcast_in_dim.55
  39.4 4.2 %all-to-all-start.1 = ((bf16[4,512,128]{2,1,0:T(8,128)(2,1)}), bf16[4,512,128]{2,1,0:T(8,128)(2,1)}, u32[]{:S(2)}, u32[]{:S(2)}) async-start(bf16[4,512,128]{2,1,0:T(8,128)(2,1)} %broadcast_in_dim.55), calls=%async_computation.1 | async-start | bytes 1048576 | tf_op jit(solution)/shard_map/all_to_all | solution.py:23
  43.6 1.5 broadcast_select_fusion
  45.1 5.8 %all-to-all-done.1 = bf16[4,512,128]{2,1,0:T(8,128)(2,1)} async-done(((bf16[4,512,128]{2,1,0:T(8,128)(2,1)}), bf16[4,512,128]{2,1,0:T(8,128)(2,1)}, u32[]{:S(2)}, u32[]{:S(2)}) %all-to-all-start.1) | async-done | bytes 524320 | tf_op jit(solution)/shard_map/all_to_all | solution.py:23
  50.9 1.5 add_convert_fusion.1
  53.0 9.3 %all_to_all.30 = bf16[4,512,128]{2,1,0:T(8,128)(2,1)S(1)} all-to-all(bf16[4,512,128]{2,1,0:T(8,128)(2,1)S(1)} %broadcast_in_dim.57), channel_id=1, replica_groups=mesh['y'=8,'z'=8,'c'=2,'rep'=4] {'rep'}, dimensions={0} | all-to-all | bytes 1048576 | tf_op jit(solution)/shard_map/all_to_all | solution.py:23
  62.3 1.0 add_convert_fusion
  63.6 0.8 copy.61
  64.5 3.7 all-to-all-start.3
  68.1 0.4 convolution_convert_fusion
  68.5 6.3 %all-to-all-done.3 = bf16[4,512,128]{2,1,0:T(8,128)(2,1)S(1)} async-done(((bf16[4,512,128]{2,1,0:T(8,128)(2,1)}), bf16[4,512,128]{2,1,0:T(8,128)(2,1)S(1)}, u32[]{:S(2)}, u32[]{:S(2)}) %all-to-all-start.3) | async-done | bytes 524320 | tf_op jit(solution)/shard_map/all_to_all | solution.py:72
  74.9 1.5 convolution_convert_fusion.1
  76.5 1.4 copy_bitcast_fusion
  77.8 1.6 pad_maximum_fusion
  79.5 14.0 %all-to-all-start.4 = ((bf16[128,4,8,128]{3,1,2,0:T(4,128)(2,1)}), bf16[128,4,8,128]{3,1,2,0:T(4,128)(2,1)S(1)}, u32[]{:S(2)}, u32[]{:S(2)}) async-start(bf16[128,4,8,128]{3,1,2,0:T(4,128)(2,1)} %pad_maximum_fusion), calls=%async_computation.4 | async-start | bytes 2097152 | tf_op jit(solution)/shard_map/all_to_all | solution.py:84
  93.6 1.3 dynamic-slice
  95.8 267.3 %all-reduce = f32[2048]{0:T(1024)S(1)} all-reduce(f32[2048]{0:T(1024)S(1)} %dynamic-update-slice), channel_id=3, replica_groups=mesh['y'=8,'z'=8,'c'=2,'rep'=4] {'y','z','c'}, use_global_device_ids=true, to_apply=%add | all-reduce | flops 2048 | bytes 16384
  363.5 0.7 fusion.13
  364.4 30.9 %all_to_all.31 = bf16[64,64,128]{2,1,0:T(8,128)(2,1)S(1)} all-to-all(bf16[64,64,128]{2,1,0:T(8,128)(2,1)S(1)} %broadcast_in_dim.62), channel_id=1, replica_groups=mesh['y'=8,'z'=8,'c'=2,'rep'=4] {'y','z'}, dimensions={0} | all-to-all | bytes 2097152 | tf_op jit(solution)/shard_map/all_to_all | solution.py:91
  395.3 7.6 %collective-permute-start = (bf16[64,64,128]{2,1,0:T(8,128)(2,1)S(1)}, bf16[64,64,128]{2,1,0:T(8,128)(2,1)S(1)}, u32[]{:S(2)}, u32[]{:S(2)}) collective-permute-start(bf16[64,64,128]{2,1,0:T(8,128)(2,1)S(1)} %all_to_all.31), channel_id=1, source_target_pairs={{0,4},{4,0},{1,5},{5,1},{2,6},{6,2},{3,7},{7,3},{8,12},{12,8},{9,1... | collective-permute-start | bytes 3145736 | tf_op jit(solution)/shard_map/ppermute | solution.py:92
  402.9 2.3 collective-permute-done
  405.6 2.3 fusion.42
  (44 shorter events, 3.0 us)
Async XLA Ops:
  0.6 22.9 %copy-start = (bf16[512,8,128]{2,1,0:T(8,128)(2,1)S(1)}, bf16[512,8,128]{2,1,0:T(8,128)(2,1)}, u32[]{:S(2)}) copy-start(bf16[512,8,128]{2,1,0:T(8,128)(2,1)} %param.21) | copy-start | bytes 3145732
  0.6 22.8 %copy-start.7 = (s32[1,4]{1,0:T(1,128)S(1)}, s32[1,4]{1,0:T(1,128)}, u32[]{:S(2)}) copy-start(s32[1,4]{1,0:T(1,128)} %param.18) | copy-start | bytes 52
  0.7 22.8 %copy-start.8 = (s32[1,4]{1,0:T(1,128)S(1)}, s32[1,4]{1,0:T(1,128)}, u32[]{:S(2)}) copy-start(s32[1,4]{1,0:T(1,128)} %param.19) | copy-start | bytes 52
  5.0 32.7 %all-to-all-start = ((bf16[128,8,128]{2,1,0:T(8,128)(2,1)}), bf16[128,8,128]{2,1,0:T(8,128)(2,1)S(1)}, u32[]{:S(2)}, u32[]{:S(2)}) async-start(bf16[128,8,128]{2,1,0:T(8,128)(2,1)} %fusion.5), calls=%async_computation | async-start | bytes 524288 | tf_op jit(solution)/shard_map/all_to_all | solution.py:48
  23.5 3.0 copy-start.1
  26.5 3.0 copy-start.3
  38.5 12.4 %copy-start.4 = (bf16[512,128]{1,0:T(8,128)(2,1)S(1)}, bf16[512,128]{1,0:T(8,128)(2,1)}, u32[]{:S(2)}) copy-start(bf16[512,128]{1,0:T(8,128)(2,1)} %param.13) | copy-start | bytes 393220
  39.4 11.5 %all-to-all-start.1 = ((bf16[4,512,128]{2,1,0:T(8,128)(2,1)}), bf16[4,512,128]{2,1,0:T(8,128)(2,1)}, u32[]{:S(2)}, u32[]{:S(2)}) async-start(bf16[4,512,128]{2,1,0:T(8,128)(2,1)} %broadcast_in_dim.55), calls=%async_computation.1 | async-start | bytes 1048576 | tf_op jit(solution)/shard_map/all_to_all | solution.py:23
  52.4 10.9 %copy-start.5 = (bf16[4,128,128]{2,1,0:T(8,128)(2,1)}, bf16[4,128,128]{2,1,0:T(8,128)(2,1)S(1)}, u32[]{:S(2)}) copy-start(bf16[4,128,128]{2,1,0:T(8,128)(2,1)S(1)} %get-tuple-element.11) | copy-start | bytes 393220
  52.4 9.9 %copy-start.2 = (bf16[4,512,128]{2,0,1:T(4,128)(2,1)S(1)}, bf16[4,512,128]{2,0,1:T(4,128)(2,1)}, u32[]{:S(2)}) copy-start(bf16[4,512,128]{2,0,1:T(4,128)(2,1)} %get-tuple-element.9) | copy-start | bytes 1572868
  52.9 10.4 %copy-start.6 = (bf16[512,128]{1,0:T(8,128)(2,1)S(1)}, bf16[512,128]{1,0:T(8,128)(2,1)}, u32[]{:S(2)}) copy-start(bf16[512,128]{1,0:T(8,128)(2,1)} %param.22) | copy-start | bytes 393220
  64.5 10.4 %all-to-all-start.3 = ((bf16[4,512,128]{2,1,0:T(8,128)(2,1)}), bf16[4,512,128]{2,1,0:T(8,128)(2,1)S(1)}, u32[]{:S(2)}, u32[]{:S(2)}) async-start(bf16[4,512,128]{2,1,0:T(8,128)(2,1)} %bitcast.35), calls=%async_computation.3 | async-start | bytes 1048576 | tf_op jit(solution)/shard_map/all_to_all | solution.py:72
  79.5 284.0 %all-to-all-start.4 = ((bf16[128,4,8,128]{3,1,2,0:T(4,128)(2,1)}), bf16[128,4,8,128]{3,1,2,0:T(4,128)(2,1)S(1)}, u32[]{:S(2)}, u32[]{:S(2)}) async-start(bf16[128,4,8,128]{3,1,2,0:T(4,128)(2,1)} %pad_maximum_fusion), calls=%async_computation.4 | async-start | bytes 2097152 | tf_op jit(solution)/shard_map/all_to_all | solution.py:84
  395.3 9.9 %collective-permute-start = (bf16[64,64,128]{2,1,0:T(8,128)(2,1)S(1)}, bf16[64,64,128]{2,1,0:T(8,128)(2,1)S(1)}, u32[]{:S(2)}, u32[]{:S(2)}) collective-permute-start(bf16[64,64,128]{2,1,0:T(8,128)(2,1)S(1)} %all_to_all.31), channel_id=1, source_target_pairs={{0,4},{4,0},{1,5},{5,1},{2,6},{6,2},{3,7},{7,3},{8,12},{12,8},{9,1... | collective-permute-start | bytes 3145736 | tf_op jit(solution)/shard_map/ppermute | solution.py:92

commit v2 on v1

--- a/solution.py
+++ b/solution.py
@@ -2,9 +2,11 @@
 import jax.numpy as jnp
 import numpy as np
 from jax import lax
-from jax.sharding import Mesh, PartitionSpec as P
-
-DOM = ("y", "z", "c")
+from jax.experimental import pallas as pl
+from jax.experimental.pallas import tpu as pltpu
+from jax.sharding import PartitionSpec as P
+
+DOM = "dom"
 BF = jnp.bfloat16
 F32 = jnp.float32
 
@@ -21,6 +23,111 @@
 def spread_rep(rows):
     copies = jnp.broadcast_to(rows[None], (4,) + rows.shape)
     return lax.all_to_all(copies, "rep", split_axis=0, concat_axis=0, tiled=True)
+
+
+def grad_body(types, core, agg, dz, keep, send):
+    reps, nodes, _ = agg.shape
+    rows = types.shape[0]
+    tile = nodes // rows
+    half = keep.shape[1] // dz.shape[1]
+    for target, side in ((send, 1 - core[0]), (keep, core[0])):
+        wide = []
+        for e in range(half):
+            part = []
+            for j in range(rows):
+                block = dz[j * tile : (j + 1) * tile, :]
+                hit = (types[j] == side * half + e).astype(F32)
+                part.append((block.astype(F32) * hit).astype(BF))
+            wide.append(jnp.concatenate(part, axis=0))
+        wide = jnp.concatenate(wide, axis=1)
+        for q in range(reps):
+            cols = agg.shape[2]
+            block = lax.dot_general(
+                agg[q], wide, (((0,), (0,)), ((), ())), preferred_element_type=F32
+            )
+            target[q * cols : (q + 1) * cols, :] = block.astype(target.dtype)
+
+
+def grad_halves(types, core, agg, dz):
+    reps, nodes, cols = agg.shape
+    half = 4 * cols
+    smem = pl.BlockSpec(memory_space=pltpu.SMEM)
+    vmem = pl.BlockSpec(memory_space=pltpu.VMEM)
+    return pl.pallas_call(
+        grad_body,
+        out_shape=(
+            jax.ShapeDtypeStruct((reps * cols, half), F32),
+            jax.ShapeDtypeStruct((reps * cols, half), BF),
+        ),
+        in_specs=[smem, smem, vmem, vmem],
+        out_specs=(vmem, vmem),
+        compiler_params=pltpu.CompilerParams(vmem_limit_bytes=32 << 20),
+        name="grad_halves",
+    )(types, core, agg, dz)
+
+
+def unpack_body(core, same, other, one, two):
+    first = core[0] == 0
+    for layer, out in enumerate((one, two)):
+        half = out.shape[1] // 2
+        cols = out.shape[2]
+        for s in range(same.shape[0]):
+            mine = same[s, layer].astype(F32)
+            theirs = other[s, layer].astype(F32)
+            low = jnp.where(first, mine, theirs)
+            high = jnp.where(first, theirs, mine)
+            rows = slice(s * mine.shape[0], (s + 1) * mine.shape[0])
+            for e in range(half):
+                out[rows, e, :] = low[:, e * cols : (e + 1) * cols]
+                out[rows, half + e, :] = high[:, e * cols : (e + 1) * cols]
+
+
+def unpack(core, same, other):
+    chunks, layers, rows, span = same.shape
+    cols = 128
+    step = 8
+    experts = 2 * span // cols
+    block = pl.BlockSpec((step, layers, rows, span), lambda i: (i, 0, 0, 0))
+    target = pl.BlockSpec((step * rows, experts, cols), lambda i: (i, 0, 0))
+    shape = jax.ShapeDtypeStruct((chunks * rows, experts, cols), F32)
+    return pl.pallas_call(
+        unpack_body,
+        grid=(chunks // step,),
+        out_shape=(shape, shape),
+        in_specs=[pl.BlockSpec(memory_space=pltpu.SMEM), block, block],
+        out_specs=(target, target),
+        name="unpack",
+    )(core, same, other)
+
+
+def rings():
+    along_y = [[[(y * 8 + z) * 2 + c for y in range(8)] for z in range(8)] for c in range(2)]
+    along_z = [[[(y * 8 + z) * 2 + c for z in range(8)] for y in range(8)] for c in range(2)]
+    return along_y[0] + along_z[1], along_z[0] + along_y[1]
+
+
+def exchange(blocks, groups):
+    return lax.all_to_all(
+        blocks, "dom", split_axis=0, concat_axis=0, axis_index_groups=groups, tiled=True
+    )
+
+
+def pair_sum(agg, dz, types, core):
+    reps, rows, tile, width = agg.shape
+    keep, send = grad_halves(
+        types, core, agg.reshape(reps, rows * tile, width), dz.reshape(rows * tile, width)
+    )
+    came = lax.ppermute(send, "dom", [(p, p ^ 1) for p in range(128)])
+    return (keep + came.astype(F32)).astype(BF).reshape(8, 64, -1)
+
+
+def gather_sum(parts):
+    return jnp.sum(parts.astype(F32), axis=0).astype(BF)
+
+
+def spread(rows, groups):
+    copies = jnp.broadcast_to(rows[None], (8,) + rows.shape)
+    return exchange(copies, groups).reshape((-1,) + rows.shape[1:])
 
 
 def shards(
@@ -38,8 +145,8 @@
     halo_pick = halo_tile[0]
     types = tile_type[0]
     send_rows = halo_send[0]
-    code = jnp.broadcast_to(types.astype(F32)[:, None, None], (rows, 4, 128)).reshape(16, 128)
-    all_types = lax.all_gather(code, DOM, axis=0, tiled=False)[:, ::4, 0]
+    core = (lax.axis_index("dom") % 2).astype(jnp.int32).reshape(1)
+    first, second = rings()
 
     index = jnp.stack([send_rows, send_rows + nodes], axis=1).reshape(-1)
     pick = (index[:, None] == jnp.arange(2 * nodes, dtype=jnp.int32)[None, :]).astype(BF)
@@ -68,37 +175,25 @@
     h_two = (h_one.astype(F32) + jax.nn.silu(z_two)).astype(BF)
     upstream = grad_out.reshape(rows, tile, cols).astype(F32)
     dz_two = (upstream * slope_silu(z_two)).astype(BF)
+    sum_two = gather_sum(exchange(pair_sum(agg_two, dz_two, types, core), first))
     partial_back = dot("jrc,qdjc->qjrd", dz_two, pick_two).astype(BF).reshape(reps, nodes, cols)
     partial_back = lax.all_to_all(partial_back, "rep", split_axis=0, concat_axis=0, tiled=True)
     dagg = jnp.sum(partial_back.astype(F32), axis=0).astype(BF).reshape(rows, tile, cols)
     dh_one = upstream + dot("jrk,jrc->jkc", local_blocks, dagg)
     dz_one = (dh_one * slope_silu(z_one)).astype(BF)
 
-    half = parts // 2
-    own = width // half
-    tiles = []
-    for agg, dz in ((agg_one, dz_one), (agg_two, dz_two)):
-        part = dot("qjrd,jrc->jqdc", agg, dz).astype(BF)
-        tiles.append(part.reshape(rows, half, own, cols).transpose(1, 0, 2, 3))
-    sent = jnp.concatenate(tiles, axis=0)
-    got = lax.all_to_all(sent, DOM, split_axis=0, concat_axis=0, tiled=True)
-    onehot = (
-        all_types[:, :, None] == jnp.arange(experts, dtype=F32)[None, None, :]
-    ).astype(BF)
-    mine = dot("pje,pjdc->dec", onehot, got).astype(BF).reshape(own * experts, cols)
-
-    copies = jnp.broadcast_to(mine[None], (half,) + mine.shape)
-    same = lax.all_to_all(copies, ("y", "z"), split_axis=0, concat_axis=0, tiled=True)
-    other = lax.ppermute(same, "c", [(0, 1), (1, 0)])
-    core = lax.axis_index("c")
-    even = jnp.where(core == 0, same, other)
-    odd = jnp.where(core == 0, other, same)
-    both = jnp.stack([even, odd], axis=1).reshape(2, width, experts, cols).astype(F32)
-    return (h_two.reshape(-1, cols), h_one.reshape(-1, cols), both[0], both[1])
+    sum_one = gather_sum(exchange(pair_sum(agg_one, dz_one, types, core), first))
+    span = sum_one.shape[1]
+    both = jnp.stack([sum_one.reshape(8, 8, span), sum_two.reshape(8, 8, span)], axis=1)
+    mine = gather_sum(exchange(both, second))
+    some = spread(mine[None], second)
+    same = spread(some, first).reshape(64, 2, 8, span)
+    other = lax.ppermute(same, "dom", [(p, p ^ 1) for p in range(128)])
+    grad_one, grad_two = unpack(core, same, other)
+    return (h_two.reshape(-1, cols), h_one.reshape(-1, cols), grad_one, grad_two)
 
 
 def solution(mesh):
-    fine = Mesh(mesh.devices.reshape(8, 8, 2, 4), ("y", "z", "c", "rep"))
     in_specs = (
         P(DOM, "rep"),
         P(DOM, "rep"),
@@ -112,4 +207,4 @@
         P(DOM, "rep"),
     )
     out_specs = (P(DOM, "rep"), P(DOM, "rep"), P(None, None, "rep"), P(None, None, "rep"))
-    return jax.shard_map(shards, mesh=fine, in_specs=in_specs, out_specs=out_specs, check_vma=False)
+    return jax.shard_map(shards, mesh=mesh, in_specs=in_specs, out_specs=out_specs, check_vma=False)

time: 409 us -> 184 us (0.45)
  blocking collectives: 308 us -> 53.4 us
  waiting for transfers between devices: 20.2 us -> 38.2 us
  Pallas kernels: 0 us -> 9.91 us
  starting transfers between devices: 47.8 us -> 53 us
  local copies, waits for them, and re-layouts: 14.5 us -> 9.73 us
    unnamed x1 -> x0, blocking collectives: 267 us -> none
    all_to_all x2 -> x4, blocking collectives: 40.2 us -> 53.4 us  [the longest x3 41.6 us: exchange(): lax.all_to_all(blocks, 'dom', split_axis=0, concat_axis=0, axis_index_gro...]
    ppermute x1 -> x3, starting transfers between devices: 7.6 us -> 19.1 us  [the longest x2 9.76 us: pair_sum(): came = lax.ppermute(send, 'dom', [(p, p ^ 1) for p in range(128)])]
    pallas_call x0 -> x3, Pallas kernels: none -> 9.91 us  [the longest x1 6.83 us: unpack(): pl.pallas_call(unpack_body, grid=(chunks // step,), out_shape=(shape, sha...]
    all_to_all x2, waiting for transfers between devices: 6.32 us -> 16 us  [exchange(): lax.all_to_all(blocks, 'dom', split_axis=0, concat_axis=0, axis_index_gro...]
    all_to_all x2, starting transfers between devices: 17.6 us -> 8.07 us  [exchange(): lax.all_to_all(blocks, 'dom', split_axis=0, concat_axis=0, axis_index_gro...]
    all_to_all x1 -> x2, waiting for transfers between devices: 5.81 us -> 12.5 us  [spread_rep(): lax.all_to_all(copies, 'rep', split_axis=0, concat_axis=0, tiled=True)]
    dot_general x12 -> x10, matrix products: 11 us -> 11.2 us  [dot(): return jnp.einsum(spec, a, b, preferred_element_type=F32)]
  transfers between devices with their start and end apart: 5 -> 8, of which waited for: 4 -> 7; matrix products, arithmetic and copies ran while one was open for 3% -> 7% of each run, Pallas kernels for 0% -> 1%
where the time goes in v2:
time: 184 us; the launch traced here: 183 us
  blocking collectives  53.4 us (29%)
  starting transfers between devices  53 us (29%)
  waiting for transfers between devices  38.2 us (21%)
  matrix products  11.2 us (6%)
  Pallas kernels  9.91 us (5%)
  local copies, waits for them, and re-layouts  9.73 us (5%)
  other arithmetic  6.19 us (3%)
    all_to_all x3, blocking collectives, exchange(): lax.all_to_all(blocks, 'dom', split_axis=0, concat_axis=0, axis_index_gro...  41.6 us
    all_to_all x1, starting transfers between devices, shards(): lax.all_to_all(picked, DOM, split_axis=0, concat_axis=0, tiled=True)  18.4 us
    all_to_all x2, waiting for transfers between devices, exchange(): lax.all_to_all(blocks, 'dom', split_axis=0, concat_axis=0, axis_index_gro...  16 us
    all_to_all x2, waiting for transfers between devices, spread_rep(): lax.all_to_all(copies, 'rep', split_axis=0, concat_axis=0, tiled=True)  12.5 us
    all_to_all x1, blocking collectives, shards(): lax.all_to_all(partial_back, 'rep', split_axis=0, concat_axis=0, tiled=True)  11.7 us
    dot_general x10, matrix products, dot(): return jnp.einsum(spec, a, b, preferred_element_type=F32)  11.2 us
    ppermute x2, starting transfers between devices, pair_sum(): came = lax.ppermute(send, 'dom', [(p, p ^ 1) for p in range(128)])  9.76 us
    ppermute x1, starting transfers between devices, shards(): other = lax.ppermute(same, 'dom', [(p, p ^ 1) for p in range(128)])  9.3 us
  transfers between devices with their start and end apart: 8, of which 7 were waited for; matrix products, arithmetic and copies ran while one was open for 7% of the time, Pallas kernels for 1%

profile of v2, /device:TPU:1, one launch (start us, length us, event | category | flops | bytes accessed | tf_op | source)
XLA Modules:
  0.0 182.6 jit_solution(12871799839689357394)
XLA Ops:
  2.5 2.5 %fusion.5 = bf16[128,8,128]{2,1,0:T(8,128)(2,1)} fusion(s32[1024]{0:T(1024)S(1)} %eq.17, bf16[512,128]{1,0:T(8,128)(2,1)} %param.14, bf16[512,128]{1,0:T(8,128)(2,1)} %param.13), kind=kOutput, calls=%fused_computation.15 | convolution fusion | flops 270139392 | bytes 528384 | tf_op jit(solution)/shard_map/ab,bc->ac/dot_general | solution.py:20
  5.0 18.4 %all-to-all-start = ((bf16[128,8,128]{2,1,0:T(8,128)(2,1)}), bf16[128,8,128]{2,1,0:T(8,128)(2,1)S(1)}, u32[]{:S(2)}, u32[]{:S(2)}) async-start(bf16[128,8,128]{2,1,0:T(8,128)(2,1)} %fusion.5), calls=%async_computation | async-start | bytes 524288 | tf_op jit(solution)/shard_map/all_to_all | solution.py:155
  23.5 2.9 %gather_fusion.2 = bf16[4,512,128]{2,0,1:T(4,128)(2,1)S(1)} fusion(bf16[512,8,128]{2,1,0:T(8,128)(2,1)S(1)} %copy-done, s32[1024]{0:T(1024)S(1)} %pad_clamp_fusion), kind=kCustom, calls=%fused_computation.1.clone | custom fusion | bytes 1048592 | tf_op jit(solution)/shard_map/jit(_take)/gather | solution.py:173
  26.5 2.9 %gather_fusion.1 = bf16[4,512,128]{2,0,1:T(4,128)(2,1)S(1)} fusion(bf16[512,8,128]{2,1,0:T(8,128)(2,1)S(1)} %copy-done.2, s32[1024]{0:T(1024)S(1)} %pad_clamp_fusion), kind=kCustom, calls=%fused_computation.clone | custom fusion | bytes 1048592 | tf_op jit(solution)/shard_map/jit(_take)/gather | solution.py:167
  29.4 1.1 fusion.23
  30.5 1.3 fusion.2
  31.8 5.9 %all-to-all-done = bf16[128,8,128]{2,1,0:T(8,128)(2,1)S(1)} async-done(((bf16[128,8,128]{2,1,0:T(8,128)(2,1)}), bf16[128,8,128]{2,1,0:T(8,128)(2,1)S(1)}, u32[]{:S(2)}, u32[]{:S(2)}) %all-to-all-start) | async-done | bytes 262176 | tf_op jit(solution)/shard_map/all_to_all | solution.py:155
  39.4 4.0 %all-to-all-start.1 = ((bf16[4,512,128]{2,1,0:T(8,128)(2,1)}), bf16[4,512,128]{2,1,0:T(8,128)(2,1)S(1)}, u32[]{:S(2)}, u32[]{:S(2)}) async-start(bf16[4,512,128]{2,1,0:T(8,128)(2,1)} %broadcast_in_dim.49), calls=%async_computation.1 | async-start | bytes 1048576 | tf_op jit(solution)/shard_map/all_to_all | solution.py:25
  43.4 1.5 broadcast_select_fusion
  44.9 5.6 %all-to-all-done.1.agg = bf16[4,512,128]{2,1,0:T(8,128)(2,1)S(1)} async-done(((bf16[4,512,128]{2,1,0:T(8,128)(2,1)}), bf16[4,512,128]{2,1,0:T(8,128)(2,1)S(1)}, u32[]{:S(2)}, u32[]{:S(2)}) %all-to-all-start.1) | async-done | bytes 524320 | tf_op jit(solution)/shard_map/all_to_all | solution.py:25
  50.6 2.1 %add_convert_fusion.3 = (bf16[4,128,128]{2,1,0:T(8,128)(2,1)S(1)}, f32[4,128,128]{2,1,0:T(8,128)}) fusion(bf16[4,128,128]{2,1,0:T(8,128)(2,1)S(1)} %bitcast.111, bf16[4,4,128,128]{3,2,1,0:T(8,128)(2,1)S(1)} %bitcast.87, bf16[4,128,4,128]{3,2,1,0:T(4,128)(2,1)} %bitcast.100), kind=kOutput, calls=%fused_computation.39 | convolution fusion | flops 67567616 | bytes 1572864 | tf_op jit(solution)/shard_map/qjrd,qdjc->jrc/dot_general | solution.py:20
  54.0 3.5 %all-to-all-start.2 = ((bf16[4,512,128]{2,1,0:T(8,128)(2,1)}), bf16[4,512,128]{2,1,0:T(8,128)(2,1)S(1)}, u32[]{:S(2)}, u32[]{:S(2)}) async-start(bf16[4,512,128]{2,1,0:T(8,128)(2,1)} %broadcast_in_dim.51), calls=%async_computation.2 | async-start | bytes 1048576 | tf_op jit(solution)/shard_map/all_to_all | solution.py:25
  57.5 6.9 %all-to-all-done.2.agg = bf16[4,512,128]{2,1,0:T(8,128)(2,1)S(1)} async-done(((bf16[4,512,128]{2,1,0:T(8,128)(2,1)}), bf16[4,512,128]{2,1,0:T(8,128)(2,1)S(1)}, u32[]{:S(2)}, u32[]{:S(2)}) %all-to-all-start.2) | async-done | bytes 524320 | tf_op jit(solution)/shard_map/all_to_all | solution.py:25
  65.4 1.8 grad_halves.3
  67.2 6.3 %collective-permute-start.1 = (bf16[512,512]{1,0:T(8,128)(2,1)}, bf16[512,512]{1,0:T(8,128)(2,1)}, u32[]{:S(2)}, u32[]{:S(2)}) collective-permute-start(bf16[512,512]{1,0:T(8,128)(2,1)} %get-tuple-element.14), channel_id=1, source_target_pairs={{0,4},{4,0},{8,12},{12,8},{16,20},{20,16},{24,28},{28,24},{32,36},... | collective-permute-start | bytes 1572872 | tf_op jit(solution)/shard_map/ppermute | solution.py:120
  73.5 1.4 fusion.3
  74.9 11.7 %all_to_all.45 = bf16[4,512,128]{2,1,0:T(8,128)(2,1)S(1)} all-to-all(bf16[4,512,128]{2,1,0:T(8,128)(2,1)S(1)} %bitcast.97), channel_id=1, replica_groups=mesh['dom'=128,'rep'=4] {'rep'}, dimensions={0} | all-to-all | bytes 1048576 | tf_op jit(solution)/shard_map/all_to_all | solution.py:180
  86.8 2.0 %add_convert_fusion = bf16[512,512]{1,0:T(8,128)(2,1)} fusion(f32[512,512]{1,0:T(8,128)S(1)} %get-tuple-element.13, bf16[512,512]{1,0:T(8,128)(2,1)} %collective-permute-done.1), kind=kLoop, calls=%fused_computation.23 | loop fusion | flops 786432 | bytes 2097152 | tf_op jit(solution)/shard_map/convert_element_type | solution.py:121
  88.8 4.6 %all-to-all-start.5 = ((bf16[8,64,512]{2,1,0:T(8,128)(2,1)}), bf16[8,64,512]{2,1,0:T(8,128)(2,1)S(1)}, u32[]{:S(2)}, u32[]{:S(2)}) async-start(bf16[8,64,512]{2,1,0:T(8,128)(2,1)} %bitcast.98), calls=%async_computation.5 | async-start | bytes 1048576 | tf_op jit(solution)/shard_map/all_to_all | solution.py:110
  93.3 1.2 fusion.8
  94.5 1.3 grad_halves.2
  95.8 3.4 %collective-permute-start = (bf16[512,512]{1,0:T(8,128)(2,1)S(1)}, bf16[512,512]{1,0:T(8,128)(2,1)S(1)}, u32[]{:S(2)}, u32[]{:S(2)}) collective-permute-start(bf16[512,512]{1,0:T(8,128)(2,1)S(1)} %get-tuple-element.12), channel_id=1, source_target_pairs={{0,4},{4,0},{8,12},{12,8},{16,20},{20,16},{24,28},{28,24},{32,36},... | collective-permute-start | bytes 1572872 | tf_op jit(solution)/shard_map/ppermute | solution.py:120
  99.2 1.5 collective-permute-done
  101.7 4.1 %all-to-all-done.5 = bf16[8,64,512]{2,1,0:T(8,128)(2,1)S(1)} async-done(((bf16[8,64,512]{2,1,0:T(8,128)(2,1)}), bf16[8,64,512]{2,1,0:T(8,128)(2,1)S(1)}, u32[]{:S(2)}, u32[]{:S(2)}) %all-to-all-start.5) | async-done | bytes 524320 | tf_op jit(solution)/shard_map/all_to_all | solution.py:110
  105.8 3.5 %all-to-all-start.4 = ((bf16[8,64,512]{2,1,0:T(8,128)(2,1)}), bf16[8,64,512]{2,1,0:T(8,128)(2,1)S(1)}, u32[]{:S(2)}, u32[]{:S(2)}) async-start(bf16[8,64,512]{2,1,0:T(8,128)(2,1)} %bitcast.40), calls=%async_computation.4 | async-start | bytes 1048576 | tf_op jit(solution)/shard_map/all_to_all | solution.py:110
  109.4 12.0 %all-to-all-done.4 = bf16[8,64,512]{2,1,0:T(8,128)(2,1)S(1)} async-done(((bf16[8,64,512]{2,1,0:T(8,128)(2,1)}), bf16[8,64,512]{2,1,0:T(8,128)(2,1)S(1)}, u32[]{:S(2)}, u32[]{:S(2)}) %all-to-all-start.4) | async-done | bytes 524320 | tf_op jit(solution)/shard_map/all_to_all | solution.py:110
  121.4 11.2 %all_to_all.46 = bf16[8,2,8,512]{3,2,1,0:T(8,128)(2,1)S(1)} all-to-all(bf16[8,2,8,512]{3,2,1,0:T(8,128)(2,1)S(1)} %pad_maximum_fusion), channel_id=1, replica_groups={{0,8,16,24,32,40,48,56},{64,72,80,88,96,104,112,120},{128,136,144,152,1..., dimensions={0} | all-to-all | bytes 262144 | tf_op jit(solution)/shard_map/all_to_all | solution.py:110
  132.6 10.3 %all_to_all.47 = bf16[8,1,2,8,512]{4,3,2,1,0:T(8,128)(2,1)S(1)} all-to-all(bf16[8,1,2,8,512]{4,3,2,1,0:T(8,128)(2,1)S(1)} %broadcast_in_dim.52), channel_id=1, replica_groups={{0,8,16,24,32,40,48,56},{64,72,80,88,96,104,112,120},{128,136,144,152,1..., dimensions={0} | all-to-all | bytes 262144 | tf_op jit(solution)/shard_map/all_to_all | solution.py:110
  143.1 20.2 %all_to_all.48 = bf16[8,8,2,8,512]{4,3,2,1,0:T(8,128)(2,1)S(1)} all-to-all(bf16[8,8,2,8,512]{4,3,2,1,0:T(8,128)(2,1)S(1)} %broadcast_in_dim.54), channel_id=1, replica_groups={{0,64,128,192,256,320,384,448},{8,72,136,200,264,328,392,456},{16,80,14..., dimensions={0} | all-to-all | bytes 2097152 | tf_op jit(solution)/shard_map/all_to_all | solution.py:110
  163.2 9.3 %collective-permute-start.2 = (bf16[64,2,8,512]{3,2,1,0:T(8,128)(2,1)S(1)}, bf16[64,2,8,512]{3,2,1,0:T(8,128)(2,1)S(1)}, u32[]{:S(2)}, u32[]{:S(2)}) collective-permute-start(bf16[64,2,8,512]{3,2,1,0:T(8,128)(2,1)S(1)} %bitcast.93), channel_id=1, source_target_pairs={{0,4},{4,0},{8,12},{12,8},{16,20},{20,16},{24,28},{28,24},{32,36},... | collective-permute-start | bytes 3145736 | tf_op jit(solution)/shard_map/ppermute | solution.py:191
  172.6 2.3 %collective-permute-done.2.other = bf16[64,2,8,512]{3,2,1,0:T(8,128)(2,1)S(1)} collective-permute-done((bf16[64,2,8,512]{3,2,1,0:T(8,128)(2,1)S(1)}, bf16[64,2,8,512]{3,2,1,0:T(8,128)(2,1)S(1)}, u32[]{:S(2)}, u32[]{:S(2)}) %collective-permute-start.2) | collective-permute-done | bytes 1048608 | tf_op jit(solution)/shard_map/ppermute | solution.py:191
  175.8 6.8 %unpack.1 = (f32[512,8,128]{2,1,0:T(8,128)}, f32[512,8,128]{2,1,0:T(8,128)}) custom-call(s32[1]{0:T(128)} %bitcast.29.core, bf16[64,2,8,512]{3,2,1,0:T(8,128)(2,1)} %bitcast.94, bf16[64,2,8,512]{3,2,1,0:T(8,128)(2,1)} %copy-done.7), custom_call_target="tpu_custom_call" | custom-call | tf_op jit(solution)/shard_map/unpack/pallas_call | solution.py:93
  (53 shorter events, 8.3 us)
Async XLA Ops:
  0.6 22.9 %copy-start = (bf16[512,8,128]{2,1,0:T(8,128)(2,1)S(1)}, bf16[512,8,128]{2,1,0:T(8,128)(2,1)}, u32[]{:S(2)}) copy-start(bf16[512,8,128]{2,1,0:T(8,128)(2,1)} %param.21) | copy-start | bytes 3145732
  0.6 22.8 %copy-start.12 = (s32[1,4]{1,0:T(1,128)S(1)}, s32[1,4]{1,0:T(1,128)}, u32[]{:S(2)}) copy-start(s32[1,4]{1,0:T(1,128)} %param.18) | copy-start | bytes 52
  0.7 22.8 %copy-start.1 = (s32[1,4]{1,0:T(1,128)S(1)}, s32[1,4]{1,0:T(1,128)}, u32[]{:S(2)}) copy-start(s32[1,4]{1,0:T(1,128)} %param.19) | copy-start | bytes 52
  5.0 32.7 %all-to-all-start = ((bf16[128,8,128]{2,1,0:T(8,128)(2,1)}), bf16[128,8,128]{2,1,0:T(8,128)(2,1)S(1)}, u32[]{:S(2)}, u32[]{:S(2)}) async-start(bf16[128,8,128]{2,1,0:T(8,128)(2,1)} %fusion.5), calls=%async_computation | async-start | bytes 524288 | tf_op jit(solution)/shard_map/all_to_all | solution.py:155
  23.5 3.0 %copy-start.2 = (bf16[512,8,128]{2,1,0:T(8,128)(2,1)S(1)}, bf16[512,8,128]{2,1,0:T(8,128)(2,1)}, u32[]{:S(2)}) copy-start(bf16[512,8,128]{2,1,0:T(8,128)(2,1)} %param.20) | copy-start | bytes 3145732
  26.5 3.0 %copy-start.8 = (bf16[512,128]{1,0:T(8,128)(2,1)S(1)}, bf16[512,128]{1,0:T(8,128)(2,1)}, u32[]{:S(2)}) copy-start(bf16[512,128]{1,0:T(8,128)(2,1)} %param.15) | copy-start | bytes 393220
  31.8 7.6 %copy-start.5 = (bf16[2,4,128,256]{2,3,1,0:T(8,128)(2,1)}, bf16[2,4,128,256]{2,3,1,0:T(8,128)(2,1)S(1)}, u32[]{:S(2)}) copy-start(bf16[2,4,128,256]{2,3,1,0:T(8,128)(2,1)S(1)} %fusion.2) | copy-start | bytes 1572868
  38.5 12.0 %copy-start.9 = (bf16[512,128]{1,0:T(8,128)(2,1)S(1)}, bf16[512,128]{1,0:T(8,128)(2,1)}, u32[]{:S(2)}) copy-start(bf16[512,128]{1,0:T(8,128)(2,1)} %param.13) | copy-start | bytes 393220
  39.4 11.2 %all-to-all-start.1 = ((bf16[4,512,128]{2,1,0:T(8,128)(2,1)}), bf16[4,512,128]{2,1,0:T(8,128)(2,1)S(1)}, u32[]{:S(2)}, u32[]{:S(2)}) async-start(bf16[4,512,128]{2,1,0:T(8,128)(2,1)} %broadcast_in_dim.49), calls=%async_computation.1 | async-start | bytes 1048576 | tf_op jit(solution)/shard_map/all_to_all | solution.py:25
  44.9 7.9 %copy-start.6 = (bf16[2,4,128,256]{2,3,1,0:T(8,128)(2,1)S(1)}, bf16[2,4,128,256]{2,3,1,0:T(8,128)(2,1)}, u32[]{:S(2)}) copy-start(bf16[2,4,128,256]{2,3,1,0:T(8,128)(2,1)} %copy-done.5) | copy-start | bytes 1572868
  52.6 12.7 %copy-start.10 = (bf16[4,128,128]{2,1,0:T(8,128)(2,1)}, bf16[4,128,128]{2,1,0:T(8,128)(2,1)S(1)}, u32[]{:S(2)}) copy-start(bf16[4,128,128]{2,1,0:T(8,128)(2,1)S(1)} %get-tuple-element.21) | copy-start | bytes 393220
  52.6 11.7 %copy-start.4 = (bf16[4,512,128]{2,0,1:T(4,128)(2,1)S(1)}, bf16[4,512,128]{2,0,1:T(4,128)(2,1)}, u32[]{:S(2)}) copy-start(bf16[4,512,128]{2,0,1:T(4,128)(2,1)} %get-tuple-element.19) | copy-start | bytes 1572868
  52.6 11.7 %copy-start.11 = (bf16[512,128]{1,0:T(8,128)(2,1)S(1)}, bf16[512,128]{1,0:T(8,128)(2,1)}, u32[]{:S(2)}) copy-start(bf16[512,128]{1,0:T(8,128)(2,1)} %param.22) | copy-start | bytes 393220
  54.0 10.4 %all-to-all-start.2 = ((bf16[4,512,128]{2,1,0:T(8,128)(2,1)}), bf16[4,512,128]{2,1,0:T(8,128)(2,1)S(1)}, u32[]{:S(2)}, u32[]{:S(2)}) async-start(bf16[4,512,128]{2,1,0:T(8,128)(2,1)} %broadcast_in_dim.51), calls=%async_computation.2 | async-start | bytes 1048576 | tf_op jit(solution)/shard_map/all_to_all | solution.py:25
  67.2 19.6 %collective-permute-start.1 = (bf16[512,512]{1,0:T(8,128)(2,1)}, bf16[512,512]{1,0:T(8,128)(2,1)}, u32[]{:S(2)}, u32[]{:S(2)}) collective-permute-start(bf16[512,512]{1,0:T(8,128)(2,1)} %get-tuple-element.14), channel_id=1, source_target_pairs={{0,4},{4,0},{8,12},{12,8},{16,20},{20,16},{24,28},{28,24},{32,36},... | collective-permute-start | bytes 1572872 | tf_op jit(solution)/shard_map/ppermute | solution.py:120
  88.8 17.0 %all-to-all-start.5 = ((bf16[8,64,512]{2,1,0:T(8,128)(2,1)}), bf16[8,64,512]{2,1,0:T(8,128)(2,1)S(1)}, u32[]{:S(2)}, u32[]{:S(2)}) async-start(bf16[8,64,512]{2,1,0:T(8,128)(2,1)} %bitcast.98), calls=%async_computation.5 | async-start | bytes 1048576 | tf_op jit(solution)/shard_map/all_to_all | solution.py:110
  95.8 4.9 %collective-permute-start = (bf16[512,512]{1,0:T(8,128)(2,1)S(1)}, bf16[512,512]{1,0:T(8,128)(2,1)S(1)}, u32[]{:S(2)}, u32[]{:S(2)}) collective-permute-start(bf16[512,512]{1,0:T(8,128)(2,1)S(1)} %get-tuple-element.12), channel_id=1, source_target_pairs={{0,4},{4,0},{8,12},{12,8},{16,20},{20,16},{24,28},{28,24},{32,36},... | collective-permute-start | bytes 1572872 | tf_op jit(solution)/shard_map/ppermute | solution.py:120
  105.8 15.6 %all-to-all-start.4 = ((bf16[8,64,512]{2,1,0:T(8,128)(2,1)}), bf16[8,64,512]{2,1,0:T(8,128)(2,1)S(1)}, u32[]{:S(2)}, u32[]{:S(2)}) async-start(bf16[8,64,512]{2,1,0:T(8,128)(2,1)} %bitcast.40), calls=%async_computation.4 | async-start | bytes 1048576 | tf_op jit(solution)/shard_map/all_to_all | solution.py:110
  163.2 11.6 %copy-start.3 = (bf16[8,8,2,8,512]{4,3,2,1,0:T(8,128)(2,1)}, bf16[8,8,2,8,512]{4,3,2,1,0:T(8,128)(2,1)S(1)}, u32[]{:S(2)}) copy-start(bf16[8,8,2,8,512]{4,3,2,1,0:T(8,128)(2,1)S(1)} %all_to_all.48) | copy-start | bytes 3145732
  163.2 11.6 %collective-permute-start.2 = (bf16[64,2,8,512]{3,2,1,0:T(8,128)(2,1)S(1)}, bf16[64,2,8,512]{3,2,1,0:T(8,128)(2,1)S(1)}, u32[]{:S(2)}, u32[]{:S(2)}) collective-permute-start(bf16[64,2,8,512]{3,2,1,0:T(8,128)(2,1)S(1)} %bitcast.93), channel_id=1, source_target_pairs={{0,4},{4,0},{8,12},{12,8},{16,20},{20,16},{24,28},{28,24},{32,36},... | collective-permute-start | bytes 3145736 | tf_op jit(solution)/shard_map/ppermute | solution.py:191
  174.8 1.0 copy-start.7

commit v3 on v1

--- a/solution.py
+++ b/solution.py
@@ -2,9 +2,11 @@
 import jax.numpy as jnp
 import numpy as np
 from jax import lax
-from jax.sharding import Mesh, PartitionSpec as P
-
-DOM = ("y", "z", "c")
+from jax.experimental import pallas as pl
+from jax.experimental.pallas import tpu as pltpu
+from jax.sharding import PartitionSpec as P
+
+DOM = "dom"
 BF = jnp.bfloat16
 F32 = jnp.float32
 
@@ -21,6 +23,149 @@
 def spread_rep(rows):
     copies = jnp.broadcast_to(rows[None], (4,) + rows.shape)
     return lax.all_to_all(copies, "rep", split_axis=0, concat_axis=0, tiled=True)
+
+
+SMEM = pl.BlockSpec(memory_space=pltpu.SMEM)
+VMEM = pl.BlockSpec(memory_space=pltpu.VMEM)
+PARAMS = pltpu.CompilerParams(vmem_limit_bytes=40 << 20)
+
+
+def grad_body(types, core, agg, dz, keep, send):
+    reps, nodes, cols = agg.shape
+    rows = types.shape[0]
+    tile = nodes // rows
+    experts = keep.shape[1] // dz.shape[1]
+    wide = []
+    for e in range(experts):
+        part = []
+        for j in range(rows):
+            block = dz[j * tile : (j + 1) * tile, :]
+            part.append((block.astype(F32) * (types[j] == e).astype(F32)).astype(BF))
+        wide.append(jnp.concatenate(part, axis=0))
+    wide = jnp.concatenate(wide, axis=1)
+    for target, side in ((send, 1 - core[0]), (keep, core[0])):
+        for i in range(reps // 2):
+            block = lax.dot_general(
+                agg[side * (reps // 2) + i],
+                wide,
+                (((0,), (0,)), ((), ())),
+                preferred_element_type=F32,
+            )
+            target[i * cols : (i + 1) * cols, :] = block.astype(target.dtype)
+
+
+def grad_halves(types, core, agg, dz):
+    reps, nodes, cols = agg.shape
+    shape = (reps * cols // 2, 8 * cols)
+    return pl.pallas_call(
+        grad_body,
+        out_shape=(jax.ShapeDtypeStruct(shape, F32), jax.ShapeDtypeStruct(shape, BF)),
+        in_specs=[SMEM, SMEM, VMEM, VMEM],
+        out_specs=(VMEM, VMEM),
+        compiler_params=PARAMS,
+        name="grad_halves",
+    )(types, core, agg, dz)
+
+
+def add_up(parts):
+    total = parts[0].astype(F32)
+    for i in range(1, parts.shape[0]):
+        total = total + parts[i].astype(F32)
+    return total
+
+
+def first_body(parts, copies):
+    total = add_up(parts).astype(BF)
+    for i in range(copies.shape[0]):
+        copies[i] = total
+
+
+def first_sum(parts):
+    return pl.pallas_call(
+        first_body,
+        out_shape=jax.ShapeDtypeStruct((8,) + parts.shape[1:], BF),
+        in_specs=[VMEM],
+        out_specs=VMEM,
+        compiler_params=PARAMS,
+        name="first_sum",
+    )(parts)
+
+
+def second_body(parts, copies, table):
+    rows, experts, cols = table.shape
+    total = add_up(parts)
+    for e in range(experts):
+        table[:, e, :] = total[:, e * cols : (e + 1) * cols]
+    laid = table[...].reshape(rows * experts, cols).astype(BF)
+    for i in range(copies.shape[0]):
+        copies[i] = laid
+
+
+def second_sum(parts):
+    _, rows, span = parts.shape
+    cols = 128
+    experts = span // cols
+    return pl.pallas_call(
+        second_body,
+        out_shape=jax.ShapeDtypeStruct((8, rows * experts, cols), BF),
+        in_specs=[VMEM],
+        out_specs=VMEM,
+        scratch_shapes=[pltpu.VMEM((rows, experts, cols), F32)],
+        compiler_params=PARAMS,
+        name="second_sum",
+    )(parts)
+
+
+def widen_body(core, same, other, one, two):
+    step = pl.program_id(0)
+    chunks = same.shape[0]
+    own = core[0] == step // (chunks // 2)
+    length = same.shape[1] // 2
+    for i in range(2):
+        at = lax.rem(step, chunks // 2) * 2 + i
+        both = jnp.where(own, same[at].astype(F32), other[at].astype(F32))
+        one[i * length : (i + 1) * length, :] = both[:length]
+        two[i * length : (i + 1) * length, :] = both[length:]
+
+
+def widen(core, same, other):
+    chunks, length, cols = same.shape
+    steps = chunks
+    target = pl.BlockSpec((length, cols), lambda i: (i, 0))
+    shape = jax.ShapeDtypeStruct((chunks * length, cols), F32)
+    return pl.pallas_call(
+        widen_body,
+        grid=(steps,),
+        out_shape=(shape, shape),
+        in_specs=[SMEM, VMEM, VMEM],
+        out_specs=(target, target),
+        compiler_params=PARAMS,
+        name="widen",
+    )(core, same, other)
+
+
+def rings():
+    along_y = [[[(y * 8 + z) * 2 + c for y in range(8)] for z in range(8)] for c in range(2)]
+    along_z = [[[(y * 8 + z) * 2 + c for z in range(8)] for y in range(8)] for c in range(2)]
+    return along_y[0] + along_z[1], along_z[0] + along_y[1]
+
+
+def exchange(blocks, groups):
+    return lax.all_to_all(
+        blocks, "dom", split_axis=0, concat_axis=0, axis_index_groups=groups, tiled=True
+    )
+
+
+def swap(rows):
+    return lax.ppermute(rows, "dom", [(p, p ^ 1) for p in range(128)])
+
+
+def pair_sum(agg, dz, types, core):
+    reps, rows, tile, width = agg.shape
+    keep, send = grad_halves(
+        types, core, agg.reshape(reps, rows * tile, width), dz.reshape(rows * tile, width)
+    )
+    return (keep + swap(send).astype(F32)).astype(BF).reshape(8, 32, -1)
 
 
 def shards(
@@ -38,8 +183,8 @@
     halo_pick = halo_tile[0]
     types = tile_type[0]
     send_rows = halo_send[0]
-    code = jnp.broadcast_to(types.astype(F32)[:, None, None], (rows, 4, 128)).reshape(16, 128)
-    all_types = lax.all_gather(code, DOM, axis=0, tiled=False)[:, ::4, 0]
+    core = (lax.axis_index("dom") % 2).astype(jnp.int32).reshape(1)
+    first, second = rings()
 
     index = jnp.stack([send_rows, send_rows + nodes], axis=1).reshape(-1)
     pick = (index[:, None] == jnp.arange(2 * nodes, dtype=jnp.int32)[None, :]).astype(BF)
@@ -68,37 +213,23 @@
     h_two = (h_one.astype(F32) + jax.nn.silu(z_two)).astype(BF)
     upstream = grad_out.reshape(rows, tile, cols).astype(F32)
     dz_two = (upstream * slope_silu(z_two)).astype(BF)
+    pair_two = pair_sum(agg_two, dz_two, types, core)
     partial_back = dot("jrc,qdjc->qjrd", dz_two, pick_two).astype(BF).reshape(reps, nodes, cols)
     partial_back = lax.all_to_all(partial_back, "rep", split_axis=0, concat_axis=0, tiled=True)
     dagg = jnp.sum(partial_back.astype(F32), axis=0).astype(BF).reshape(rows, tile, cols)
     dh_one = upstream + dot("jrk,jrc->jkc", local_blocks, dagg)
     dz_one = (dh_one * slope_silu(z_one)).astype(BF)
 
-    half = parts // 2
-    own = width // half
-    tiles = []
-    for agg, dz in ((agg_one, dz_one), (agg_two, dz_two)):
-        part = dot("qjrd,jrc->jqdc", agg, dz).astype(BF)
-        tiles.append(part.reshape(rows, half, own, cols).transpose(1, 0, 2, 3))
-    sent = jnp.concatenate(tiles, axis=0)
-    got = lax.all_to_all(sent, DOM, split_axis=0, concat_axis=0, tiled=True)
-    onehot = (
-        all_types[:, :, None] == jnp.arange(experts, dtype=F32)[None, None, :]
-    ).astype(BF)
-    mine = dot("pje,pjdc->dec", onehot, got).astype(BF).reshape(own * experts, cols)
-
-    copies = jnp.broadcast_to(mine[None], (half,) + mine.shape)
-    same = lax.all_to_all(copies, ("y", "z"), split_axis=0, concat_axis=0, tiled=True)
-    other = lax.ppermute(same, "c", [(0, 1), (1, 0)])
-    core = lax.axis_index("c")
-    even = jnp.where(core == 0, same, other)
-    odd = jnp.where(core == 0, other, same)
-    both = jnp.stack([even, odd], axis=1).reshape(2, width, experts, cols).astype(F32)
-    return (h_two.reshape(-1, cols), h_one.reshape(-1, cols), both[0], both[1])
+    pair_one = pair_sum(agg_one, dz_one, types, core)
+    both = exchange(jnp.concatenate([pair_one, pair_two], axis=1), first)
+    both = exchange(first_sum(both), second)
+    same = exchange(second_sum(both), first)
+    grad_one, grad_two = widen(core, same, swap(same))
+    grad_one, grad_two = grad_one.reshape(w_one.shape), grad_two.reshape(w_two.shape)
+    return (h_two.reshape(-1, cols), h_one.reshape(-1, cols), grad_one, grad_two)
 
 
 def solution(mesh):
-    fine = Mesh(mesh.devices.reshape(8, 8, 2, 4), ("y", "z", "c", "rep"))
     in_specs = (
         P(DOM, "rep"),
         P(DOM, "rep"),
@@ -112,4 +243,4 @@
         P(DOM, "rep"),
     )
     out_specs = (P(DOM, "rep"), P(DOM, "rep"), P(None, None, "rep"), P(None, None, "rep"))
-    return jax.shard_map(shards, mesh=fine, in_specs=in_specs, out_specs=out_specs, check_vma=False)
+    return jax.shard_map(shards, mesh=mesh, in_specs=in_specs, out_specs=out_specs, check_vma=False)

time: 409 us -> 166 us (0.41)
  blocking collectives: 308 us -> 72.9 us
  Pallas kernels: 0 us -> 7.12 us
  waiting for transfers between devices: 20.2 us -> 14.1 us
  local copies, waits for them, and re-layouts: 14.5 us -> 8.63 us
    unnamed x1 -> x0, blocking collectives: 267 us -> none
    all_to_all x1 -> x3, blocking collectives: 30.9 us -> 63.6 us  [exchange(): lax.all_to_all(blocks, 'dom', split_axis=0, concat_axis=0, axis_index_gro...]
    all_to_all x1 -> x0, starting transfers between devices: 14 us -> none  [shards(): got = lax.all_to_all(sent, DOM, split_axis=0, concat_axis=0, tiled=True)]
    ppermute x1 -> x3, starting transfers between devices: 7.6 us -> 18.9 us  [swap(): return lax.ppermute(rows, 'dom', [(p, p ^ 1) for p in range(128)])]
    pallas_call x0 -> x5, Pallas kernels: none -> 7.12 us  [the longest x1 3.48 us: widen(): pl.pallas_call(widen_body, grid=(steps,), out_shape=(shape, shape), in_sp...]
    all_to_all x1, waiting for transfers between devices: 6.32 us -> 0.01 us  [shards(): lax.all_to_all(partial_back, 'rep', split_axis=0, concat_axis=0, tiled=True)]
    dot_general x12 -> x10, matrix products: 11 us -> 10.2 us  [dot(): return jnp.einsum(spec, a, b, preferred_element_type=F32)]
  transfers between devices with their start and end apart: 5 -> 6, of which waited for: 4 -> 4; matrix products, arithmetic and copies ran while one was open for 3% -> 8% of each run, Pallas kernels for 0% -> 2%
where the time goes in v3:
time: 166 us; the launch traced here: 165 us
  blocking collectives  72.9 us (44%)
  starting transfers between devices  45.5 us (27%)
  waiting for transfers between devices  14.1 us (8%)
  matrix products  10.2 us (6%)
  local copies, waits for them, and re-layouts  8.63 us (5%)
  Pallas kernels  7.12 us (4%)
  other arithmetic  5.54 us (3%)
    all_to_all x3, blocking collectives, exchange(): lax.all_to_all(blocks, 'dom', split_axis=0, concat_axis=0, axis_index_gro...  63.6 us
    ppermute x3, starting transfers between devices, swap(): return lax.ppermute(rows, 'dom', [(p, p ^ 1) for p in range(128)])  18.9 us
    all_to_all x1, starting transfers between devices, shards(): lax.all_to_all(picked, DOM, split_axis=0, concat_axis=0, tiled=True)  18.4 us
    dot_general x10, matrix products, dot(): return jnp.einsum(spec, a, b, preferred_element_type=F32)  10.2 us
    all_to_all x1, blocking collectives, spread_rep(): lax.all_to_all(copies, 'rep', split_axis=0, concat_axis=0, tiled=True)  9.33 us
    all_to_all x1, waiting for transfers between devices, shards(): lax.all_to_all(picked, DOM, split_axis=0, concat_axis=0, tiled=True)  5.85 us
    all_to_all x1, waiting for transfers between devices, spread_rep(): lax.all_to_all(copies, 'rep', split_axis=0, concat_axis=0, tiled=True)  5.62 us
    all_to_all x1, starting transfers between devices, shards(): lax.all_to_all(partial_back, 'rep', split_axis=0, concat_axis=0, tiled=True)  4.13 us
  transfers between devices with their start and end apart: 6, of which 4 were waited for; matrix products, arithmetic and copies ran while one was open for 8% of the time, Pallas kernels for 2%

profile of v3, /device:TPU:1, one launch (start us, length us, event | category | flops | bytes accessed | tf_op | source)
XLA Modules:
  0.0 164.9 jit_solution(4737083413295418857)
XLA Ops:
  0.7 0.8 broadcast_add_fusion
  1.4 0.7 pad_add_fusion
  2.5 2.5 %fusion.5 = bf16[128,8,128]{2,1,0:T(8,128)(2,1)} fusion(s32[1024]{0:T(1024)S(1)} %eq.17, bf16[512,128]{1,0:T(8,128)(2,1)} %param.14, bf16[512,128]{1,0:T(8,128)(2,1)} %param.13), kind=kOutput, calls=%fused_computation.15 | convolution fusion | flops 270139392 | bytes 528384 | tf_op jit(solution)/shard_map/ab,bc->ac/dot_general | solution.py:20
  5.0 18.4 %all-to-all-start = ((bf16[128,8,128]{2,1,0:T(8,128)(2,1)}), bf16[128,8,128]{2,1,0:T(8,128)(2,1)S(1)}, u32[]{:S(2)}, u32[]{:S(2)}) async-start(bf16[128,8,128]{2,1,0:T(8,128)(2,1)} %fusion.5), calls=%async_computation | async-start | bytes 524288 | tf_op jit(solution)/shard_map/all_to_all | solution.py:193
  23.5 2.9 %gather_fusion.2 = bf16[4,512,128]{2,0,1:T(4,128)(2,1)S(1)} fusion(bf16[512,8,128]{2,1,0:T(8,128)(2,1)S(1)} %copy-done, s32[1024]{0:T(1024)S(1)} %pad_clamp_fusion), kind=kCustom, calls=%fused_computation.1.clone | custom fusion | bytes 1048592 | tf_op jit(solution)/shard_map/jit(_take)/gather | solution.py:211
  26.5 2.9 %gather_fusion.1 = bf16[4,512,128]{2,0,1:T(4,128)(2,1)S(1)} fusion(bf16[512,8,128]{2,1,0:T(8,128)(2,1)S(1)} %copy-done.2, s32[1024]{0:T(1024)S(1)} %pad_clamp_fusion), kind=kCustom, calls=%fused_computation.clone | custom fusion | bytes 1048592 | tf_op jit(solution)/shard_map/jit(_take)/gather | solution.py:205
  29.4 1.1 fusion.23
  30.5 1.3 fusion.2
  31.8 5.9 %all-to-all-done = bf16[128,8,128]{2,1,0:T(8,128)(2,1)S(1)} async-done(((bf16[128,8,128]{2,1,0:T(8,128)(2,1)}), bf16[128,8,128]{2,1,0:T(8,128)(2,1)S(1)}, u32[]{:S(2)}, u32[]{:S(2)}) %all-to-all-start) | async-done | bytes 262176 | tf_op jit(solution)/shard_map/all_to_all | solution.py:193
  37.6 0.6 gather_fusion
  38.6 0.9 broadcast_in_dim.37
  39.4 4.0 %all-to-all-start.1 = ((bf16[4,512,128]{2,1,0:T(8,128)(2,1)}), bf16[4,512,128]{2,1,0:T(8,128)(2,1)S(1)}, u32[]{:S(2)}, u32[]{:S(2)}) async-start(bf16[4,512,128]{2,1,0:T(8,128)(2,1)} %broadcast_in_dim.37), calls=%async_computation.1 | async-start | bytes 1048576 | tf_op jit(solution)/shard_map/all_to_all | solution.py:25
  43.5 1.5 broadcast_select_fusion
  45.0 5.6 %all-to-all-done.1.agg = bf16[4,512,128]{2,1,0:T(8,128)(2,1)S(1)} async-done(((bf16[4,512,128]{2,1,0:T(8,128)(2,1)}), bf16[4,512,128]{2,1,0:T(8,128)(2,1)S(1)}, u32[]{:S(2)}, u32[]{:S(2)}) %all-to-all-start.1) | async-done | bytes 524320 | tf_op jit(solution)/shard_map/all_to_all | solution.py:25
  50.6 2.0 %add_convert_fusion.3 = (bf16[4,128,128]{2,1,0:T(8,128)(2,1)S(1)}, f32[4,128,128]{2,1,0:T(8,128)}) fusion(bf16[4,128,128]{2,1,0:T(8,128)(2,1)S(1)} %bitcast.104, bf16[4,4,128,128]{3,2,1,0:T(8,128)(2,1)S(1)} %bitcast.85, bf16[4,128,4,128]{3,2,1,0:T(4,128)(2,1)} %bitcast.96), kind=kOutput, calls=%fused_computation.40 | convolution fusion | flops 67567616 | bytes 1572864 | tf_op jit(solution)/shard_map/qjrd,qdjc->jrc/dot_general | solution.py:20
  53.2 9.3 %all_to_all.35.agg = bf16[4,512,128]{2,1,0:T(8,128)(2,1)S(1)} all-to-all(bf16[4,512,128]{2,1,0:T(8,128)(2,1)S(1)} %broadcast_in_dim.39), channel_id=1, replica_groups=mesh['dom'=128,'rep'=4] {'rep'}, dimensions={0} | all-to-all | bytes 1048576 | tf_op jit(solution)/shard_map/all_to_all | solution.py:25
  62.5 1.0 fusion.14
  63.8 0.8 copy.31
  64.7 4.1 %all-to-all-start.3 = ((bf16[4,512,128]{2,1,0:T(8,128)(2,1)}), bf16[4,512,128]{2,1,0:T(8,128)(2,1)}, u32[]{:S(2)}, u32[]{:S(2)}) async-start(bf16[4,512,128]{2,1,0:T(8,128)(2,1)} %bitcast.36), calls=%async_computation.3 | async-start | bytes 1048576 | tf_op jit(solution)/shard_map/all_to_all | solution.py:218
  68.8 1.8 %grad_halves.3 = (f32[256,1024]{1,0:T(8,128)S(1)}, bf16[256,1024]{1,0:T(8,128)(2,1)}) custom-call(s32[4]{0:T(128)S(1)} %bitcast.89, s32[1]{0:T(128)} %bitcast.29.core, bf16[4,512,128]{2,1,0:T(8,128)(2,1)S(1)} %all_to_all.35.agg, bf16[512,128]{1,0:T(8,128)(2,1)S(1)} %bitcast.87), custom_call_target="tpu_custom_call" | custom-call | tf_op jit(solution)/shard_map/grad_halves/pallas_call | solution.py:60
  70.6 6.5 %collective-permute-start.1 = (bf16[256,1024]{1,0:T(8,128)(2,1)}, bf16[256,1024]{1,0:T(8,128)(2,1)}, u32[]{:S(2)}, u32[]{:S(2)}) collective-permute-start(bf16[256,1024]{1,0:T(8,128)(2,1)} %get-tuple-element.14), channel_id=1, source_target_pairs={{0,4},{4,0},{8,12},{12,8},{16,20},{20,16},{24,28},{28,24},{32,36},... | collective-permute-start | bytes 1572872 | tf_op jit(solution)/shard_map/ppermute | solution.py:160
  77.2 1.1 reduce_sum.12
  78.3 1.2 fusion.8
  79.5 1.3 grad_halves.2
  80.8 6.1 %collective-permute-start = (bf16[256,1024]{1,0:T(8,128)(2,1)S(1)}, bf16[256,1024]{1,0:T(8,128)(2,1)S(1)}, u32[]{:S(2)}, u32[]{:S(2)}) collective-permute-start(bf16[256,1024]{1,0:T(8,128)(2,1)S(1)} %get-tuple-element.12), channel_id=1, source_target_pairs={{0,4},{4,0},{8,12},{12,8},{16,20},{20,16},{24,28},{28,24},{32,36},... | collective-permute-start | bytes 1572872 | tf_op jit(solution)/shard_map/ppermute | solution.py:160
  86.9 1.2 add_convert_fusion
  88.7 22.1 %all_to_all.36.parts = bf16[8,64,1024]{2,1,0:T(8,128)(2,1)S(1)} all-to-all(bf16[8,64,1024]{2,1,0:T(8,128)(2,1)S(1)} %pad_maximum_fusion), channel_id=1, replica_groups={{0,64,128,192,256,320,384,448},{8,72,136,200,264,328,392,456},{16,80,14..., dimensions={0} | all-to-all | bytes 2097152 | tf_op jit(solution)/shard_map/all_to_all | solution.py:154
  111.0 21.3 %all_to_all.37.parts = bf16[8,64,1024]{2,1,0:T(8,128)(2,1)S(1)} all-to-all(bf16[8,64,1024]{2,1,0:T(8,128)(2,1)S(1)} %first_sum.1), channel_id=1, replica_groups={{0,8,16,24,32,40,48,56},{64,72,80,88,96,104,112,120},{128,136,144,152,1..., dimensions={0} | all-to-all | bytes 2097152 | tf_op jit(solution)/shard_map/all_to_all | solution.py:154
  132.7 20.2 %all_to_all.38.same = bf16[8,512,128]{2,1,0:T(8,128)(2,1)S(1)} all-to-all(bf16[8,512,128]{2,1,0:T(8,128)(2,1)S(1)} %second_sum.1), channel_id=1, replica_groups={{0,64,128,192,256,320,384,448},{8,72,136,200,264,328,392,456},{16,80,14..., dimensions={0} | all-to-all | bytes 2097152 | tf_op jit(solution)/shard_map/all_to_all | solution.py:154
  152.9 6.3 %collective-permute-start.2 = (bf16[8,512,128]{2,1,0:T(8,128)(2,1)S(1)}, bf16[8,512,128]{2,1,0:T(8,128)(2,1)S(1)}, u32[]{:S(2)}, u32[]{:S(2)}) collective-permute-start(bf16[8,512,128]{2,1,0:T(8,128)(2,1)S(1)} %all_to_all.38.same), channel_id=1, source_target_pairs={{0,4},{4,0},{8,12},{12,8},{16,20},{20,16},{24,28},{28,24},{32,36},... | collective-permute-start | bytes 3145736 | tf_op jit(solution)/shard_map/ppermute | solution.py:160
  159.1 2.3 %collective-permute-done.2.other = bf16[8,512,128]{2,1,0:T(8,128)(2,1)S(1)} collective-permute-done((bf16[8,512,128]{2,1,0:T(8,128)(2,1)S(1)}, bf16[8,512,128]{2,1,0:T(8,128)(2,1)S(1)}, u32[]{:S(2)}, u32[]{:S(2)}) %collective-permute-start.2) | collective-permute-done | bytes 1048608 | tf_op jit(solution)/shard_map/ppermute | solution.py:160
  161.4 3.5 %widen.1 = (f32[4096,128]{1,0:T(8,128)}, f32[4096,128]{1,0:T(8,128)}) custom-call(s32[1]{0:T(128)} %bitcast.29.core, bf16[8,512,128]{2,1,0:T(8,128)(2,1)S(1)} %all_to_all.38.same, bf16[8,512,128]{2,1,0:T(8,128)(2,1)S(1)} %collective-permute-done.2.other), custom_call_target="tpu_custom_call" | custom-call | tf_op jit(solution)/shard_map/widen/pallas_call | solution.py:136
  (44 shorter events, 2.7 us)
Async XLA Ops:
  0.6 22.9 %copy-start = (bf16[512,8,128]{2,1,0:T(8,128)(2,1)S(1)}, bf16[512,8,128]{2,1,0:T(8,128)(2,1)}, u32[]{:S(2)}) copy-start(bf16[512,8,128]{2,1,0:T(8,128)(2,1)} %param.21) | copy-start | bytes 3145732
  0.6 22.8 %copy-start.11 = (s32[1,4]{1,0:T(1,128)S(1)}, s32[1,4]{1,0:T(1,128)}, u32[]{:S(2)}) copy-start(s32[1,4]{1,0:T(1,128)} %param.18) | copy-start | bytes 52
  0.7 22.8 %copy-start.1 = (s32[1,4]{1,0:T(1,128)S(1)}, s32[1,4]{1,0:T(1,128)}, u32[]{:S(2)}) copy-start(s32[1,4]{1,0:T(1,128)} %param.19) | copy-start | bytes 52
  5.0 32.7 %all-to-all-start = ((bf16[128,8,128]{2,1,0:T(8,128)(2,1)}), bf16[128,8,128]{2,1,0:T(8,128)(2,1)S(1)}, u32[]{:S(2)}, u32[]{:S(2)}) async-start(bf16[128,8,128]{2,1,0:T(8,128)(2,1)} %fusion.5), calls=%async_computation | async-start | bytes 524288 | tf_op jit(solution)/shard_map/all_to_all | solution.py:193
  23.5 3.0 %copy-start.2 = (bf16[512,8,128]{2,1,0:T(8,128)(2,1)S(1)}, bf16[512,8,128]{2,1,0:T(8,128)(2,1)}, u32[]{:S(2)}) copy-start(bf16[512,8,128]{2,1,0:T(8,128)(2,1)} %param.20) | copy-start | bytes 3145732
  26.5 3.0 %copy-start.6 = (bf16[512,128]{1,0:T(8,128)(2,1)S(1)}, bf16[512,128]{1,0:T(8,128)(2,1)}, u32[]{:S(2)}) copy-start(bf16[512,128]{1,0:T(8,128)(2,1)} %param.15) | copy-start | bytes 393220
  31.8 7.6 %copy-start.3 = (bf16[2,4,128,256]{2,3,1,0:T(8,128)(2,1)}, bf16[2,4,128,256]{2,3,1,0:T(8,128)(2,1)S(1)}, u32[]{:S(2)}) copy-start(bf16[2,4,128,256]{2,3,1,0:T(8,128)(2,1)S(1)} %fusion.2) | copy-start | bytes 1572868
  38.5 12.0 %copy-start.8 = (bf16[512,128]{1,0:T(8,128)(2,1)S(1)}, bf16[512,128]{1,0:T(8,128)(2,1)}, u32[]{:S(2)}) copy-start(bf16[512,128]{1,0:T(8,128)(2,1)} %param.13) | copy-start | bytes 393220
  39.4 11.2 %all-to-all-start.1 = ((bf16[4,512,128]{2,1,0:T(8,128)(2,1)}), bf16[4,512,128]{2,1,0:T(8,128)(2,1)S(1)}, u32[]{:S(2)}, u32[]{:S(2)}) async-start(bf16[4,512,128]{2,1,0:T(8,128)(2,1)} %broadcast_in_dim.37), calls=%async_computation.1 | async-start | bytes 1048576 | tf_op jit(solution)/shard_map/all_to_all | solution.py:25
  43.4 9.2 %copy-start.7 = (bf16[512,128]{1,0:T(8,128)(2,1)S(1)}, bf16[512,128]{1,0:T(8,128)(2,1)}, u32[]{:S(2)}) copy-start(bf16[512,128]{1,0:T(8,128)(2,1)} %param.15) | copy-start | bytes 393220
  45.0 7.9 %copy-start.4 = (bf16[2,4,128,256]{2,3,1,0:T(8,128)(2,1)S(1)}, bf16[2,4,128,256]{2,3,1,0:T(8,128)(2,1)}, u32[]{:S(2)}) copy-start(bf16[2,4,128,256]{2,3,1,0:T(8,128)(2,1)} %copy-done.3) | copy-start | bytes 1572868
  52.6 10.9 %copy-start.9 = (bf16[4,128,128]{2,1,0:T(8,128)(2,1)}, bf16[4,128,128]{2,1,0:T(8,128)(2,1)S(1)}, u32[]{:S(2)}) copy-start(bf16[4,128,128]{2,1,0:T(8,128)(2,1)S(1)} %get-tuple-element.21) | copy-start | bytes 393220
  52.6 9.9 %copy-start.5 = (bf16[4,512,128]{2,0,1:T(4,128)(2,1)S(1)}, bf16[4,512,128]{2,0,1:T(4,128)(2,1)}, u32[]{:S(2)}) copy-start(bf16[4,512,128]{2,0,1:T(4,128)(2,1)} %get-tuple-element.19) | copy-start | bytes 1572868
  52.6 9.9 %copy-start.10 = (bf16[512,128]{1,0:T(8,128)(2,1)S(1)}, bf16[512,128]{1,0:T(8,128)(2,1)}, u32[]{:S(2)}) copy-start(bf16[512,128]{1,0:T(8,128)(2,1)} %param.22) | copy-start | bytes 393220
  64.7 12.5 %all-to-all-start.3 = ((bf16[4,512,128]{2,1,0:T(8,128)(2,1)}), bf16[4,512,128]{2,1,0:T(8,128)(2,1)}, u32[]{:S(2)}, u32[]{:S(2)}) async-start(bf16[4,512,128]{2,1,0:T(8,128)(2,1)} %bitcast.36), calls=%async_computation.3 | async-start | bytes 1048576 | tf_op jit(solution)/shard_map/all_to_all | solution.py:218
  70.6 16.3 %collective-permute-start.1 = (bf16[256,1024]{1,0:T(8,128)(2,1)}, bf16[256,1024]{1,0:T(8,128)(2,1)}, u32[]{:S(2)}, u32[]{:S(2)}) collective-permute-start(bf16[256,1024]{1,0:T(8,128)(2,1)} %get-tuple-element.14), channel_id=1, source_target_pairs={{0,4},{4,0},{8,12},{12,8},{16,20},{20,16},{24,28},{28,24},{32,36},... | collective-permute-start | bytes 1572872 | tf_op jit(solution)/shard_map/ppermute | solution.py:160
  80.8 7.6 %collective-permute-start = (bf16[256,1024]{1,0:T(8,128)(2,1)S(1)}, bf16[256,1024]{1,0:T(8,128)(2,1)S(1)}, u32[]{:S(2)}, u32[]{:S(2)}) collective-permute-start(bf16[256,1024]{1,0:T(8,128)(2,1)S(1)} %get-tuple-element.12), channel_id=1, source_target_pairs={{0,4},{4,0},{8,12},{12,8},{16,20},{20,16},{24,28},{28,24},{32,36},... | collective-permute-start | bytes 1572872 | tf_op jit(solution)/shard_map/ppermute | solution.py:160
  152.9 8.5 %collective-permute-start.2 = (bf16[8,512,128]{2,1,0:T(8,128)(2,1)S(1)}, bf16[8,512,128]{2,1,0:T(8,128)(2,1)S(1)}, u32[]{:S(2)}, u32[]{:S(2)}) collective-permute-start(bf16[8,512,128]{2,1,0:T(8,128)(2,1)S(1)} %all_to_all.38.same), channel_id=1, source_target_pairs={{0,4},{4,0},{8,12},{12,8},{16,20},{20,16},{24,28},{28,24},{32,36},... | collective-permute-start | bytes 3145736 | tf_op jit(solution)/shard_map/ppermute | solution.py:160

commit v4 on v0

v4 whole, which is shorter than its diff:
```python
import jax
import jax.numpy as jnp
from jax import lax
from jax.experimental import pallas as pl
from jax.experimental.pallas import tpu as pltpu
from jax.sharding import PartitionSpec as P

BF = jnp.bfloat16
F32 = jnp.float32
SMEM = pl.BlockSpec(memory_space=pltpu.SMEM)
VMEM = pl.BlockSpec(memory_space=pltpu.VMEM)
ANY = pl.BlockSpec(memory_space=pl.ANY)
PARAMS = pltpu.CompilerParams(vmem_limit_bytes=40 << 20)
PAIR = 2
RING = 16
CROSS = 4
REPS = 4
TILE = 128


def call(body, name, ins, outs, scratch=()):
    return pl.pallas_call(
        body,
        out_shape=tuple(jax.ShapeDtypeStruct(shape, kind) for shape, kind in outs),
        in_specs=list(ins),
        out_specs=tuple(VMEM for _ in outs),
        scratch_shapes=list(scratch),
        compiler_params=PARAMS,
        name=name,
    )


def dot(a, b, dims=((1,), (0,))):
    return lax.dot_general(a, b, (dims, ((), ())), preferred_element_type=F32)


def block(j):
    return slice(j * TILE, (j + 1) * TILE)


def iota(shape, axis):
    return lax.broadcasted_iota(jnp.int32, shape, axis)


def pick_body(send, feats, hist, out, rows):
    cap, parts = send.shape
    nodes, cols = feats.shape
    table = jnp.concatenate([feats[...], hist[...]], axis=1)
    for c in range(cap):
        hit = (iota((nodes, parts), 0) == send[c : c + 1, :]).astype(F32).astype(BF)
        got = dot(hit, table, ((0,), (0,)))
        rows[:, c, :] = got[:, :cols]
        rows[:, cap + c, :] = got[:, cols:]
    out[...] = rows[...].astype(BF)


def select_body(types, weights, out):
    rows, width, _ = out.shape
    experts = weights.shape[0] // width
    span = TILE // rows
    shape = (rows * span, span * experts)
    at, source = iota(shape, 0), iota(shape, 1)
    kind = jnp.zeros(shape, jnp.int32)
    for j in range(rows):
        kind = jnp.where(at // span == j, types[j], kind)
    hit = (source == (at % span) * experts + kind).astype(F32).astype(BF)
    for i in range(width // span):
        got = dot(hit, weights[i * span * experts : (i + 1) * span * experts, :]).astype(BF)
        for j in range(rows):
            out[j, i * span : (i + 1) * span, :] = got[j * span : (j + 1) * span]


def ready_body(local, halo_val, feats, base, wide):
    cap = wide.shape[2] // 2 // 32
    shape = (TILE, 2 * TILE)
    k, m = iota(shape, 0), iota(shape, 1)
    spot = (k // cap) * (2 * cap) + k % cap
    first = (m == spot).astype(F32).astype(BF)
    second = (m == spot + cap).astype(F32).astype(BF)
    for j in range(wide.shape[0]):
        base[block(j), :] = dot(local[block(j), :], feats[block(j), :])
        wide[j, :TILE, :] = dot(halo_val[block(j), :], first).astype(BF)
        wide[j, TILE:, :] = dot(halo_val[block(j), :], second).astype(BF)


def gather_body(pick, landed, wide, base, copies, part):
    for j in range(wide.shape[0]):
        both = dot(wide[j], landed[pick[j]])
        agg = (base[block(j), :] + both[:TILE]).astype(BF)
        part[block(j), :] = both[TILE:]
        for q in range(copies.shape[0]):
            copies[q, block(j), :] = agg


def forward(agg, weights, j):
    rows = jnp.concatenate([agg[q, block(j), :] for q in range(agg.shape[0])], axis=1)
    z = dot(rows, weights[j])
    sig = jax.nn.sigmoid(z)
    return z * sig, sig * (1.0 + z * (1.0 - sig))


def one_body(agg, weights, feats, local, part, hidden, slope, copies):
    for j in range(weights.shape[0]):
        act, bend = forward(agg, weights, j)
        slope[block(j), :] = bend
        h = (feats[block(j), :].astype(F32) + act).astype(BF)
        hidden[block(j), :] = h
        mixed = (dot(local[block(j), :], h) + part[block(j), :]).astype(BF)
        for q in range(copies.shape[0]):
            copies[q, block(j), :] = mixed


def two_body(agg, weights, h_one, grad, hidden, dz, back):
    cols = dz.shape[1]
    for j in range(weights.shape[0]):
        act, bend = forward(agg, weights, j)
        hidden[block(j), :] = (h_one[block(j), :].astype(F32) + act).astype(BF)
        d = (grad[block(j), :].astype(F32) * bend).astype(BF)
        dz[block(j), :] = d
        term = dot(d, weights[j], ((1,), (1,))).astype(BF)
        for q in range(back.shape[0]):
            back[q, block(j), :] = term[:, q * cols : (q + 1) * cols]


def write_grad(types, core, agg, dz, keep, send):
    reps, _, cols = agg.shape
    rows = types.shape[0]
    experts = keep.shape[1] // cols
    wide = []
    for e in range(experts):
        part = []
        for j in range(rows):
            part.append((dz[block(j), :].astype(F32) * (types[j] == e).astype(F32)).astype(BF))
        wide.append(jnp.concatenate(part, axis=0))
    wide = jnp.concatenate(wide, axis=1)
    for target, side in ((send, 1 - core[0]), (keep, core[0])):
        for i in range(reps // 2):
            got = dot(agg[side * (reps // 2) + i], wide, ((0,), (0,)))
            target[i * cols : (i + 1) * cols, :] = got.astype(target.dtype)


def back_body(types, core, parts, local, grad, slope, agg, keep, send, dz):
    for j in range(types.shape[0]):
        total = parts[0, block(j), :].astype(F32)
        for q in range(1, parts.shape[0]):
            total = total + parts[q, block(j), :].astype(F32)
        dh = grad[block(j), :].astype(F32) + dot(
            local[block(j), :], total.astype(BF), ((0,), (0,))
        )
        dz[block(j), :] = (dh * slope[block(j), :]).astype(BF)
    write_grad(types, core, agg, dz, keep, send)


def add_up(parts):
    total = parts[0].astype(F32)
    for i in range(1, parts.shape[0]):
        total = total + parts[i].astype(F32)
    return total


def first_body(parts, copies):
    total = add_up(parts).astype(BF)
    for i in range(copies.shape[0]):
        copies[i] = total


def second_body(parts, copies, table):
    rows, experts, cols = table.shape
    total = add_up(parts)
    for e in range(experts):
        table[:, e, :] = total[:, e * cols : (e + 1) * cols]
    laid = table[...].reshape(rows * experts, cols).astype(BF)
    for i in range(copies.shape[0]):
        copies[i] = laid


def widen_body(core, half, *refs):
    one, two = refs[-2:]
    step = pl.program_id(0)
    length = half.shape[1] // 2
    count = one.shape[0] // length
    for i in range(count):
        rows = half[step * count + i].astype(F32)
        one[i * length : (i + 1) * length, :] = rows[:length]
        two[i * length : (i + 1) * length, :] = rows[length:]


def widen(core, half, before=()):
    chunks, length, cols = half.shape
    steps = 4
    own = not before
    height = chunks // steps * (length // 2)
    target = pl.BlockSpec(
        (height, cols), lambda i, c: ((c[0] if own else 1 - c[0]) * steps + i, 0)
    )
    shape = jax.ShapeDtypeStruct((chunks * length, cols), F32)
    return pl.pallas_call(
        widen_body,
        grid_spec=pltpu.PrefetchScalarGridSpec(
            num_scalar_prefetch=1,
            grid=(steps,),
            in_specs=[VMEM] + [ANY] * len(before),
            out_specs=(target, target),
        ),
        out_shape=(shape, shape),
        input_output_aliases={} if own else {2: 0, 3: 1},
        compiler_params=PARAMS,
        name="widen_own" if own else "widen_other",
    )(core, half, *before)


def rings():
    def device(core, line, cross):
        y, z = (line, cross) if core == 0 else (cross, line)
        return (y * 8 + z) * 2 + core

    first = [
        [device(core, line, pair * PAIR + i) for i in range(PAIR) for line in range(8)]
        for core in range(2)
        for pair in range(8 // PAIR)
    ]
    second = [
        [device(core, line, pair * PAIR + i) for pair in range(8 // PAIR)]
        for core in range(2)
        for line in range(8)
        for i in range(PAIR)
    ]
    return first, second


def exchange(blocks, groups):
    return lax.all_to_all(
        blocks, "dom", split_axis=0, concat_axis=0, axis_index_groups=groups, tiled=True
    )


def across(blocks):
    return lax.all_to_all(blocks, "rep", split_axis=0, concat_axis=0, tiled=True)


def swap(rows):
    return lax.ppermute(rows, "dom", [(p, p ^ 1) for p in range(128)])


def shards(
    feats, hist_one, local_val, halo_val, halo_send, halo_tile, tile_type, w_one, w_two, grad_out
):
    nodes, cols = feats.shape
    rows = nodes // TILE
    width, experts, _ = w_one.shape
    parts, cap = halo_send.shape[1], halo_send.shape[2]
    pick, types = halo_tile[0], tile_type[0]
    core = lax.rem(lax.axis_index("dom"), 2).astype(jnp.int32).reshape(1)
    first, second = rings()
    flat = (nodes, cols)
    copied = (REPS, nodes, cols)

    (rows_out,) = call(
        pick_body,
        "pick",
        [VMEM] * 3,
        [((parts, 2 * cap, cols), BF)],
        [pltpu.VMEM((parts, 2 * cap, cols), F32)],
    )(jnp.swapaxes(halo_send[0], 0, 1), feats, hist_one)
    landed = lax.all_to_all(rows_out, "dom", split_axis=0, concat_axis=0, tiled=True)
    landed = landed.reshape(rows, 2 * TILE, cols)

    select = call(select_body, "select", [SMEM, VMEM], [((rows, width, cols), BF)])
    (pick_one,) = select(types, w_one.reshape(width * experts, cols))
    (pick_two,) = select(types, w_two.reshape(width * experts, cols))
    base, wide = call(
        ready_body, "ready", [VMEM] * 3, [(flat, F32), ((rows, 2 * TILE, 2 * TILE), BF)]
    )(local_val, halo_val, feats)

    copies, part = call(gather_body, "gather", [SMEM] + [VMEM] * 3, [(copied, BF), (flat, F32)])(
        pick, landed, wide, base
    )
    agg_one = across(copies)
    h_one, slope, copies = call(
        one_body, "one", [VMEM] * 5, [(flat, BF), (flat, F32), (copied, BF)]
    )(agg_one, pick_one, feats, local_val, part)
    agg_two = across(copies)
    h_two, dz_two, back = call(
        two_body, "two", [VMEM] * 4, [(flat, BF), (flat, BF), (copied, BF)]
    )(agg_two, pick_two, h_one, grad_out)
    back = across(back)

    half = (width // 2, experts * cols)
    keep_two, send_two = call(
        write_grad, "grad_two", [SMEM] * 2 + [VMEM] * 2, [(half, F32), (half, BF)]
    )(types, core, agg_two, dz_two)
    keep_one, send_one = call(
        back_body,
        "back",
        [SMEM] * 2 + [VMEM] * 5,
        [(half, F32), (half, BF)],
        [pltpu.VMEM(flat, BF)],
    )(types, core, back, local_val, grad_out, slope, agg_one)
    pair_one = (keep_one + swap(send_one).astype(F32)).astype(BF)
    pair_two = (keep_two + swap(send_two).astype(F32)).astype(BF)

    split = (RING, width // 2 // RING, experts * cols)
    both = jnp.concatenate([pair_one.reshape(split), pair_two.reshape(split)], axis=1)
    both = exchange(both, first)
    few = both.shape[1]
    (both,) = call(first_body, "first_sum", [VMEM], [((CROSS,) + both.shape[1:], BF)])(both)
    both = exchange(both, second)
    (both,) = call(
        second_body,
        "second_sum",
        [VMEM],
        [((RING, few * experts, cols), BF)],
        [pltpu.VMEM((few, experts, cols), F32)],
    )(both)
    same = exchange(both, first)
    grad_one, grad_two = widen(core, swap(same), widen(core, same))
    return h_two, h_one, grad_one.reshape(w_one.shape), grad_two.reshape(w_two.shape)


def solution(mesh):
    in_specs = (
        P("dom", "rep"),
        P("dom", "rep"),
        P("dom", None),
        P("dom", None),
        P("dom", None, None),
        P("dom", None),
        P("dom", None),
        P(None, None, "rep"),
        P(None, None, "rep"),
        P("dom", "rep"),
    )
    out_specs = (P("dom", "rep"), P("dom", "rep"), P(None, None, "rep"), P(None, None, "rep"))
    return jax.shard_map(shards, mesh=mesh, in_specs=in_specs, out_specs=out_specs, check_vma=False)
```

time: 366 us -> 156 us (0.43)
  waiting for transfers between devices: 234 us -> 25.4 us
  Pallas kernels: 0 us -> 15.7 us
  blocking collectives: 47.8 us -> 63.4 us
  between operations: 14.4 us -> 0.82 us
  local copies, waits for them, and re-layouts: 19.3 us -> 5.88 us
  matrix products: 9.73 us -> 0 us
  starting transfers between devices: 34.7 us -> 44 us
    psum x1 -> x0, waiting for transfers between devices: 207 us -> none  [shards(): lax.psum((grad_term(agg_one, dz_one, onehot), grad_term(agg_two, dz_two,...]
    all_to_all x0 -> x3, blocking collectives: none -> 63.4 us  [exchange(): lax.all_to_all(blocks, 'dom', split_axis=0, concat_axis=0, axis_index_gro...]
    all_gather x4 -> x0, blocking collectives: 47.8 us -> none  [the longest x2 24.1 us: mix_layer(): lax.all_gather(halo, 'rep', axis=1, tiled=True)]
    unnamed x3 -> x0, waiting for transfers between devices: 26.3 us -> none
    all_to_all x2 -> x4, waiting for transfers between devices: 0.53 us -> 23.3 us  [the longest x3 12.1 us: across(): lax.all_to_all(blocks, 'rep', split_axis=0, concat_axis=0, tiled=True)]
    pallas_call x0 -> x13, Pallas kernels: none -> 15.7 us  [the longest x2 3.67 us: widen(): pl.pallas_call(widen_body, grid_spec=pltpu.PrefetchScalarGridSpec(num_sca...]
    ppermute x0 -> x3, starting transfers between devices: none -> 14.5 us  [swap(): return lax.ppermute(rows, 'dom', [(p, p ^ 1) for p in range(128)])]
    gather x6 -> x0, local copies, waits for them, and re-layouts: 11.4 us -> none  [the longest x2 5.86 us: expert_forward(): chosen = jnp.take(weights, types, axis=1)]
  transfers between devices with their start and end apart: 4 -> 7, of which waited for: 3 -> 5; matrix products, arithmetic and copies ran while one was open for 3% -> 0% of each run, Pallas kernels for 0% -> 5%
where the time goes in v4:
time: 156 us
  blocking collectives  63.4 us (41%)
  starting transfers between devices  44 us (28%)
  waiting for transfers between devices  25.4 us (16%)
  Pallas kernels  15.7 us (10%)
  local copies, waits for them, and re-layouts  5.88 us (4%)
    all_to_all x3, blocking collectives, exchange(): lax.all_to_all(blocks, 'dom', split_axis=0, concat_axis=0, axis_index_gro...  63.4 us
    all_to_all x1, starting transfers between devices, shards(): lax.all_to_all(rows_out, 'dom', split_axis=0, concat_axis=0, tiled=True)  18.4 us
    ppermute x3, starting transfers between devices, swap(): return lax.ppermute(rows, 'dom', [(p, p ^ 1) for p in range(128)])  14.5 us
    all_to_all x3, waiting for transfers between devices, across(): lax.all_to_all(blocks, 'rep', split_axis=0, concat_axis=0, tiled=True)  12.1 us
    all_to_all x1, waiting for transfers between devices, shards(): lax.all_to_all(rows_out, 'dom', split_axis=0, concat_axis=0, tiled=True)  11.2 us
    all_to_all x3, starting transfers between devices, across(): lax.all_to_all(blocks, 'rep', split_axis=0, concat_axis=0, tiled=True)  11.1 us
    unnamed x28, local copies, waits for them, and re-layouts  5.88 us
    pallas_call x2, Pallas kernels, widen(): pl.pallas_call(widen_body, grid_spec=pltpu.PrefetchScalarGridSpec(num_sca...  3.67 us
  transfers between devices with their start and end apart: 7, of which 5 were waited for; matrix products, arithmetic and copies ran while one was open for 0% of the time, Pallas kernels for 5%

profile of v4, /device:TPU:1, one launch (start us, length us, event | category | flops | bytes accessed | tf_op | source)
XLA Modules:
  0.0 155.6 jit_solution(11079339198093411706)
XLA Ops:
  0.7 0.9 copy-done
  1.6 0.9 copy-done.10
  2.5 0.7 copy-done.12
  3.1 1.3 pick.1
  4.4 18.4 %all-to-all-start = ((bf16[128,8,128]{2,1,0:T(8,128)(2,1)}), bf16[128,8,128]{2,1,0:T(8,128)(2,1)S(1)}, u32[]{:S(2)}, u32[]{:S(2)}) async-start(bf16[128,8,128]{2,1,0:T(8,128)(2,1)} %pick.1), calls=%async_computation | async-start | bytes 524288 | tf_op jit(solution)/shard_map/all_to_all | solution.py:265
  22.9 0.9 copy-done.1
  23.8 0.9 copy-done.3
  24.7 0.9 copy-done.8
  25.9 11.2 %all-to-all-done = bf16[128,8,128]{2,1,0:T(8,128)(2,1)S(1)} async-done(((bf16[128,8,128]{2,1,0:T(8,128)(2,1)}), bf16[128,8,128]{2,1,0:T(8,128)(2,1)S(1)}, u32[]{:S(2)}, u32[]{:S(2)}) %all-to-all-start) | async-done | bytes 262176 | tf_op jit(solution)/shard_map/all_to_all | solution.py:265
  37.1 0.7 copy-done.13
  37.7 1.6 %gather.1 = (bf16[4,512,128]{2,1,0:T(8,128)(2,1)}, f32[512,128]{1,0:T(8,128)S(1)}) custom-call(s32[4]{0:T(128)S(1)} %bitcast.21, bf16[4,256,128]{2,1,0:T(8,128)(2,1)S(1)} %bitcast.15, bf16[4,256,256]{2,1,0:T(8,128)(2,1)S(1)} %get-tuple-element.22.wide, f32[512,128]{1,0:T(8,128)S(1)} %get-tuple-element.23.base), custom_call_target="tpu_custom_call" | custom-call | tf_op jit(solution)/shard_map/gather/pallas_call | solution.py:275
  39.3 4.0 %all-to-all-start.1 = ((bf16[4,512,128]{2,1,0:T(8,128)(2,1)}), bf16[4,512,128]{2,1,0:T(8,128)(2,1)S(1)}, u32[]{:S(2)}, u32[]{:S(2)}) async-start(bf16[4,512,128]{2,1,0:T(8,128)(2,1)} %get-tuple-element.24), calls=%async_computation.1 | async-start | bytes 1048576 | tf_op jit(solution)/shard_map/all_to_all | solution.py:238
  43.3 1.0 select.4.weights
  44.3 6.2 %all-to-all-done.1.agg = bf16[4,512,128]{2,1,0:T(8,128)(2,1)S(1)} async-done(((bf16[4,512,128]{2,1,0:T(8,128)(2,1)}), bf16[4,512,128]{2,1,0:T(8,128)(2,1)S(1)}, u32[]{:S(2)}, u32[]{:S(2)}) %all-to-all-start.1) | async-done | bytes 524320 | tf_op jit(solution)/shard_map/all_to_all | solution.py:238
  50.5 1.7 %one.1 = (bf16[512,128]{1,0:T(8,128)(2,1)}, f32[512,128]{1,0:T(8,128)S(1)}, bf16[4,512,128]{2,1,0:T(8,128)(2,1)}) custom-call(bf16[4,512,128]{2,1,0:T(8,128)(2,1)S(1)} %all-to-all-done.1.agg, bf16[4,512,128]{2,1,0:T(8,128)(2,1)S(1)} %select.4.weights, bf16[512,128]{1,0:T(8,128)(2,1)S(1)} %copy-done.2, bf16[512,128]{1,0:T(8,128)(2,1)S(1)} %copy-done.4, ...), custom_call_target="tpu_custom_call" | custom-call | tf_op jit(solution)/shard_map/one/pallas_call | solution.py:279
  52.2 3.6 %all-to-all-start.2 = ((bf16[4,512,128]{2,1,0:T(8,128)(2,1)}), bf16[4,512,128]{2,1,0:T(8,128)(2,1)S(1)}, u32[]{:S(2)}, u32[]{:S(2)}) async-start(bf16[4,512,128]{2,1,0:T(8,128)(2,1)} %get-tuple-element.26), calls=%async_computation.2 | async-start | bytes 1048576 | tf_op jit(solution)/shard_map/all_to_all | solution.py:238
  55.8 1.0 select.5.weights
  56.8 5.9 %all-to-all-done.2.agg = bf16[4,512,128]{2,1,0:T(8,128)(2,1)S(1)} async-done(((bf16[4,512,128]{2,1,0:T(8,128)(2,1)}), bf16[4,512,128]{2,1,0:T(8,128)(2,1)S(1)}, u32[]{:S(2)}, u32[]{:S(2)}) %all-to-all-start.2) | async-done | bytes 524320 | tf_op jit(solution)/shard_map/all_to_all | solution.py:238
  62.7 1.7 %two.1 = (bf16[512,128]{1,0:T(8,128)(2,1)}, bf16[512,128]{1,0:T(8,128)(2,1)S(1)}, bf16[4,512,128]{2,1,0:T(8,128)(2,1)}) custom-call(bf16[4,512,128]{2,1,0:T(8,128)(2,1)S(1)} %all-to-all-done.2.agg, bf16[4,512,128]{2,1,0:T(8,128)(2,1)S(1)} %select.5.weights, bf16[512,128]{1,0:T(8,128)(2,1)S(1)} %copy-done.9, bf16[512,128]{1,0:T(8,128)(2,1)S(1)} %copy-done.7), custom_call_target="tpu_custom_call" | custom-call | tf_op jit(solution)/shard_map/two/pallas_call | solution.py:283
  64.3 3.5 %all-to-all-start.3 = ((bf16[4,512,128]{2,1,0:T(8,128)(2,1)}), bf16[4,512,128]{2,1,0:T(8,128)(2,1)S(1)}, u32[]{:S(2)}, u32[]{:S(2)}) async-start(bf16[4,512,128]{2,1,0:T(8,128)(2,1)} %get-tuple-element.29), calls=%async_computation.3 | async-start | bytes 1048576 | tf_op jit(solution)/shard_map/all_to_all | solution.py:238
  67.8 1.8 %grad_two.1 = (f32[256,1024]{1,0:T(8,128)S(1)}, bf16[256,1024]{1,0:T(8,128)(2,1)}) custom-call(s32[4]{0:T(128)S(1)} %bitcast.18, s32[1]{0:T(128)} %bitcast.7.core, bf16[4,512,128]{2,1,0:T(8,128)(2,1)S(1)} %all-to-all-done.2.agg, bf16[512,128]{1,0:T(8,128)(2,1)S(1)} %get-tuple-element.33.dz), custom_call_target="tpu_custom_call" | custom-call | tf_op jit(solution)/shard_map/grad_two/pallas_call | solution.py:289
  69.6 6.3 %collective-permute-start.1 = (bf16[256,1024]{1,0:T(8,128)(2,1)}, bf16[256,1024]{1,0:T(8,128)(2,1)S(1)}, u32[]{:S(2)}, u32[]{:S(2)}) collective-permute-start(bf16[256,1024]{1,0:T(8,128)(2,1)} %get-tuple-element.35), channel_id=1, source_target_pairs={{0,4},{4,0},{8,12},{12,8},{16,20},{20,16},{24,28},{28,24},{32,36},... | collective-permute-start | bytes 1572872 | tf_op jit(solution)/shard_map/ppermute | solution.py:242
  76.0 1.5 back.1
  77.5 6.2 %collective-permute-start = (bf16[256,1024]{1,0:T(8,128)(2,1)S(1)}, bf16[256,1024]{1,0:T(8,128)(2,1)S(1)}, u32[]{:S(2)}, u32[]{:S(2)}) collective-permute-start(bf16[256,1024]{1,0:T(8,128)(2,1)S(1)} %get-tuple-element.32), channel_id=1, source_target_pairs={{0,4},{4,0},{8,12},{12,8},{16,20},{20,16},{24,28},{28,24},{32,36},... | collective-permute-start | bytes 1572872 | tf_op jit(solution)/shard_map/ppermute | solution.py:242
  83.9 1.4 collective-permute-done
  85.5 25.7 %all_to_all.35.parts = bf16[16,32,1024]{2,1,0:T(8,128)(2,1)S(1)} all-to-all(bf16[16,32,1024]{2,1,0:T(8,128)(2,1)S(1)} %pad_maximum_fusion), channel_id=1, replica_groups={{0,64,128,192,256,320,384,448,8,72,136,200,264,328,392,456},{16,80,144,..., dimensions={0} | all-to-all | bytes 2097152 | tf_op jit(solution)/shard_map/all_to_all | solution.py:232
  111.3 11.7 %all_to_all.36.parts = bf16[4,32,1024]{2,1,0:T(8,128)(2,1)S(1)} all-to-all(bf16[4,32,1024]{2,1,0:T(8,128)(2,1)S(1)} %first_sum.1), channel_id=1, replica_groups={{0,16,32,48},{8,24,40,56},{64,80,96,112},{72,88,104,120},{128,144,160,1..., dimensions={0} | all-to-all | bytes 524288 | tf_op jit(solution)/shard_map/all_to_all | solution.py:232
  123.2 26.0 %all_to_all.37.half = bf16[16,256,128]{2,1,0:T(8,128)(2,1)S(1)} all-to-all(bf16[16,256,128]{2,1,0:T(8,128)(2,1)S(1)} %second_sum.1), channel_id=1, replica_groups={{0,64,128,192,256,320,384,448,8,72,136,200,264,328,392,456},{16,80,144,..., dimensions={0} | all-to-all | bytes 2097152 | tf_op jit(solution)/shard_map/all_to_all | solution.py:232
  149.2 1.9 %collective-permute-start.2 = (bf16[16,256,128]{2,1,0:T(8,128)(2,1)S(1)}, bf16[16,256,128]{2,1,0:T(8,128)(2,1)S(1)}, u32[]{:S(2)}, u32[]{:S(2)}) collective-permute-start(bf16[16,256,128]{2,1,0:T(8,128)(2,1)S(1)} %all_to_all.37.half), channel_id=1, source_target_pairs={{0,4},{4,0},{8,12},{12,8},{16,20},{20,16},{24,28},{28,24},{32,36},... | collective-permute-start | bytes 3145736 | tf_op jit(solution)/shard_map/ppermute | solution.py:242
  151.1 1.9 %widen_own.1 = (f32[4096,128]{1,0:T(8,128)}, f32[4096,128]{1,0:T(8,128)}) custom-call(s32[1]{0:T(128)} %bitcast.7.core, bf16[16,256,128]{2,1,0:T(8,128)(2,1)S(1)} %all_to_all.37.half), custom_call_target="tpu_custom_call" | custom-call | tf_op jit(solution)/shard_map/widen_own/pallas_call | solution.py:197
  153.0 0.8 collective-permute-done.2.half
  153.7 1.8 %widen_other.1 = (f32[4096,128]{1,0:T(8,128)}, f32[4096,128]{1,0:T(8,128)}) custom-call(s32[1]{0:T(128)} %bitcast.7.core, bf16[16,256,128]{2,1,0:T(8,128)(2,1)S(1)} %collective-permute-done.2.half, f32[4096,128]{1,0:T(8,128)} %get-tuple-element.36.refs_0_, f32[4096,128]{1,0:T(8,128)} %get-tuple-element.37.refs_1_), custom_call_target="tpu_custom_call", output_to_operand_aliasing={{0}: (2, {}), {1}: (3, {})} | custom-call | tf_op jit(solution)/shard_map/widen_other/pallas_call | solution.py:197
  (29 shorter events, 1.1 us)
Async XLA Ops:
  0.6 42.7 %copy-start.11 = (s32[1,4]{1,0:T(1,128)S(1)}, s32[1,4]{1,0:T(1,128)}, u32[]{:S(2)}) copy-start(s32[1,4]{1,0:T(1,128)} %param.16) | copy-start | bytes 52
  0.6 0.9 copy-start
  1.6 0.9 copy-start.10
  2.5 0.7 copy-start.12
  3.1 40.2 %copy-start.5 = (bf16[512,8,128]{2,1,0:T(8,128)(2,1)S(1)}, bf16[512,8,128]{2,1,0:T(8,128)(2,1)}, u32[]{:S(2)}) copy-start(bf16[512,8,128]{2,1,0:T(8,128)(2,1)} %param.17) | copy-start | bytes 3145732
  4.4 32.7 %all-to-all-start = ((bf16[128,8,128]{2,1,0:T(8,128)(2,1)}), bf16[128,8,128]{2,1,0:T(8,128)(2,1)S(1)}, u32[]{:S(2)}, u32[]{:S(2)}) async-start(bf16[128,8,128]{2,1,0:T(8,128)(2,1)} %pick.1), calls=%async_computation | async-start | bytes 524288 | tf_op jit(solution)/shard_map/all_to_all | solution.py:265
  22.9 0.9 copy-start.1
  23.8 0.9 copy-start.3
  24.7 0.9 copy-start.8
  25.6 24.9 %copy-start.2 = (bf16[512,128]{1,0:T(8,128)(2,1)S(1)}, bf16[512,128]{1,0:T(8,128)(2,1)}, u32[]{:S(2)}) copy-start(bf16[512,128]{1,0:T(8,128)(2,1)} %feats.5) | copy-start | bytes 393220
  25.6 24.9 %copy-start.4 = (bf16[512,128]{1,0:T(8,128)(2,1)S(1)}, bf16[512,128]{1,0:T(8,128)(2,1)}, u32[]{:S(2)}) copy-start(bf16[512,128]{1,0:T(8,128)(2,1)} %local.5) | copy-start | bytes 393220
  37.1 0.7 copy-start.13
  39.3 11.2 %all-to-all-start.1 = ((bf16[4,512,128]{2,1,0:T(8,128)(2,1)}), bf16[4,512,128]{2,1,0:T(8,128)(2,1)S(1)}, u32[]{:S(2)}, u32[]{:S(2)}) async-start(bf16[4,512,128]{2,1,0:T(8,128)(2,1)} %get-tuple-element.24), calls=%async_computation.1 | async-start | bytes 1048576 | tf_op jit(solution)/shard_map/all_to_all | solution.py:238
  44.3 11.5 %copy-start.6 = (bf16[512,8,128]{2,1,0:T(8,128)(2,1)S(1)}, bf16[512,8,128]{2,1,0:T(8,128)(2,1)}, u32[]{:S(2)}) copy-start(bf16[512,8,128]{2,1,0:T(8,128)(2,1)} %param.18) | copy-start | bytes 3145732
  50.5 12.2 %copy-start.7 = (bf16[512,128]{1,0:T(8,128)(2,1)S(1)}, bf16[512,128]{1,0:T(8,128)(2,1)}, u32[]{:S(2)}) copy-start(bf16[512,128]{1,0:T(8,128)(2,1)} %grad.3) | copy-start | bytes 393220
  52.2 10.5 %copy-start.9 = (bf16[512,128]{1,0:T(8,128)(2,1)S(1)}, bf16[512,128]{1,0:T(8,128)(2,1)}, u32[]{:S(2)}) copy-start(bf16[512,128]{1,0:T(8,128)(2,1)} %get-tuple-element.19.h_one) | copy-start | bytes 393220
  52.2 10.5 %all-to-all-start.2 = ((bf16[4,512,128]{2,1,0:T(8,128)(2,1)}), bf16[4,512,128]{2,1,0:T(8,128)(2,1)S(1)}, u32[]{:S(2)}, u32[]{:S(2)}) async-start(bf16[4,512,128]{2,1,0:T(8,128)(2,1)} %get-tuple-element.26), calls=%async_computation.2 | async-start | bytes 1048576 | tf_op jit(solution)/shard_map/all_to_all | solution.py:238
  64.3 11.6 %all-to-all-start.3 = ((bf16[4,512,128]{2,1,0:T(8,128)(2,1)}), bf16[4,512,128]{2,1,0:T(8,128)(2,1)S(1)}, u32[]{:S(2)}, u32[]{:S(2)}) async-start(bf16[4,512,128]{2,1,0:T(8,128)(2,1)} %get-tuple-element.29), calls=%async_computation.3 | async-start | bytes 1048576 | tf_op jit(solution)/shard_map/all_to_all | solution.py:238
  69.6 14.1 %collective-permute-start.1 = (bf16[256,1024]{1,0:T(8,128)(2,1)}, bf16[256,1024]{1,0:T(8,128)(2,1)S(1)}, u32[]{:S(2)}, u32[]{:S(2)}) collective-permute-start(bf16[256,1024]{1,0:T(8,128)(2,1)} %get-tuple-element.35), channel_id=1, source_target_pairs={{0,4},{4,0},{8,12},{12,8},{16,20},{20,16},{24,28},{28,24},{32,36},... | collective-permute-start | bytes 1572872 | tf_op jit(solution)/shard_map/ppermute | solution.py:242
  77.5 7.7 %collective-permute-start = (bf16[256,1024]{1,0:T(8,128)(2,1)S(1)}, bf16[256,1024]{1,0:T(8,128)(2,1)S(1)}, u32[]{:S(2)}, u32[]{:S(2)}) collective-permute-start(bf16[256,1024]{1,0:T(8,128)(2,1)S(1)} %get-tuple-element.32), channel_id=1, source_target_pairs={{0,4},{4,0},{8,12},{12,8},{16,20},{20,16},{24,28},{28,24},{32,36},... | collective-permute-start | bytes 1572872 | tf_op jit(solution)/shard_map/ppermute | solution.py:242
  149.2 4.5 %collective-permute-start.2 = (bf16[16,256,128]{2,1,0:T(8,128)(2,1)S(1)}, bf16[16,256,128]{2,1,0:T(8,128)(2,1)S(1)}, u32[]{:S(2)}, u32[]{:S(2)}) collective-permute-start(bf16[16,256,128]{2,1,0:T(8,128)(2,1)S(1)} %all_to_all.37.half), channel_id=1, source_target_pairs={{0,4},{4,0},{8,12},{12,8},{16,20},{20,16},{24,28},{28,24},{32,36},... | collective-permute-start | bytes 3145736 | tf_op jit(solution)/shard_map/ppermute | solution.py:242

commit v5 on v4

--- a/solution.py
+++ b/solution.py
@@ -10,7 +10,9 @@
 SMEM = pl.BlockSpec(memory_space=pltpu.SMEM)
 VMEM = pl.BlockSpec(memory_space=pltpu.VMEM)
 ANY = pl.BlockSpec(memory_space=pl.ANY)
+FAR = pl.BlockSpec(memory_space=pltpu.HBM)
 PARAMS = pltpu.CompilerParams(vmem_limit_bytes=40 << 20)
+FULL = pltpu.CompilerParams(vmem_limit_bytes=60 << 20)
 PAIR = 2
 RING = 16
 CROSS = 4
@@ -18,14 +20,14 @@
 TILE = 128
 
 
-def call(body, name, ins, outs, scratch=()):
+def call(body, name, ins, outs, scratch=(), params=PARAMS):
     return pl.pallas_call(
         body,
         out_shape=tuple(jax.ShapeDtypeStruct(shape, kind) for shape, kind in outs),
         in_specs=list(ins),
         out_specs=tuple(VMEM for _ in outs),
         scratch_shapes=list(scratch),
-        compiler_params=PARAMS,
+        compiler_params=params,
         name=name,
     )
 
@@ -42,21 +44,33 @@
     return lax.broadcasted_iota(jnp.int32, shape, axis)
 
 
-def pick_body(send, feats, hist, out, rows):
+def fetch(sources, targets, sems):
+    copies = [
+        pltpu.make_async_copy(source, target, sems.at[i])
+        for i, (source, target) in enumerate(zip(sources, targets))
+    ]
+    for copy in copies:
+        copy.start()
+    return copies
+
+
+def pick_body(send_far, feats_far, hist_far, out, rows, send, table, sems):
     cap, parts = send.shape
-    nodes, cols = feats.shape
-    table = jnp.concatenate([feats[...], hist[...]], axis=1)
+    nodes, cols = feats_far.shape
+    targets = (send, table.at[:, :cols], table.at[:, cols:])
+    for copy in fetch((send_far, feats_far, hist_far), targets, sems):
+        copy.wait()
     for c in range(cap):
         hit = (iota((nodes, parts), 0) == send[c : c + 1, :]).astype(F32).astype(BF)
-        got = dot(hit, table, ((0,), (0,)))
+        got = dot(hit, table[...], ((0,), (0,)))
         rows[:, c, :] = got[:, :cols]
         rows[:, cap + c, :] = got[:, cols:]
     out[...] = rows[...].astype(BF)
 
 
-def select_body(types, weights, out):
+def select_rows(types, weights, out):
     rows, width, _ = out.shape
-    experts = weights.shape[0] // width
+    experts = weights.shape[1]
     span = TILE // rows
     shape = (rows * span, span * experts)
     at, source = iota(shape, 0), iota(shape, 1)
@@ -65,27 +79,37 @@
         kind = jnp.where(at // span == j, types[j], kind)
     hit = (source == (at % span) * experts + kind).astype(F32).astype(BF)
     for i in range(width // span):
-        got = dot(hit, weights[i * span * experts : (i + 1) * span * experts, :]).astype(BF)
+        part = weights[i * span : (i + 1) * span].reshape(span * experts, -1)
+        got = dot(hit, part).astype(BF)
         for j in range(rows):
             out[j, i * span : (i + 1) * span, :] = got[j * span : (j + 1) * span]
 
 
-def ready_body(local, halo_val, feats, base, wide):
+def ready_body(pick, types, *refs):
+    far, (base, wide, one, two), near, sems = refs[:5], refs[5:9], refs[9:14], refs[14]
+    copies = fetch(far, near, sems)
+    local, halo_val, feats, w_one, w_two = near
     cap = wide.shape[2] // 2 // 32
     shape = (TILE, 2 * TILE)
     k, m = iota(shape, 0), iota(shape, 1)
     spot = (k // cap) * (2 * cap) + k % cap
     first = (m == spot).astype(F32).astype(BF)
     second = (m == spot + cap).astype(F32).astype(BF)
+    for copy in copies[:3]:
+        copy.wait()
     for j in range(wide.shape[0]):
         base[block(j), :] = dot(local[block(j), :], feats[block(j), :])
-        wide[j, :TILE, :] = dot(halo_val[block(j), :], first).astype(BF)
-        wide[j, TILE:, :] = dot(halo_val[block(j), :], second).astype(BF)
+        wide[pick[j], :TILE, :] = dot(halo_val[block(j), :], first).astype(BF)
+        wide[pick[j], TILE:, :] = dot(halo_val[block(j), :], second).astype(BF)
+    copies[3].wait()
+    select_rows(types, w_one, one)
+    copies[4].wait()
+    select_rows(types, w_two, two)
 
 
 def gather_body(pick, landed, wide, base, copies, part):
     for j in range(wide.shape[0]):
-        both = dot(wide[j], landed[pick[j]])
+        both = dot(wide[pick[j]], landed[pick[j]])
         agg = (base[block(j), :] + both[:TILE]).astype(BF)
         part[block(j), :] = both[TILE:]
         for q in range(copies.shape[0]):
@@ -187,7 +211,7 @@
 
 def widen(core, half, before=()):
     chunks, length, cols = half.shape
-    steps = 4
+    steps = 8
     own = not before
     height = chunks // steps * (length // 2)
     target = pl.BlockSpec(
@@ -258,19 +282,30 @@
     (rows_out,) = call(
         pick_body,
         "pick",
-        [VMEM] * 3,
+        [FAR] * 3,
         [((parts, 2 * cap, cols), BF)],
-        [pltpu.VMEM((parts, 2 * cap, cols), F32)],
+        [
+            pltpu.VMEM((parts, 2 * cap, cols), F32),
+            pltpu.VMEM((cap, parts), jnp.int32),
+            pltpu.VMEM((nodes, 2 * cols), BF),
+            pltpu.SemaphoreType.DMA((3,)),
+        ],
+        FULL,
     )(jnp.swapaxes(halo_send[0], 0, 1), feats, hist_one)
     landed = lax.all_to_all(rows_out, "dom", split_axis=0, concat_axis=0, tiled=True)
     landed = landed.reshape(rows, 2 * TILE, cols)
 
-    select = call(select_body, "select", [SMEM, VMEM], [((rows, width, cols), BF)])
-    (pick_one,) = select(types, w_one.reshape(width * experts, cols))
-    (pick_two,) = select(types, w_two.reshape(width * experts, cols))
-    base, wide = call(
-        ready_body, "ready", [VMEM] * 3, [(flat, F32), ((rows, 2 * TILE, 2 * TILE), BF)]
-    )(local_val, halo_val, feats)
+    chosen = (rows, width, cols)
+    base, wide, pick_one, pick_two = call(
+        ready_body,
+        "ready",
+        [SMEM] * 2 + [FAR] * 5,
+        [(flat, F32), ((rows, 2 * TILE, 2 * TILE), BF), (chosen, BF), (chosen, BF)],
+        [pltpu.VMEM(flat, BF)] * 3
+        + [pltpu.VMEM(w_one.shape, BF)] * 2
+        + [pltpu.SemaphoreType.DMA((5,))],
+        FULL,
+    )(pick, types, local_val, halo_val, feats, w_one, w_two)
 
     copies, part = call(gather_body, "gather", [SMEM] + [VMEM] * 3, [(copied, BF), (flat, F32)])(
         pick, landed, wide, base

time: 156 us -> 156 us (level)
  blocking collectives: 63.4 us -> 83.3 us
  waiting for transfers between devices: 25.4 us -> 10.5 us
  starting transfers between devices: 44 us -> 36.3 us
  Pallas kernels: 15.7 us -> 19.7 us
  local copies, waits for them, and re-layouts: 5.88 us -> 2.94 us
    all_to_all x0 -> x2, blocking collectives: none -> 20.5 us  [across(): lax.all_to_all(blocks, 'rep', split_axis=0, concat_axis=0, tiled=True)]
    all_to_all x3 -> x1, waiting for transfers between devices: 12.1 us -> 0.01 us  [across(): lax.all_to_all(blocks, 'rep', split_axis=0, concat_axis=0, tiled=True)]
    all_to_all x3 -> x1, starting transfers between devices: 11.1 us -> 3.47 us  [across(): lax.all_to_all(blocks, 'rep', split_axis=0, concat_axis=0, tiled=True)]
    unnamed x28 -> x20, local copies, waits for them, and re-layouts: 5.88 us -> 2.94 us
    pallas_call x4 -> x2, Pallas kernels: 3.53 us -> 6.25 us  [the longest x1 3.95 us: shards(): call(ready_body, 'ready', [SMEM] * 2 + [FAR] * 5, [(flat, F32), ((rows, 2...]
    pallas_call x2, Pallas kernels: 3.67 us -> 5.92 us  [widen(): pl.pallas_call(widen_body, grid_spec=pltpu.PrefetchScalarGridSpec(num_sca...]
    ppermute x3, waiting for transfers between devices: 2.13 us -> 0.3 us  [swap(): return lax.ppermute(rows, 'dom', [(p, p ^ 1) for p in range(128)])]
  transfers between devices with their start and end apart: 7 -> 5, of which waited for: 5 -> 2; matrix products, arithmetic and copies ran while one was open for 0% -> 1% of each run, Pallas kernels for 5% -> 7%
where the time goes in v5:
time: 156 us; the launch traced here: 155 us
  blocking collectives  83.3 us (53%)
  starting transfers between devices  36.3 us (23%)
  Pallas kernels  19.7 us (13%)
  waiting for transfers between devices  10.5 us (7%)
  local copies, waits for them, and re-layouts  2.94 us (2%)
    all_to_all x3, blocking collectives, exchange(): lax.all_to_all(blocks, 'dom', split_axis=0, concat_axis=0, axis_index_gro...  62.8 us
    all_to_all x2, blocking collectives, across(): lax.all_to_all(blocks, 'rep', split_axis=0, concat_axis=0, tiled=True)  20.5 us
    all_to_all x1, starting transfers between devices, shards(): lax.all_to_all(rows_out, 'dom', split_axis=0, concat_axis=0, tiled=True)  18.4 us
    ppermute x3, starting transfers between devices, swap(): return lax.ppermute(rows, 'dom', [(p, p ^ 1) for p in range(128)])  14.4 us
    all_to_all x1, waiting for transfers between devices, shards(): lax.all_to_all(rows_out, 'dom', split_axis=0, concat_axis=0, tiled=True)  10.2 us
    pallas_call x2, Pallas kernels, widen(): pl.pallas_call(widen_body, grid_spec=pltpu.PrefetchScalarGridSpec(num_sca...  5.92 us
    pallas_call x1, Pallas kernels, shards(): call(ready_body, 'ready', [SMEM] * 2 + [FAR] * 5, [(flat, F32), ((rows, 2...  3.95 us
    all_to_all x1, starting transfers between devices, across(): lax.all_to_all(blocks, 'rep', split_axis=0, concat_axis=0, tiled=True)  3.47 us
  transfers between devices with their start and end apart: 5, of which 2 were waited for; matrix products, arithmetic and copies ran while one was open for 1% of the time, Pallas kernels for 7%

profile of v5, /device:TPU:1, one launch (start us, length us, event | category | flops | bytes accessed | tf_op | source)
XLA Modules:
  0.0 155.1 jit_solution(4281131710939526462)
XLA Ops:
  0.6 0.0 copy-start.9
  0.6 2.3 %pick.1 = bf16[128,8,128]{2,1,0:T(8,128)(2,1)} custom-call(s32[4,128]{1,0:T(4,128)} %bitcast.21, bf16[512,128]{1,0:T(8,128)(2,1)} %feats.1, bf16[512,128]{1,0:T(8,128)(2,1)} %hist_far.1), custom_call_target="tpu_custom_call" | custom-call | tf_op jit(solution)/shard_map/pick/pallas_call | solution.py:282
  3.0 18.4 %all-to-all-start = ((bf16[128,8,128]{2,1,0:T(8,128)(2,1)}), bf16[128,8,128]{2,1,0:T(8,128)(2,1)S(1)}, u32[]{:S(2)}, u32[]{:S(2)}) async-start(bf16[128,8,128]{2,1,0:T(8,128)(2,1)} %pick.1), calls=%async_computation | async-start | bytes 524288 | tf_op jit(solution)/shard_map/all_to_all | solution.py:295
  21.4 0.0 copy-start
  21.4 0.0 copy-start.1
  21.4 3.9 %ready.1 = (f32[512,128]{1,0:T(8,128)}, bf16[4,256,256]{2,1,0:T(8,128)(2,1)}, bf16[4,512,128]{2,1,0:T(8,128)(2,1)}, bf16[4,512,128]{2,1,0:T(8,128)(2,1)}) custom-call(s32[4]{0:T(128)} %bitcast.15, s32[4]{0:T(128)} %bitcast.12, bf16[512,128]{1,0:T(8,128)(2,1)} %local.3, bf16[512,128]{1,0:T(8,128)(2,1)} %refs_1_.1, bf16[512,128]{1,0:T(8,128)(2,1)} %feats.1, ...), custom_call_target="tpu_custom_call" | custom-call | tf_op jit(solution)/shard_map/ready/pallas_call | solution.py:299
  25.4 10.2 %all-to-all-done = bf16[128,8,128]{2,1,0:T(8,128)(2,1)S(1)} async-done(((bf16[128,8,128]{2,1,0:T(8,128)(2,1)}), bf16[128,8,128]{2,1,0:T(8,128)(2,1)S(1)}, u32[]{:S(2)}, u32[]{:S(2)}) %all-to-all-start) | async-done | bytes 262176 | tf_op jit(solution)/shard_map/all_to_all | solution.py:295
  35.6 1.0 copy-done.4
  36.7 0.9 copy-done.6
  37.6 0.8 gather.1
  38.5 11.1 %all_to_all.35.agg = bf16[4,512,128]{2,1,0:T(8,128)(2,1)S(1)} all-to-all(bf16[4,512,128]{2,1,0:T(8,128)(2,1)S(1)} %get-tuple-element.26), channel_id=1, replica_groups=mesh['dom'=128,'rep'=4] {'rep'}, dimensions={0} | all-to-all | bytes 1048576 | tf_op jit(solution)/shard_map/all_to_all | solution.py:262
  49.6 1.4 one.1
  51.0 9.5 %all_to_all.36.agg = bf16[4,512,128]{2,1,0:T(8,128)(2,1)S(1)} all-to-all(bf16[4,512,128]{2,1,0:T(8,128)(2,1)S(1)} %get-tuple-element.29), channel_id=1, replica_groups=mesh['dom'=128,'rep'=4] {'rep'}, dimensions={0} | all-to-all | bytes 1048576 | tf_op jit(solution)/shard_map/all_to_all | solution.py:262
  60.4 0.9 copy-done.7
  61.3 1.7 %two.1 = (bf16[512,128]{1,0:T(8,128)(2,1)}, bf16[512,128]{1,0:T(8,128)(2,1)S(1)}, bf16[4,512,128]{2,1,0:T(8,128)(2,1)}) custom-call(bf16[4,512,128]{2,1,0:T(8,128)(2,1)S(1)} %all_to_all.36.agg, bf16[4,512,128]{2,1,0:T(8,128)(2,1)S(1)} %copy-done.3, bf16[512,128]{1,0:T(8,128)(2,1)S(1)} %copy-done.7, bf16[512,128]{1,0:T(8,128)(2,1)S(1)} %copy-done.5), custom_call_target="tpu_custom_call" | custom-call | tf_op jit(solution)/shard_map/two/pallas_call | solution.py:318
  63.0 3.5 %all-to-all-start.3 = ((bf16[4,512,128]{2,1,0:T(8,128)(2,1)}), bf16[4,512,128]{2,1,0:T(8,128)(2,1)S(1)}, u32[]{:S(2)}, u32[]{:S(2)}) async-start(bf16[4,512,128]{2,1,0:T(8,128)(2,1)} %get-tuple-element.33), calls=%async_computation.3 | async-start | bytes 1048576 | tf_op jit(solution)/shard_map/all_to_all | solution.py:262
  66.5 1.8 %grad_two.1 = (f32[256,1024]{1,0:T(8,128)S(1)}, bf16[256,1024]{1,0:T(8,128)(2,1)}) custom-call(s32[4]{0:T(128)S(1)} %bitcast.13, s32[1]{0:T(128)} %bitcast.5.core, bf16[4,512,128]{2,1,0:T(8,128)(2,1)S(1)} %all_to_all.36.agg, bf16[512,128]{1,0:T(8,128)(2,1)S(1)} %get-tuple-element.37.dz), custom_call_target="tpu_custom_call" | custom-call | tf_op jit(solution)/shard_map/grad_two/pallas_call | solution.py:324
  68.3 6.3 %collective-permute-start.1 = (bf16[256,1024]{1,0:T(8,128)(2,1)}, bf16[256,1024]{1,0:T(8,128)(2,1)}, u32[]{:S(2)}, u32[]{:S(2)}) collective-permute-start(bf16[256,1024]{1,0:T(8,128)(2,1)} %get-tuple-element.39), channel_id=1, source_target_pairs={{0,4},{4,0},{8,12},{12,8},{16,20},{20,16},{24,28},{28,24},{32,36},... | collective-permute-start | bytes 1572872 | tf_op jit(solution)/shard_map/ppermute | solution.py:266
  74.7 1.5 back.1
  76.1 6.2 %collective-permute-start = (bf16[256,1024]{1,0:T(8,128)(2,1)S(1)}, bf16[256,1024]{1,0:T(8,128)(2,1)S(1)}, u32[]{:S(2)}, u32[]{:S(2)}) collective-permute-start(bf16[256,1024]{1,0:T(8,128)(2,1)S(1)} %get-tuple-element.36), channel_id=1, source_target_pairs={{0,4},{4,0},{8,12},{12,8},{16,20},{20,16},{24,28},{28,24},{32,36},... | collective-permute-start | bytes 1572872 | tf_op jit(solution)/shard_map/ppermute | solution.py:266
  82.4 1.2 add_convert_fusion
  83.6 0.3 collective-permute-done
  83.9 0.1 add_convert_fusion.1
  84.0 0.1 pad_maximum_fusion
  84.1 25.3 %all_to_all.37.parts = bf16[16,32,1024]{2,1,0:T(8,128)(2,1)S(1)} all-to-all(bf16[16,32,1024]{2,1,0:T(8,128)(2,1)S(1)} %pad_maximum_fusion), channel_id=1, replica_groups={{0,64,128,192,256,320,384,448,8,72,136,200,264,328,392,456},{16,80,144,..., dimensions={0} | all-to-all | bytes 2097152 | tf_op jit(solution)/shard_map/all_to_all | solution.py:256
  109.5 0.1 first_sum.1
  109.6 11.8 %all_to_all.38.parts = bf16[4,32,1024]{2,1,0:T(8,128)(2,1)S(1)} all-to-all(bf16[4,32,1024]{2,1,0:T(8,128)(2,1)S(1)} %first_sum.1), channel_id=1, replica_groups={{0,16,32,48},{8,24,40,56},{64,80,96,112},{72,88,104,120},{128,144,160,1..., dimensions={0} | all-to-all | bytes 524288 | tf_op jit(solution)/shard_map/all_to_all | solution.py:256
  121.4 0.2 second_sum.1
  121.6 25.7 %all_to_all.39.half = bf16[16,256,128]{2,1,0:T(8,128)(2,1)S(1)} all-to-all(bf16[16,256,128]{2,1,0:T(8,128)(2,1)S(1)} %second_sum.1), channel_id=1, replica_groups={{0,64,128,192,256,320,384,448,8,72,136,200,264,328,392,456},{16,80,144,..., dimensions={0} | all-to-all | bytes 2097152 | tf_op jit(solution)/shard_map/all_to_all | solution.py:256
  147.2 1.9 %collective-permute-start.2 = (bf16[16,256,128]{2,1,0:T(8,128)(2,1)S(1)}, bf16[16,256,128]{2,1,0:T(8,128)(2,1)S(1)}, u32[]{:S(2)}, u32[]{:S(2)}) collective-permute-start(bf16[16,256,128]{2,1,0:T(8,128)(2,1)S(1)} %all_to_all.39.half), channel_id=1, source_target_pairs={{0,4},{4,0},{8,12},{12,8},{16,20},{20,16},{24,28},{28,24},{32,36},... | collective-permute-start | bytes 3145736 | tf_op jit(solution)/shard_map/ppermute | solution.py:266
  149.2 3.0 %widen_own.1 = (f32[4096,128]{1,0:T(8,128)}, f32[4096,128]{1,0:T(8,128)}) custom-call(s32[1]{0:T(128)} %bitcast.5.core, bf16[16,256,128]{2,1,0:T(8,128)(2,1)S(1)} %all_to_all.39.half), custom_call_target="tpu_custom_call" | custom-call | tf_op jit(solution)/shard_map/widen_own/pallas_call | solution.py:221
  152.1 2.9 %widen_other.1 = (f32[4096,128]{1,0:T(8,128)}, f32[4096,128]{1,0:T(8,128)}) custom-call(s32[1]{0:T(128)} %bitcast.5.core, bf16[16,256,128]{2,1,0:T(8,128)(2,1)S(1)} %collective-permute-done.2.half, f32[4096,128]{1,0:T(8,128)} %get-tuple-element.40.refs_0_, f32[4096,128]{1,0:T(8,128)} %get-tuple-element.41.refs_1_), custom_call_target="tpu_custom_call", output_to_operand_aliasing={{0}: (2, {}), {1}: (3, {})} | custom-call | tf_op jit(solution)/shard_map/widen_other/pallas_call | solution.py:221
  (17 shorter events, 0.0 us)
Async XLA Ops:
  0.6 35.0 %copy-start.9 = (s32[1,4]{1,0:T(1,128)S(1)}, s32[1,4]{1,0:T(1,128)}, u32[]{:S(2)}) copy-start(s32[1,4]{1,0:T(1,128)} %param.15) | copy-start | bytes 52
  3.0 32.7 %all-to-all-start = ((bf16[128,8,128]{2,1,0:T(8,128)(2,1)}), bf16[128,8,128]{2,1,0:T(8,128)(2,1)S(1)}, u32[]{:S(2)}, u32[]{:S(2)}) async-start(bf16[128,8,128]{2,1,0:T(8,128)(2,1)} %pick.1), calls=%async_computation | async-start | bytes 524288 | tf_op jit(solution)/shard_map/all_to_all | solution.py:295
  21.4 28.2 %copy-start = (bf16[512,128]{1,0:T(8,128)(2,1)S(1)}, bf16[512,128]{1,0:T(8,128)(2,1)}, u32[]{:S(2)}) copy-start(bf16[512,128]{1,0:T(8,128)(2,1)} %feats.1) | copy-start | bytes 393220
  21.4 28.2 %copy-start.1 = (bf16[512,128]{1,0:T(8,128)(2,1)S(1)}, bf16[512,128]{1,0:T(8,128)(2,1)}, u32[]{:S(2)}) copy-start(bf16[512,128]{1,0:T(8,128)(2,1)} %local.3) | copy-start | bytes 393220
  25.4 24.2 %copy-start.2 = (bf16[4,512,128]{2,1,0:T(8,128)(2,1)S(1)}, bf16[4,512,128]{2,1,0:T(8,128)(2,1)}, u32[]{:S(2)}) copy-start(bf16[4,512,128]{2,1,0:T(8,128)(2,1)} %get-tuple-element.27.weights) | copy-start | bytes 1572868
  35.6 1.0 copy-start.4
  36.7 0.9 copy-start.6
  38.4 22.0 %copy-start.3 = (bf16[4,512,128]{2,1,0:T(8,128)(2,1)S(1)}, bf16[4,512,128]{2,1,0:T(8,128)(2,1)}, u32[]{:S(2)}) copy-start(bf16[4,512,128]{2,1,0:T(8,128)(2,1)} %get-tuple-element.30.weights) | copy-start | bytes 1572868
  38.5 22.0 %copy-start.5 = (bf16[512,128]{1,0:T(8,128)(2,1)S(1)}, bf16[512,128]{1,0:T(8,128)(2,1)}, u32[]{:S(2)}) copy-start(bf16[512,128]{1,0:T(8,128)(2,1)} %grad.3) | copy-start | bytes 393220
  51.0 15.5 %copy-start.8 = (s32[1,4]{1,0:T(1,128)S(1)}, s32[1,4]{1,0:T(1,128)}, u32[]{:S(2)}) copy-start(s32[1,4]{1,0:T(1,128)} %param.16) | copy-start | bytes 52
  60.4 0.9 copy-start.7
  63.0 11.7 %all-to-all-start.3 = ((bf16[4,512,128]{2,1,0:T(8,128)(2,1)}), bf16[4,512,128]{2,1,0:T(8,128)(2,1)S(1)}, u32[]{:S(2)}, u32[]{:S(2)}) async-start(bf16[4,512,128]{2,1,0:T(8,128)(2,1)} %get-tuple-element.33), calls=%async_computation.3 | async-start | bytes 1048576 | tf_op jit(solution)/shard_map/all_to_all | solution.py:262
  68.3 14.0 %collective-permute-start.1 = (bf16[256,1024]{1,0:T(8,128)(2,1)}, bf16[256,1024]{1,0:T(8,128)(2,1)}, u32[]{:S(2)}, u32[]{:S(2)}) collective-permute-start(bf16[256,1024]{1,0:T(8,128)(2,1)} %get-tuple-element.39), channel_id=1, source_target_pairs={{0,4},{4,0},{8,12},{12,8},{16,20},{20,16},{24,28},{28,24},{32,36},... | collective-permute-start | bytes 1572872 | tf_op jit(solution)/shard_map/ppermute | solution.py:266
  76.1 7.7 %collective-permute-start = (bf16[256,1024]{1,0:T(8,128)(2,1)S(1)}, bf16[256,1024]{1,0:T(8,128)(2,1)S(1)}, u32[]{:S(2)}, u32[]{:S(2)}) collective-permute-start(bf16[256,1024]{1,0:T(8,128)(2,1)S(1)} %get-tuple-element.36), channel_id=1, source_target_pairs={{0,4},{4,0},{8,12},{12,8},{16,20},{20,16},{24,28},{28,24},{32,36},... | collective-permute-start | bytes 1572872 | tf_op jit(solution)/shard_map/ppermute | solution.py:266
  147.2 4.9 %collective-permute-start.2 = (bf16[16,256,128]{2,1,0:T(8,128)(2,1)S(1)}, bf16[16,256,128]{2,1,0:T(8,128)(2,1)S(1)}, u32[]{:S(2)}, u32[]{:S(2)}) collective-permute-start(bf16[16,256,128]{2,1,0:T(8,128)(2,1)S(1)} %all_to_all.39.half), channel_id=1, source_target_pairs={{0,4},{4,0},{8,12},{12,8},{16,20},{20,16},{24,28},{28,24},{32,36},... | collective-permute-start | bytes 3145736 | tf_op jit(solution)/shard_map/ppermute | solution.py:266

commit v6 on v5

--- a/solution.py
+++ b/solution.py
@@ -85,26 +85,25 @@
             out[j, i * span : (i + 1) * span, :] = got[j * span : (j + 1) * span]
 
 
-def ready_body(pick, types, *refs):
-    far, (base, wide, one, two), near, sems = refs[:5], refs[5:9], refs[9:14], refs[14]
-    copies = fetch(far, near, sems)
-    local, halo_val, feats, w_one, w_two = near
+def choose_body(types, w_one_far, w_two_far, one, two, w_one, w_two, sems):
+    copies = fetch((w_one_far, w_two_far), (w_one, w_two), sems)
+    copies[0].wait()
+    select_rows(types, w_one, one)
+    copies[1].wait()
+    select_rows(types, w_two, two)
+
+
+def ready_body(pick, local, halo_val, feats, base, wide):
     cap = wide.shape[2] // 2 // 32
     shape = (TILE, 2 * TILE)
     k, m = iota(shape, 0), iota(shape, 1)
     spot = (k // cap) * (2 * cap) + k % cap
     first = (m == spot).astype(F32).astype(BF)
     second = (m == spot + cap).astype(F32).astype(BF)
-    for copy in copies[:3]:
-        copy.wait()
     for j in range(wide.shape[0]):
         base[block(j), :] = dot(local[block(j), :], feats[block(j), :])
         wide[pick[j], :TILE, :] = dot(halo_val[block(j), :], first).astype(BF)
         wide[pick[j], TILE:, :] = dot(halo_val[block(j), :], second).astype(BF)
-    copies[3].wait()
-    select_rows(types, w_one, one)
-    copies[4].wait()
-    select_rows(types, w_two, two)
 
 
 def gather_body(pick, landed, wide, base, copies, part):
@@ -123,12 +122,13 @@
     return z * sig, sig * (1.0 + z * (1.0 - sig))
 
 
-def one_body(agg, weights, feats, local, part, hidden, slope, copies):
+def one_body(agg, weights, feats, local, part, hidden, near, slope, copies):
     for j in range(weights.shape[0]):
         act, bend = forward(agg, weights, j)
         slope[block(j), :] = bend
         h = (feats[block(j), :].astype(F32) + act).astype(BF)
         hidden[block(j), :] = h
+        near[block(j), :] = h
         mixed = (dot(local[block(j), :], h) + part[block(j), :]).astype(BF)
         for q in range(copies.shape[0]):
             copies[q, block(j), :] = mixed
@@ -182,15 +182,14 @@
     return total
 
 
-def first_body(parts, copies):
-    total = add_up(parts).astype(BF)
-    for i in range(copies.shape[0]):
-        copies[i] = total
-
-
-def second_body(parts, copies, table):
+def first_body(parts, total):
+    total[...] = add_up(parts).astype(BF)
+
+
+def second_body(own, left, right, opposite, copies, table):
     rows, experts, cols = table.shape
-    total = add_up(parts)
+    total = own[...].astype(F32) + opposite[...].astype(F32)
+    total = total + (left[...].astype(F32) + right[...].astype(F32))
     for e in range(experts):
         table[:, e, :] = total[:, e * cols : (e + 1) * cols]
     laid = table[...].reshape(rows * experts, cols).astype(BF)
@@ -211,7 +210,7 @@
 
 def widen(core, half, before=()):
     chunks, length, cols = half.shape
-    steps = 8
+    steps = 2
     own = not before
     height = chunks // steps * (length // 2)
     target = pl.BlockSpec(
@@ -296,28 +295,33 @@
     landed = landed.reshape(rows, 2 * TILE, cols)
 
     chosen = (rows, width, cols)
-    base, wide, pick_one, pick_two = call(
+    pick_one, pick_two = call(
+        choose_body,
+        "choose",
+        [SMEM] + [FAR] * 2,
+        [(chosen, BF)] * 2,
+        [pltpu.VMEM(w_one.shape, BF)] * 2 + [pltpu.SemaphoreType.DMA((2,))],
+        FULL,
+    )(types, w_one, w_two)
+    base, wide = call(
         ready_body,
         "ready",
-        [SMEM] * 2 + [FAR] * 5,
-        [(flat, F32), ((rows, 2 * TILE, 2 * TILE), BF), (chosen, BF), (chosen, BF)],
-        [pltpu.VMEM(flat, BF)] * 3
-        + [pltpu.VMEM(w_one.shape, BF)] * 2
-        + [pltpu.SemaphoreType.DMA((5,))],
-        FULL,
-    )(pick, types, local_val, halo_val, feats, w_one, w_two)
-
+        [SMEM] + [VMEM] * 3,
+        [(flat, F32), ((rows, 2 * TILE, 2 * TILE), BF)],
+    )(pick, local_val, halo_val, feats)
+
+    base, wide, pick_one, pick_two = lax.optimization_barrier((base, wide, pick_one, pick_two))
     copies, part = call(gather_body, "gather", [SMEM] + [VMEM] * 3, [(copied, BF), (flat, F32)])(
         pick, landed, wide, base
     )
     agg_one = across(copies)
-    h_one, slope, copies = call(
-        one_body, "one", [VMEM] * 5, [(flat, BF), (flat, F32), (copied, BF)]
+    h_one, near, slope, copies = call(
+        one_body, "one", [VMEM] * 5, [(flat, BF)] * 2 + [(flat, F32), (copied, BF)]
     )(agg_one, pick_one, feats, local_val, part)
     agg_two = across(copies)
     h_two, dz_two, back = call(
         two_body, "two", [VMEM] * 4, [(flat, BF), (flat, BF), (copied, BF)]
-    )(agg_two, pick_two, h_one, grad_out)
+    )(agg_two, pick_two, near, grad_out)
     back = across(back)
 
     half = (width // 2, experts * cols)
@@ -338,15 +342,21 @@
     both = jnp.concatenate([pair_one.reshape(split), pair_two.reshape(split)], axis=1)
     both = exchange(both, first)
     few = both.shape[1]
-    (both,) = call(first_body, "first_sum", [VMEM], [((CROSS,) + both.shape[1:], BF)])(both)
-    both = exchange(both, second)
+    (own,) = call(first_body, "first_sum", [VMEM], [(both.shape[1:], BF)])(both)
+    shifted = [
+        lax.ppermute(
+            own, "dom", [(g[i], g[(i + k) % CROSS]) for g in second for i in range(CROSS)]
+        )
+        for k in (2, 1, 3)
+    ]
+    opposite, left, right = shifted
     (both,) = call(
         second_body,
         "second_sum",
-        [VMEM],
+        [VMEM] * 4,
         [((RING, few * experts, cols), BF)],
         [pltpu.VMEM((few, experts, cols), F32)],
-    )(both)
+    )(own, left, right, opposite)
     same = exchange(both, first)
     grad_one, grad_two = widen(core, swap(same), widen(core, same))
     return h_two, h_one, grad_one.reshape(w_one.shape), grad_two.reshape(w_two.shape)

time: 156 us -> 155 us (level)
  blocking collectives: 83.3 us -> 73.1 us
  starting transfers between devices: 36.3 us -> 46.4 us
  Pallas kernels: 19.7 us -> 17.1 us
  waiting for transfers between devices: 10.5 us -> 12.1 us
    all_to_all x3 -> x2, blocking collectives: 62.8 us -> 52.6 us  [exchange(): lax.all_to_all(blocks, 'dom', split_axis=0, concat_axis=0, axis_index_gro...]
    ppermute x0 -> x3, starting transfers between devices: none -> 10.1 us  [shards(): lax.ppermute(own, 'dom', [(g[i], g[(i + k) % CROSS]) for g in second for...]
    ppermute x0 -> x3, waiting for transfers between devices: none -> 4.37 us  [shards(): lax.ppermute(own, 'dom', [(g[i], g[(i + k) % CROSS]) for g in second for...]
    all_to_all x1, waiting for transfers between devices: 10.2 us -> 6.26 us  [shards(): lax.all_to_all(rows_out, 'dom', split_axis=0, concat_axis=0, tiled=True)]
    pallas_call x2, Pallas kernels: 5.92 us -> 2.79 us  [widen(): pl.pallas_call(widen_body, grid_spec=pltpu.PrefetchScalarGridSpec(num_sca...]
    pallas_call x4 -> x5, Pallas kernels: 5.67 us -> 6.26 us  [the longest x1 3.68 us: shards(): call(choose_body, 'choose', [SMEM] + [FAR] * 2, [(chosen, BF)] * 2, [pltp...]
    unnamed x20 -> x22, local copies, waits for them, and re-layouts: 2.94 us -> 3.4 us
  transfers between devices with their start and end apart: 5 -> 8, of which waited for: 2 -> 5; matrix products, arithmetic and copies ran while one was open for 1% -> 1% of each run, Pallas kernels for 7% -> 6%
where the time goes in v6:
time: 155 us
  blocking collectives  73.1 us (47%)
  starting transfers between devices  46.4 us (30%)
  Pallas kernels  17.1 us (11%)
  waiting for transfers between devices  12.1 us (8%)
  local copies, waits for them, and re-layouts  3.4 us (2%)
    all_to_all x2, blocking collectives, exchange(): lax.all_to_all(blocks, 'dom', split_axis=0, concat_axis=0, axis_index_gro...  52.6 us
    all_to_all x2, blocking collectives, across(): lax.all_to_all(blocks, 'rep', split_axis=0, concat_axis=0, tiled=True)  20.5 us
    all_to_all x1, starting transfers between devices, shards(): lax.all_to_all(rows_out, 'dom', split_axis=0, concat_axis=0, tiled=True)  18.4 us
    ppermute x3, starting transfers between devices, swap(): return lax.ppermute(rows, 'dom', [(p, p ^ 1) for p in range(128)])  14.4 us
    ppermute x3, starting transfers between devices, shards(): lax.ppermute(own, 'dom', [(g[i], g[(i + k) % CROSS]) for g in second for...  10.1 us
    all_to_all x1, waiting for transfers between devices, shards(): lax.all_to_all(rows_out, 'dom', split_axis=0, concat_axis=0, tiled=True)  6.26 us
    ppermute x3, waiting for transfers between devices, shards(): lax.ppermute(own, 'dom', [(g[i], g[(i + k) % CROSS]) for g in second for...  4.37 us
    pallas_call x1, Pallas kernels, shards(): call(choose_body, 'choose', [SMEM] + [FAR] * 2, [(chosen, BF)] * 2, [pltp...  3.68 us
  transfers between devices with their start and end apart: 8, of which 5 were waited for; matrix products, arithmetic and copies ran while one was open for 1% of the time, Pallas kernels for 6%

profile of v6, /device:TPU:1, one launch (start us, length us, event | category | flops | bytes accessed | tf_op | source)
XLA Modules:
  0.0 154.6 jit_solution(2996607523729428388)
XLA Ops:
  0.6 2.3 %pick.1 = bf16[128,8,128]{2,1,0:T(8,128)(2,1)} custom-call(s32[4,128]{1,0:T(4,128)} %bitcast.21, bf16[512,128]{1,0:T(8,128)(2,1)} %feats.3, bf16[512,128]{1,0:T(8,128)(2,1)} %hist_far.1), custom_call_target="tpu_custom_call" | custom-call | tf_op jit(solution)/shard_map/pick/pallas_call | solution.py:281
  2.9 18.4 %all-to-all-start = ((bf16[128,8,128]{2,1,0:T(8,128)(2,1)}), bf16[128,8,128]{2,1,0:T(8,128)(2,1)S(1)}, u32[]{:S(2)}, u32[]{:S(2)}) async-start(bf16[128,8,128]{2,1,0:T(8,128)(2,1)} %pick.1), calls=%async_computation | async-start | bytes 524288 | tf_op jit(solution)/shard_map/all_to_all | solution.py:294
  21.4 0.9 copy-done
  22.3 0.9 copy-done.2
  23.2 0.9 copy-done.7
  24.1 0.7 copy-done.9
  24.8 0.9 ready.1
  25.7 3.7 %choose.1 = (bf16[4,512,128]{2,1,0:T(8,128)(2,1)}, bf16[4,512,128]{2,1,0:T(8,128)(2,1)}) custom-call(s32[4]{0:T(128)} %bitcast.12, bf16[512,8,128]{2,1,0:T(8,128)(2,1)} %w_one_far.1, bf16[512,8,128]{2,1,0:T(8,128)(2,1)} %w_two_far.1), custom_call_target="tpu_custom_call" | custom-call | tf_op jit(solution)/shard_map/choose/pallas_call | solution.py:298
  29.4 6.3 %all-to-all-done = bf16[128,8,128]{2,1,0:T(8,128)(2,1)S(1)} async-done(((bf16[128,8,128]{2,1,0:T(8,128)(2,1)}), bf16[128,8,128]{2,1,0:T(8,128)(2,1)S(1)}, u32[]{:S(2)}, u32[]{:S(2)}) %all-to-all-start) | async-done | bytes 262176 | tf_op jit(solution)/shard_map/all_to_all | solution.py:294
  35.6 0.8 gather.1
  36.5 11.1 %all_to_all.30.agg = bf16[4,512,128]{2,1,0:T(8,128)(2,1)S(1)} all-to-all(bf16[4,512,128]{2,1,0:T(8,128)(2,1)S(1)} %get-tuple-element.35), channel_id=1, replica_groups=mesh['dom'=128,'rep'=4] {'rep'}, dimensions={0} | all-to-all | bytes 1048576 | tf_op jit(solution)/shard_map/all_to_all | solution.py:261
  47.6 1.4 one.1
  49.0 9.5 %all_to_all.31.agg = bf16[4,512,128]{2,1,0:T(8,128)(2,1)S(1)} all-to-all(bf16[4,512,128]{2,1,0:T(8,128)(2,1)S(1)} %get-tuple-element.38), channel_id=1, replica_groups=mesh['dom'=128,'rep'=4] {'rep'}, dimensions={0} | all-to-all | bytes 1048576 | tf_op jit(solution)/shard_map/all_to_all | solution.py:261
  58.4 1.7 %two.1 = (bf16[512,128]{1,0:T(8,128)(2,1)}, bf16[512,128]{1,0:T(8,128)(2,1)S(1)}, bf16[4,512,128]{2,1,0:T(8,128)(2,1)}) custom-call(bf16[4,512,128]{2,1,0:T(8,128)(2,1)S(1)} %all_to_all.31.agg, bf16[4,512,128]{2,1,0:T(8,128)(2,1)S(1)} %copy-done.5, bf16[512,128]{1,0:T(8,128)(2,1)S(1)} %get-tuple-element.40.h_one, bf16[512,128]{1,0:T(8,128)(2,1)S(1)} %copy-done.6), custom_call_target="tpu_custom_call" | custom-call | tf_op jit(solution)/shard_map/two/pallas_call | solution.py:322
  60.1 3.5 %all-to-all-start.3 = ((bf16[4,512,128]{2,1,0:T(8,128)(2,1)}), bf16[4,512,128]{2,1,0:T(8,128)(2,1)S(1)}, u32[]{:S(2)}, u32[]{:S(2)}) async-start(bf16[4,512,128]{2,1,0:T(8,128)(2,1)} %get-tuple-element.43), calls=%async_computation.3 | async-start | bytes 1048576 | tf_op jit(solution)/shard_map/all_to_all | solution.py:261
  63.6 1.8 %grad_two.1 = (f32[256,1024]{1,0:T(8,128)S(1)}, bf16[256,1024]{1,0:T(8,128)(2,1)}) custom-call(s32[4]{0:T(128)S(1)} %bitcast.13, s32[1]{0:T(128)} %bitcast.5.core, bf16[4,512,128]{2,1,0:T(8,128)(2,1)S(1)} %all_to_all.31.agg, bf16[512,128]{1,0:T(8,128)(2,1)S(1)} %get-tuple-element.47.dz), custom_call_target="tpu_custom_call" | custom-call | tf_op jit(solution)/shard_map/grad_two/pallas_call | solution.py:328
  65.4 6.3 %collective-permute-start.1 = (bf16[256,1024]{1,0:T(8,128)(2,1)}, bf16[256,1024]{1,0:T(8,128)(2,1)}, u32[]{:S(2)}, u32[]{:S(2)}) collective-permute-start(bf16[256,1024]{1,0:T(8,128)(2,1)} %get-tuple-element.49), channel_id=1, source_target_pairs={{0,4},{4,0},{8,12},{12,8},{16,20},{20,16},{24,28},{28,24},{32,36},... | collective-permute-start | bytes 1572872 | tf_op jit(solution)/shard_map/ppermute | solution.py:265
  71.8 1.5 back.1
  73.2 6.2 %collective-permute-start = (bf16[256,1024]{1,0:T(8,128)(2,1)S(1)}, bf16[256,1024]{1,0:T(8,128)(2,1)S(1)}, u32[]{:S(2)}, u32[]{:S(2)}) collective-permute-start(bf16[256,1024]{1,0:T(8,128)(2,1)S(1)} %get-tuple-element.46), channel_id=1, source_target_pairs={{0,4},{4,0},{8,12},{12,8},{16,20},{20,16},{24,28},{28,24},{32,36},... | collective-permute-start | bytes 1572872 | tf_op jit(solution)/shard_map/ppermute | solution.py:265
  79.5 1.2 add_convert_fusion
  80.7 0.3 collective-permute-done
  81.2 25.5 %all_to_all.32.parts = bf16[16,32,1024]{2,1,0:T(8,128)(2,1)S(1)} all-to-all(bf16[16,32,1024]{2,1,0:T(8,128)(2,1)S(1)} %pad_maximum_fusion), channel_id=1, replica_groups={{0,64,128,192,256,320,384,448,8,72,136,200,264,328,392,456},{16,80,144,..., dimensions={0} | all-to-all | bytes 2097152 | tf_op jit(solution)/shard_map/all_to_all | solution.py:255
  106.8 3.8 %collective-permute-start.4 = (bf16[32,1024]{1,0:T(8,128)(2,1)S(1)}, bf16[32,1024]{1,0:T(8,128)(2,1)S(1)}, u32[]{:S(2)}, u32[]{:S(2)}) collective-permute-start(bf16[32,1024]{1,0:T(8,128)(2,1)S(1)} %first_sum.1.own), channel_id=1, source_target_pairs={{0,32},{16,48},{32,0},{48,16},{8,40},{24,56},{40,8},{56,24},{64,96... | collective-permute-start | bytes 196616 | tf_op jit(solution)/shard_map/ppermute | solution.py:347
  110.6 3.5 %collective-permute-start.3 = (bf16[32,1024]{1,0:T(8,128)(2,1)S(1)}, bf16[32,1024]{1,0:T(8,128)(2,1)S(1)}, u32[]{:S(2)}, u32[]{:S(2)}) collective-permute-start(bf16[32,1024]{1,0:T(8,128)(2,1)S(1)} %first_sum.1.own), channel_id=1, source_target_pairs={{0,48},{16,0},{32,16},{48,32},{8,56},{24,8},{40,24},{56,40},{64,11... | collective-permute-start | bytes 196616 | tf_op jit(solution)/shard_map/ppermute | solution.py:347
  114.1 2.8 %collective-permute-start.2 = (bf16[32,1024]{1,0:T(8,128)(2,1)S(1)}, bf16[32,1024]{1,0:T(8,128)(2,1)S(1)}, u32[]{:S(2)}, u32[]{:S(2)}) collective-permute-start(bf16[32,1024]{1,0:T(8,128)(2,1)S(1)} %first_sum.1.own), channel_id=1, source_target_pairs={{0,16},{16,32},{32,48},{48,0},{8,24},{24,40},{40,56},{56,8},{64,80... | collective-permute-start | bytes 196616 | tf_op jit(solution)/shard_map/ppermute | solution.py:347
  117.0 0.5 collective-permute-done.3.right
  117.5 3.9 %collective-permute-done.2.left = bf16[32,1024]{1,0:T(8,128)(2,1)S(1)} collective-permute-done((bf16[32,1024]{1,0:T(8,128)(2,1)S(1)}, bf16[32,1024]{1,0:T(8,128)(2,1)S(1)}, u32[]{:S(2)}, u32[]{:S(2)}) %collective-permute-start.2) | collective-permute-done | bytes 65568 | tf_op jit(solution)/shard_map/ppermute | solution.py:347
  121.5 27.1 %all_to_all.33.half = bf16[16,256,128]{2,1,0:T(8,128)(2,1)S(1)} all-to-all(bf16[16,256,128]{2,1,0:T(8,128)(2,1)S(1)} %second_sum.1), channel_id=1, replica_groups={{0,64,128,192,256,320,384,448,8,72,136,200,264,328,392,456},{16,80,144,..., dimensions={0} | all-to-all | bytes 2097152 | tf_op jit(solution)/shard_map/all_to_all | solution.py:255
  148.6 1.9 %collective-permute-start.5 = (bf16[16,256,128]{2,1,0:T(8,128)(2,1)S(1)}, bf16[16,256,128]{2,1,0:T(8,128)(2,1)S(1)}, u32[]{:S(2)}, u32[]{:S(2)}) collective-permute-start(bf16[16,256,128]{2,1,0:T(8,128)(2,1)S(1)} %all_to_all.33.half), channel_id=1, source_target_pairs={{0,4},{4,0},{8,12},{12,8},{16,20},{20,16},{24,28},{28,24},{32,36},... | collective-permute-start | bytes 3145736 | tf_op jit(solution)/shard_map/ppermute | solution.py:265
  150.6 1.4 widen_own.1
  152.0 1.2 collective-permute-done.5.half
  153.2 1.4 widen_other.1
  (25 shorter events, 0.6 us)
Async XLA Ops:
  0.6 35.0 %copy-start.10 = (s32[1,4]{1,0:T(1,128)S(1)}, s32[1,4]{1,0:T(1,128)}, u32[]{:S(2)}) copy-start(s32[1,4]{1,0:T(1,128)} %param.15) | copy-start | bytes 52
  2.9 32.7 %all-to-all-start = ((bf16[128,8,128]{2,1,0:T(8,128)(2,1)}), bf16[128,8,128]{2,1,0:T(8,128)(2,1)S(1)}, u32[]{:S(2)}, u32[]{:S(2)}) async-start(bf16[128,8,128]{2,1,0:T(8,128)(2,1)} %pick.1), calls=%async_computation | async-start | bytes 524288 | tf_op jit(solution)/shard_map/all_to_all | solution.py:294
  21.4 0.9 copy-start
  22.3 0.9 copy-start.2
  23.2 0.9 copy-start.7
  24.1 0.7 copy-start.9
  25.6 21.9 %copy-start.1 = (bf16[512,128]{1,0:T(8,128)(2,1)S(1)}, bf16[512,128]{1,0:T(8,128)(2,1)}, u32[]{:S(2)}) copy-start(bf16[512,128]{1,0:T(8,128)(2,1)} %feats.3) | copy-start | bytes 393220
  25.6 21.9 %copy-start.3 = (bf16[512,128]{1,0:T(8,128)(2,1)S(1)}, bf16[512,128]{1,0:T(8,128)(2,1)}, u32[]{:S(2)}) copy-start(bf16[512,128]{1,0:T(8,128)(2,1)} %local.5) | copy-start | bytes 393220
  29.3 18.2 %copy-start.4 = (bf16[4,512,128]{2,1,0:T(8,128)(2,1)S(1)}, bf16[4,512,128]{2,1,0:T(8,128)(2,1)}, u32[]{:S(2)}) copy-start(bf16[4,512,128]{2,1,0:T(8,128)(2,1)} %get-tuple-element.36.weights) | copy-start | bytes 1572868
  36.4 22.0 %copy-start.5 = (bf16[4,512,128]{2,1,0:T(8,128)(2,1)S(1)}, bf16[4,512,128]{2,1,0:T(8,128)(2,1)}, u32[]{:S(2)}) copy-start(bf16[4,512,128]{2,1,0:T(8,128)(2,1)} %get-tuple-element.39.weights) | copy-start | bytes 1572868
  36.5 22.0 %copy-start.6 = (bf16[512,128]{1,0:T(8,128)(2,1)S(1)}, bf16[512,128]{1,0:T(8,128)(2,1)}, u32[]{:S(2)}) copy-start(bf16[512,128]{1,0:T(8,128)(2,1)} %grad.3) | copy-start | bytes 393220
  49.0 14.6 %copy-start.8 = (s32[1,4]{1,0:T(1,128)S(1)}, s32[1,4]{1,0:T(1,128)}, u32[]{:S(2)}) copy-start(s32[1,4]{1,0:T(1,128)} %param.16) | copy-start | bytes 52
  60.1 11.7 %all-to-all-start.3 = ((bf16[4,512,128]{2,1,0:T(8,128)(2,1)}), bf16[4,512,128]{2,1,0:T(8,128)(2,1)S(1)}, u32[]{:S(2)}, u32[]{:S(2)}) async-start(bf16[4,512,128]{2,1,0:T(8,128)(2,1)} %get-tuple-element.43), calls=%async_computation.3 | async-start | bytes 1048576 | tf_op jit(solution)/shard_map/all_to_all | solution.py:261
  65.4 14.0 %collective-permute-start.1 = (bf16[256,1024]{1,0:T(8,128)(2,1)}, bf16[256,1024]{1,0:T(8,128)(2,1)}, u32[]{:S(2)}, u32[]{:S(2)}) collective-permute-start(bf16[256,1024]{1,0:T(8,128)(2,1)} %get-tuple-element.49), channel_id=1, source_target_pairs={{0,4},{4,0},{8,12},{12,8},{16,20},{20,16},{24,28},{28,24},{32,36},... | collective-permute-start | bytes 1572872 | tf_op jit(solution)/shard_map/ppermute | solution.py:265
  73.2 7.7 %collective-permute-start = (bf16[256,1024]{1,0:T(8,128)(2,1)S(1)}, bf16[256,1024]{1,0:T(8,128)(2,1)S(1)}, u32[]{:S(2)}, u32[]{:S(2)}) collective-permute-start(bf16[256,1024]{1,0:T(8,128)(2,1)S(1)} %get-tuple-element.46), channel_id=1, source_target_pairs={{0,4},{4,0},{8,12},{12,8},{16,20},{20,16},{24,28},{28,24},{32,36},... | collective-permute-start | bytes 1572872 | tf_op jit(solution)/shard_map/ppermute | solution.py:265
  106.8 10.1 %collective-permute-start.4 = (bf16[32,1024]{1,0:T(8,128)(2,1)S(1)}, bf16[32,1024]{1,0:T(8,128)(2,1)S(1)}, u32[]{:S(2)}, u32[]{:S(2)}) collective-permute-start(bf16[32,1024]{1,0:T(8,128)(2,1)S(1)} %first_sum.1.own), channel_id=1, source_target_pairs={{0,32},{16,48},{32,0},{48,16},{8,40},{24,56},{40,8},{56,24},{64,96... | collective-permute-start | bytes 196616 | tf_op jit(solution)/shard_map/ppermute | solution.py:347
  110.6 6.8 %collective-permute-start.3 = (bf16[32,1024]{1,0:T(8,128)(2,1)S(1)}, bf16[32,1024]{1,0:T(8,128)(2,1)S(1)}, u32[]{:S(2)}, u32[]{:S(2)}) collective-permute-start(bf16[32,1024]{1,0:T(8,128)(2,1)S(1)} %first_sum.1.own), channel_id=1, source_target_pairs={{0,48},{16,0},{32,16},{48,32},{8,56},{24,8},{40,24},{56,40},{64,11... | collective-permute-start | bytes 196616 | tf_op jit(solution)/shard_map/ppermute | solution.py:347
  114.1 7.2 %collective-permute-start.2 = (bf16[32,1024]{1,0:T(8,128)(2,1)S(1)}, bf16[32,1024]{1,0:T(8,128)(2,1)S(1)}, u32[]{:S(2)}, u32[]{:S(2)}) collective-permute-start(bf16[32,1024]{1,0:T(8,128)(2,1)S(1)} %first_sum.1.own), channel_id=1, source_target_pairs={{0,16},{16,32},{32,48},{48,0},{8,24},{24,40},{40,56},{56,8},{64,80... | collective-permute-start | bytes 196616 | tf_op jit(solution)/shard_map/ppermute | solution.py:347
  148.6 4.5 %collective-permute-start.5 = (bf16[16,256,128]{2,1,0:T(8,128)(2,1)S(1)}, bf16[16,256,128]{2,1,0:T(8,128)(2,1)S(1)}, u32[]{:S(2)}, u32[]{:S(2)}) collective-permute-start(bf16[16,256,128]{2,1,0:T(8,128)(2,1)S(1)} %all_to_all.33.half), channel_id=1, source_target_pairs={{0,4},{4,0},{8,12},{12,8},{16,20},{20,16},{24,28},{28,24},{32,36},... | collective-permute-start | bytes 3145736 | tf_op jit(solution)/shard_map/ppermute | solution.py:265

commit v7 on v6

--- a/solution.py
+++ b/solution.py
@@ -182,14 +182,15 @@
     return total
 
 
-def first_body(parts, total):
-    total[...] = add_up(parts).astype(BF)
-
-
-def second_body(own, left, right, opposite, copies, table):
+def first_body(parts, copies):
+    total = add_up(parts).astype(BF)
+    for i in range(copies.shape[0]):
+        copies[i] = total
+
+
+def second_body(parts, copies, table):
     rows, experts, cols = table.shape
-    total = own[...].astype(F32) + opposite[...].astype(F32)
-    total = total + (left[...].astype(F32) + right[...].astype(F32))
+    total = add_up(parts)
     for e in range(experts):
         table[:, e, :] = total[:, e * cols : (e + 1) * cols]
     laid = table[...].reshape(rows * experts, cols).astype(BF)
@@ -342,21 +343,15 @@
     both = jnp.concatenate([pair_one.reshape(split), pair_two.reshape(split)], axis=1)
     both = exchange(both, first)
     few = both.shape[1]
-    (own,) = call(first_body, "first_sum", [VMEM], [(both.shape[1:], BF)])(both)
-    shifted = [
-        lax.ppermute(
-            own, "dom", [(g[i], g[(i + k) % CROSS]) for g in second for i in range(CROSS)]
-        )
-        for k in (2, 1, 3)
-    ]
-    opposite, left, right = shifted
+    (both,) = call(first_body, "first_sum", [VMEM], [((CROSS,) + both.shape[1:], BF)])(both)
+    both = exchange(both, second)
     (both,) = call(
         second_body,
         "second_sum",
-        [VMEM] * 4,
+        [VMEM],
         [((RING, few * experts, cols), BF)],
         [pltpu.VMEM((few, experts, cols), F32)],
-    )(own, left, right, opposite)
+    )(both)
     same = exchange(both, first)
     grad_one, grad_two = widen(core, swap(same), widen(core, same))
     return h_two, h_one, grad_one.reshape(w_one.shape), grad_two.reshape(w_two.shape)

time: 155 us -> 151 us (0.974)
  blocking collectives: 73.1 us -> 82.7 us
  starting transfers between devices: 46.4 us -> 37.6 us
  waiting for transfers between devices: 12.1 us -> 7.4 us
    ppermute x3 -> x0, starting transfers between devices: 10.1 us -> none  [shards(): lax.ppermute(own, 'dom', [(g[i], g[(i + k) % CROSS]) for g in second for...]
    all_to_all x2 -> x3, blocking collectives: 52.6 us -> 62.2 us  [exchange(): lax.all_to_all(blocks, 'dom', split_axis=0, concat_axis=0, axis_index_gro...]
    ppermute x3 -> x0, waiting for transfers between devices: 4.37 us -> none  [shards(): lax.ppermute(own, 'dom', [(g[i], g[(i + k) % CROSS]) for g in second for...]
  transfers between devices with their start and end apart: 8 -> 5, of which waited for: 5 -> 3; matrix products, arithmetic and copies ran while one was open for 1% -> 1% of each run, Pallas kernels for 6% -> 6%
where the time goes in v7:
time: 151 us
  blocking collectives  82.7 us (55%)
  starting transfers between devices  37.6 us (25%)
  Pallas kernels  17.2 us (11%)
  waiting for transfers between devices  7.4 us (5%)
  local copies, waits for them, and re-layouts  3.4 us (2%)
    all_to_all x3, blocking collectives, exchange(): lax.all_to_all(blocks, 'dom', split_axis=0, concat_axis=0, axis_index_gro...  62.2 us
    all_to_all x2, blocking collectives, across(): lax.all_to_all(blocks, 'rep', split_axis=0, concat_axis=0, tiled=True)  20.5 us
    all_to_all x1, starting transfers between devices, shards(): lax.all_to_all(rows_out, 'dom', split_axis=0, concat_axis=0, tiled=True)  18.4 us
    ppermute x3, starting transfers between devices, swap(): return lax.ppermute(rows, 'dom', [(p, p ^ 1) for p in range(128)])  15.7 us
    all_to_all x1, waiting for transfers between devices, shards(): lax.all_to_all(rows_out, 'dom', split_axis=0, concat_axis=0, tiled=True)  6.25 us
    pallas_call x1, Pallas kernels, shards(): call(choose_body, 'choose', [SMEM] + [FAR] * 2, [(chosen, BF)] * 2, [pltp...  3.68 us
    all_to_all x1, starting transfers between devices, across(): lax.all_to_all(blocks, 'rep', split_axis=0, concat_axis=0, tiled=True)  3.47 us
    unnamed x22, local copies, waits for them, and re-layouts  3.4 us
  transfers between devices with their start and end apart: 5, of which 3 were waited for; matrix products, arithmetic and copies ran while one was open for 1% of the time, Pallas kernels for 6%

profile of v7, /device:TPU:1, one launch (start us, length us, event | category | flops | bytes accessed | tf_op | source)
XLA Modules:
  0.0 150.5 jit_solution(3770217072215185551)
XLA Ops:
  0.6 2.3 %pick.1 = bf16[128,8,128]{2,1,0:T(8,128)(2,1)} custom-call(s32[4,128]{1,0:T(4,128)} %bitcast.21, bf16[512,128]{1,0:T(8,128)(2,1)} %feats.3, bf16[512,128]{1,0:T(8,128)(2,1)} %hist_far.1), custom_call_target="tpu_custom_call" | custom-call | tf_op jit(solution)/shard_map/pick/pallas_call | solution.py:282
  3.0 18.4 %all-to-all-start = ((bf16[128,8,128]{2,1,0:T(8,128)(2,1)}), bf16[128,8,128]{2,1,0:T(8,128)(2,1)S(1)}, u32[]{:S(2)}, u32[]{:S(2)}) async-start(bf16[128,8,128]{2,1,0:T(8,128)(2,1)} %pick.1), calls=%async_computation | async-start | bytes 524288 | tf_op jit(solution)/shard_map/all_to_all | solution.py:295
  21.4 0.9 copy-done
  22.3 0.9 copy-done.2
  23.2 0.9 copy-done.7
  24.1 0.7 copy-done.9
  24.8 0.9 ready.1
  25.7 3.7 %choose.1 = (bf16[4,512,128]{2,1,0:T(8,128)(2,1)}, bf16[4,512,128]{2,1,0:T(8,128)(2,1)}) custom-call(s32[4]{0:T(128)} %bitcast.12, bf16[512,8,128]{2,1,0:T(8,128)(2,1)} %w_one_far.1, bf16[512,8,128]{2,1,0:T(8,128)(2,1)} %w_two_far.1), custom_call_target="tpu_custom_call" | custom-call | tf_op jit(solution)/shard_map/choose/pallas_call | solution.py:299
  29.4 6.3 %all-to-all-done = bf16[128,8,128]{2,1,0:T(8,128)(2,1)S(1)} async-done(((bf16[128,8,128]{2,1,0:T(8,128)(2,1)}), bf16[128,8,128]{2,1,0:T(8,128)(2,1)S(1)}, u32[]{:S(2)}, u32[]{:S(2)}) %all-to-all-start) | async-done | bytes 262176 | tf_op jit(solution)/shard_map/all_to_all | solution.py:295
  35.6 0.8 gather.1
  36.5 11.1 %all_to_all.35.agg = bf16[4,512,128]{2,1,0:T(8,128)(2,1)S(1)} all-to-all(bf16[4,512,128]{2,1,0:T(8,128)(2,1)S(1)} %get-tuple-element.35), channel_id=1, replica_groups=mesh['dom'=128,'rep'=4] {'rep'}, dimensions={0} | all-to-all | bytes 1048576 | tf_op jit(solution)/shard_map/all_to_all | solution.py:262
  47.6 1.4 one.1
  49.0 9.5 %all_to_all.36.agg = bf16[4,512,128]{2,1,0:T(8,128)(2,1)S(1)} all-to-all(bf16[4,512,128]{2,1,0:T(8,128)(2,1)S(1)} %get-tuple-element.38), channel_id=1, replica_groups=mesh['dom'=128,'rep'=4] {'rep'}, dimensions={0} | all-to-all | bytes 1048576 | tf_op jit(solution)/shard_map/all_to_all | solution.py:262
  58.4 1.7 %two.1 = (bf16[512,128]{1,0:T(8,128)(2,1)}, bf16[512,128]{1,0:T(8,128)(2,1)S(1)}, bf16[4,512,128]{2,1,0:T(8,128)(2,1)}) custom-call(bf16[4,512,128]{2,1,0:T(8,128)(2,1)S(1)} %all_to_all.36.agg, bf16[4,512,128]{2,1,0:T(8,128)(2,1)S(1)} %copy-done.5, bf16[512,128]{1,0:T(8,128)(2,1)S(1)} %get-tuple-element.40.h_one, bf16[512,128]{1,0:T(8,128)(2,1)S(1)} %copy-done.6), custom_call_target="tpu_custom_call" | custom-call | tf_op jit(solution)/shard_map/two/pallas_call | solution.py:323
  60.1 3.5 %all-to-all-start.3 = ((bf16[4,512,128]{2,1,0:T(8,128)(2,1)}), bf16[4,512,128]{2,1,0:T(8,128)(2,1)S(1)}, u32[]{:S(2)}, u32[]{:S(2)}) async-start(bf16[4,512,128]{2,1,0:T(8,128)(2,1)} %get-tuple-element.43), calls=%async_computation.3 | async-start | bytes 1048576 | tf_op jit(solution)/shard_map/all_to_all | solution.py:262
  63.6 1.8 %grad_two.1 = (f32[256,1024]{1,0:T(8,128)S(1)}, bf16[256,1024]{1,0:T(8,128)(2,1)}) custom-call(s32[4]{0:T(128)S(1)} %bitcast.13, s32[1]{0:T(128)} %bitcast.5.core, bf16[4,512,128]{2,1,0:T(8,128)(2,1)S(1)} %all_to_all.36.agg, bf16[512,128]{1,0:T(8,128)(2,1)S(1)} %get-tuple-element.47.dz), custom_call_target="tpu_custom_call" | custom-call | tf_op jit(solution)/shard_map/grad_two/pallas_call | solution.py:329
  65.4 6.3 %collective-permute-start.1 = (bf16[256,1024]{1,0:T(8,128)(2,1)}, bf16[256,1024]{1,0:T(8,128)(2,1)}, u32[]{:S(2)}, u32[]{:S(2)}) collective-permute-start(bf16[256,1024]{1,0:T(8,128)(2,1)} %get-tuple-element.49), channel_id=1, source_target_pairs={{0,4},{4,0},{8,12},{12,8},{16,20},{20,16},{24,28},{28,24},{32,36},... | collective-permute-start | bytes 1572872 | tf_op jit(solution)/shard_map/ppermute | solution.py:266
  71.8 1.5 back.1
  73.2 6.2 %collective-permute-start = (bf16[256,1024]{1,0:T(8,128)(2,1)S(1)}, bf16[256,1024]{1,0:T(8,128)(2,1)S(1)}, u32[]{:S(2)}, u32[]{:S(2)}) collective-permute-start(bf16[256,1024]{1,0:T(8,128)(2,1)S(1)} %get-tuple-element.46), channel_id=1, source_target_pairs={{0,4},{4,0},{8,12},{12,8},{16,20},{20,16},{24,28},{28,24},{32,36},... | collective-permute-start | bytes 1572872 | tf_op jit(solution)/shard_map/ppermute | solution.py:266
  79.5 1.2 add_convert_fusion
  80.7 0.3 collective-permute-done
  81.0 0.1 add_convert_fusion.1
  81.1 0.1 pad_maximum_fusion
  81.2 25.4 %all_to_all.37.parts = bf16[16,32,1024]{2,1,0:T(8,128)(2,1)S(1)} all-to-all(bf16[16,32,1024]{2,1,0:T(8,128)(2,1)S(1)} %pad_maximum_fusion), channel_id=1, replica_groups={{0,64,128,192,256,320,384,448,8,72,136,200,264,328,392,456},{16,80,144,..., dimensions={0} | all-to-all | bytes 2097152 | tf_op jit(solution)/shard_map/all_to_all | solution.py:256
  106.7 0.1 first_sum.1
  106.8 11.6 %all_to_all.38.parts = bf16[4,32,1024]{2,1,0:T(8,128)(2,1)S(1)} all-to-all(bf16[4,32,1024]{2,1,0:T(8,128)(2,1)S(1)} %first_sum.1), channel_id=1, replica_groups={{0,16,32,48},{8,24,40,56},{64,80,96,112},{72,88,104,120},{128,144,160,1..., dimensions={0} | all-to-all | bytes 524288 | tf_op jit(solution)/shard_map/all_to_all | solution.py:256
  118.5 0.2 second_sum.1
  118.6 25.1 %all_to_all.39.half = bf16[16,256,128]{2,1,0:T(8,128)(2,1)S(1)} all-to-all(bf16[16,256,128]{2,1,0:T(8,128)(2,1)S(1)} %second_sum.1), channel_id=1, replica_groups={{0,64,128,192,256,320,384,448,8,72,136,200,264,328,392,456},{16,80,144,..., dimensions={0} | all-to-all | bytes 2097152 | tf_op jit(solution)/shard_map/all_to_all | solution.py:256
  143.7 3.2 %collective-permute-start.2 = (bf16[16,256,128]{2,1,0:T(8,128)(2,1)S(1)}, bf16[16,256,128]{2,1,0:T(8,128)(2,1)S(1)}, u32[]{:S(2)}, u32[]{:S(2)}) collective-permute-start(bf16[16,256,128]{2,1,0:T(8,128)(2,1)S(1)} %all_to_all.39.half), channel_id=1, source_target_pairs={{0,4},{4,0},{8,12},{12,8},{16,20},{20,16},{24,28},{28,24},{32,36},... | collective-permute-start | bytes 3145736 | tf_op jit(solution)/shard_map/ppermute | solution.py:266
  146.9 1.4 widen_own.1
  148.3 0.8 collective-permute-done.2.half
  149.1 1.4 widen_other.1
  (20 shorter events, 0.1 us)
Async XLA Ops:
  0.6 35.0 %copy-start.10 = (s32[1,4]{1,0:T(1,128)S(1)}, s32[1,4]{1,0:T(1,128)}, u32[]{:S(2)}) copy-start(s32[1,4]{1,0:T(1,128)} %param.15) | copy-start | bytes 52
  3.0 32.7 %all-to-all-start = ((bf16[128,8,128]{2,1,0:T(8,128)(2,1)}), bf16[128,8,128]{2,1,0:T(8,128)(2,1)S(1)}, u32[]{:S(2)}, u32[]{:S(2)}) async-start(bf16[128,8,128]{2,1,0:T(8,128)(2,1)} %pick.1), calls=%async_computation | async-start | bytes 524288 | tf_op jit(solution)/shard_map/all_to_all | solution.py:295
  21.4 0.9 copy-start
  22.3 0.9 copy-start.2
  23.2 0.9 copy-start.7
  24.1 0.7 copy-start.9
  25.6 21.9 %copy-start.1 = (bf16[512,128]{1,0:T(8,128)(2,1)S(1)}, bf16[512,128]{1,0:T(8,128)(2,1)}, u32[]{:S(2)}) copy-start(bf16[512,128]{1,0:T(8,128)(2,1)} %feats.3) | copy-start | bytes 393220
  25.7 21.9 %copy-start.3 = (bf16[512,128]{1,0:T(8,128)(2,1)S(1)}, bf16[512,128]{1,0:T(8,128)(2,1)}, u32[]{:S(2)}) copy-start(bf16[512,128]{1,0:T(8,128)(2,1)} %local.5) | copy-start | bytes 393220
  29.4 18.2 %copy-start.4 = (bf16[4,512,128]{2,1,0:T(8,128)(2,1)S(1)}, bf16[4,512,128]{2,1,0:T(8,128)(2,1)}, u32[]{:S(2)}) copy-start(bf16[4,512,128]{2,1,0:T(8,128)(2,1)} %get-tuple-element.36.weights) | copy-start | bytes 1572868
  36.5 22.0 %copy-start.5 = (bf16[4,512,128]{2,1,0:T(8,128)(2,1)S(1)}, bf16[4,512,128]{2,1,0:T(8,128)(2,1)}, u32[]{:S(2)}) copy-start(bf16[4,512,128]{2,1,0:T(8,128)(2,1)} %get-tuple-element.39.weights) | copy-start | bytes 1572868
  36.5 22.0 %copy-start.6 = (bf16[512,128]{1,0:T(8,128)(2,1)S(1)}, bf16[512,128]{1,0:T(8,128)(2,1)}, u32[]{:S(2)}) copy-start(bf16[512,128]{1,0:T(8,128)(2,1)} %grad.3) | copy-start | bytes 393220
  49.0 14.6 %copy-start.8 = (s32[1,4]{1,0:T(1,128)S(1)}, s32[1,4]{1,0:T(1,128)}, u32[]{:S(2)}) copy-start(s32[1,4]{1,0:T(1,128)} %param.16) | copy-start | bytes 52
  60.1 11.7 %all-to-all-start.3 = ((bf16[4,512,128]{2,1,0:T(8,128)(2,1)}), bf16[4,512,128]{2,1,0:T(8,128)(2,1)S(1)}, u32[]{:S(2)}, u32[]{:S(2)}) async-start(bf16[4,512,128]{2,1,0:T(8,128)(2,1)} %get-tuple-element.43), calls=%async_computation.3 | async-start | bytes 1048576 | tf_op jit(solution)/shard_map/all_to_all | solution.py:262
  65.4 14.0 %collective-permute-start.1 = (bf16[256,1024]{1,0:T(8,128)(2,1)}, bf16[256,1024]{1,0:T(8,128)(2,1)}, u32[]{:S(2)}, u32[]{:S(2)}) collective-permute-start(bf16[256,1024]{1,0:T(8,128)(2,1)} %get-tuple-element.49), channel_id=1, source_target_pairs={{0,4},{4,0},{8,12},{12,8},{16,20},{20,16},{24,28},{28,24},{32,36},... | collective-permute-start | bytes 1572872 | tf_op jit(solution)/shard_map/ppermute | solution.py:266
  73.2 7.7 %collective-permute-start = (bf16[256,1024]{1,0:T(8,128)(2,1)S(1)}, bf16[256,1024]{1,0:T(8,128)(2,1)S(1)}, u32[]{:S(2)}, u32[]{:S(2)}) collective-permute-start(bf16[256,1024]{1,0:T(8,128)(2,1)S(1)} %get-tuple-element.46), channel_id=1, source_target_pairs={{0,4},{4,0},{8,12},{12,8},{16,20},{20,16},{24,28},{28,24},{32,36},... | collective-permute-start | bytes 1572872 | tf_op jit(solution)/shard_map/ppermute | solution.py:266
  143.7 5.4 %collective-permute-start.2 = (bf16[16,256,128]{2,1,0:T(8,128)(2,1)S(1)}, bf16[16,256,128]{2,1,0:T(8,128)(2,1)S(1)}, u32[]{:S(2)}, u32[]{:S(2)}) collective-permute-start(bf16[16,256,128]{2,1,0:T(8,128)(2,1)S(1)} %all_to_all.39.half), channel_id=1, source_target_pairs={{0,4},{4,0},{8,12},{12,8},{16,20},{20,16},{24,28},{28,24},{32,36},... | collective-permute-start | bytes 3145736 | tf_op jit(solution)/shard_map/ppermute | solution.py:266

commit v8 on v7

--- a/solution.py
+++ b/solution.py
@@ -54,17 +54,25 @@
     return copies
 
 
-def pick_body(send_far, feats_far, hist_far, out, rows, send, table, sems):
+def pick_body(core, send_far, feats_far, hist_far, out, rows, send, table, sems):
     cap, parts = send.shape
     nodes, cols = feats_far.shape
-    targets = (send, table.at[:, :cols], table.at[:, cols:])
-    for copy in fetch((send_far, feats_far, hist_far), targets, sems):
+    chips = parts // 2
+    copies = fetch(
+        (send_far, feats_far, hist_far), (send, table.at[:, :cols], table.at[:, cols:]), sems
+    )
+    at, source = iota((parts, parts), 0), iota((parts, parts), 1)
+    side = jnp.where(at < chips, core[0], 1 - core[0])
+    order = (source == (at % chips) * 2 + side).astype(F32).astype(BF)
+    for copy in copies:
         copy.wait()
     for c in range(cap):
         hit = (iota((nodes, parts), 0) == send[c : c + 1, :]).astype(F32).astype(BF)
-        got = dot(hit, table[...], ((0,), (0,)))
-        rows[:, c, :] = got[:, :cols]
-        rows[:, cap + c, :] = got[:, cols:]
+        got = dot(order, dot(hit, table[...], ((0,), (0,))).astype(BF))
+        for k in range(2):
+            half = got[k * chips : (k + 1) * chips]
+            rows[:, 2 * k * cap + c, :] = half[:, :cols]
+            rows[:, (2 * k + 1) * cap + c, :] = half[:, cols:]
     out[...] = rows[...].astype(BF)
 
 
@@ -85,19 +93,18 @@
             out[j, i * span : (i + 1) * span, :] = got[j * span : (j + 1) * span]
 
 
-def choose_body(types, w_one_far, w_two_far, one, two, w_one, w_two, sems):
-    copies = fetch((w_one_far, w_two_far), (w_one, w_two), sems)
-    copies[0].wait()
-    select_rows(types, w_one, one)
-    copies[1].wait()
-    select_rows(types, w_two, two)
-
-
-def ready_body(pick, local, halo_val, feats, base, wide):
+def choose_body(types, far, out, near, sems):
+    (copy,) = fetch((far,), (near,), sems)
+    copy.wait()
+    select_rows(types, near, out)
+
+
+def ready_body(core, pick, local, halo_val, feats, base, wide):
     cap = wide.shape[2] // 2 // 32
     shape = (TILE, 2 * TILE)
     k, m = iota(shape, 0), iota(shape, 1)
-    spot = (k // cap) * (2 * cap) + k % cap
+    half = jnp.where((k // cap) % 2 == core[0], 0, TILE)
+    spot = half + (k // cap // 2) * (2 * cap) + k % cap
     first = (m == spot).astype(F32).astype(BF)
     second = (m == spot + cap).astype(F32).astype(BF)
     for j in range(wide.shape[0]):
@@ -106,9 +113,10 @@
         wide[pick[j], TILE:, :] = dot(halo_val[block(j), :], second).astype(BF)
 
 
-def gather_body(pick, landed, wide, base, copies, part):
+def gather_body(pick, landed, other, wide, base, copies, part):
     for j in range(wide.shape[0]):
-        both = dot(wide[pick[j]], landed[pick[j]])
+        halo = jnp.concatenate([landed[pick[j]], other[pick[j]]], axis=0)
+        both = dot(wide[pick[j]], halo)
         agg = (base[block(j), :] + both[:TILE]).astype(BF)
         part[block(j), :] = both[TILE:]
         for q in range(copies.shape[0]):
@@ -282,38 +290,43 @@
     (rows_out,) = call(
         pick_body,
         "pick",
-        [FAR] * 3,
-        [((parts, 2 * cap, cols), BF)],
+        [SMEM] + [FAR] * 3,
+        [((parts // 2, 4 * cap, cols), BF)],
         [
-            pltpu.VMEM((parts, 2 * cap, cols), F32),
+            pltpu.VMEM((parts // 2, 4 * cap, cols), F32),
             pltpu.VMEM((cap, parts), jnp.int32),
             pltpu.VMEM((nodes, 2 * cols), BF),
             pltpu.SemaphoreType.DMA((3,)),
         ],
         FULL,
-    )(jnp.swapaxes(halo_send[0], 0, 1), feats, hist_one)
-    landed = lax.all_to_all(rows_out, "dom", split_axis=0, concat_axis=0, tiled=True)
-    landed = landed.reshape(rows, 2 * TILE, cols)
-
+    )(core, jnp.swapaxes(halo_send[0], 0, 1), feats, hist_one)
+    alike = [[2 * chip + c for chip in range(parts // 2)] for c in range(2)]
+    landed = exchange(rows_out, alike)
+    flat_halo = (rows, TILE, cols)
     chosen = (rows, width, cols)
-    pick_one, pick_two = call(
+    choose = call(
         choose_body,
         "choose",
-        [SMEM] + [FAR] * 2,
-        [(chosen, BF)] * 2,
-        [pltpu.VMEM(w_one.shape, BF)] * 2 + [pltpu.SemaphoreType.DMA((2,))],
+        [SMEM, FAR],
+        [(chosen, BF)],
+        [pltpu.VMEM(w_one.shape, BF), pltpu.SemaphoreType.DMA((1,))],
         FULL,
-    )(types, w_one, w_two)
+    )
+    (pick_one,) = choose(types, w_one)
+    (pick_two,) = choose(types, w_two)
     base, wide = call(
         ready_body,
         "ready",
-        [SMEM] + [VMEM] * 3,
+        [SMEM] * 2 + [VMEM] * 3,
         [(flat, F32), ((rows, 2 * TILE, 2 * TILE), BF)],
-    )(pick, local_val, halo_val, feats)
-
-    base, wide, pick_one, pick_two = lax.optimization_barrier((base, wide, pick_one, pick_two))
-    copies, part = call(gather_body, "gather", [SMEM] + [VMEM] * 3, [(copied, BF), (flat, F32)])(
-        pick, landed, wide, base
+    )(core, pick, local_val, halo_val, feats)
+
+    landed, base, wide, pick_one = lax.optimization_barrier((landed, base, wide, pick_one))
+    other = swap(landed[:, 2 * cap :]).reshape(flat_halo)
+    landed = landed[:, : 2 * cap].reshape(flat_halo)
+    base, pick_two = lax.optimization_barrier((base, pick_two))
+    copies, part = call(gather_body, "gather", [SMEM] + [VMEM] * 4, [(copied, BF), (flat, F32)])(
+        pick, landed, other, wide, base
     )
     agg_one = across(copies)
     h_one, near, slope, copies = call(

time: 151 us -> 157 us (1.040)
  waiting for transfers between devices: 7.4 us -> 11 us
  local copies, waits for them, and re-layouts: 3.4 us -> 0.06 us
  Pallas kernels: 17.2 us -> 20.2 us
    all_to_all x2, blocking collectives: 20.5 us -> 24.2 us  [across(): lax.all_to_all(blocks, 'rep', split_axis=0, concat_axis=0, tiled=True)]
    unnamed x22 -> x16, local copies, waits for them, and re-layouts: 3.4 us -> 0.04 us
    pallas_call x4 -> x5, Pallas kernels: 7.68 us -> 10.7 us  [the longest x1 3.11 us: shards(): pick_one, = choose(types, w_one)]
    all_to_all x3, blocking collectives: 62.2 us -> 59.6 us  [exchange(): lax.all_to_all(blocks, 'dom', split_axis=0, concat_axis=0, axis_index_gro...]
    ppermute x3 -> x4, starting transfers between devices: 15.7 us -> 18 us  [swap(): return lax.ppermute(rows, 'dom', [(p, p ^ 1) for p in range(128)])]
    all_to_all x1, waiting for transfers between devices: 6.25 us -> 8.49 us  [exchange(): lax.all_to_all(blocks, 'dom', split_axis=0, concat_axis=0, axis_index_gro...]
  transfers between devices with their start and end apart: 5 -> 6, of which waited for: 3 -> 4; matrix products, arithmetic and copies ran while one was open for 1% -> 1% of each run, Pallas kernels for 6% -> 8%
where the time goes in v8:
time: 157 us; the launch traced here: 156 us
  blocking collectives  83.7 us (53%)
  starting transfers between devices  38.7 us (25%)
  Pallas kernels  20.2 us (13%)
  waiting for transfers between devices  11 us (7%)
    all_to_all x3, blocking collectives, exchange(): lax.all_to_all(blocks, 'dom', split_axis=0, concat_axis=0, axis_index_gro...  59.6 us
    all_to_all x2, blocking collectives, across(): lax.all_to_all(blocks, 'rep', split_axis=0, concat_axis=0, tiled=True)  24.2 us
    ppermute x4, starting transfers between devices, swap(): return lax.ppermute(rows, 'dom', [(p, p ^ 1) for p in range(128)])  18 us
    all_to_all x1, starting transfers between devices, exchange(): lax.all_to_all(blocks, 'dom', split_axis=0, concat_axis=0, axis_index_gro...  17.1 us
    all_to_all x1, waiting for transfers between devices, exchange(): lax.all_to_all(blocks, 'dom', split_axis=0, concat_axis=0, axis_index_gro...  8.49 us
    all_to_all x1, starting transfers between devices, across(): lax.all_to_all(blocks, 'rep', split_axis=0, concat_axis=0, tiled=True)  3.47 us
  transfers between devices with their start and end apart: 6, of which 4 were waited for; matrix products, arithmetic and copies ran while one was open for 1% of the time, Pallas kernels for 8%

profile of v8, /device:TPU:1, one launch (start us, length us, event | category | flops | bytes accessed | tf_op | source)
XLA Modules:
  0.0 155.9 jit_solution(10789483998806950156)
XLA Ops:
  0.7 2.8 %pick.1 = bf16[64,16,128]{2,1,0:T(8,128)(2,1)} custom-call(s32[1]{0:T(128)} %bitcast.1.core, s32[4,128]{1,0:T(4,128)} %bitcast.24, bf16[512,128]{1,0:T(8,128)(2,1)} %feats.3, bf16[512,128]{1,0:T(8,128)(2,1)} %hist_far.1), custom_call_target="tpu_custom_call" | custom-call | tf_op jit(solution)/shard_map/pick/pallas_call | solution.py:290
  3.4 17.1 %all-to-all-start = ((bf16[64,16,128]{2,1,0:T(8,128)(2,1)}), bf16[64,16,128]{2,1,0:T(8,128)(2,1)S(1)}, u32[]{:S(2)}, u32[]{:S(2)}) async-start(bf16[64,16,128]{2,1,0:T(8,128)(2,1)} %pick.1), calls=%async_computation | async-start | bytes 524288 | tf_op jit(solution)/shard_map/all_to_all | solution.py:264
  20.6 3.1 %choose.2.weights = bf16[4,512,128]{2,1,0:T(8,128)(2,1)} custom-call(s32[4]{0:T(128)} %bitcast.14, bf16[512,8,128]{2,1,0:T(8,128)(2,1)} %far.2), custom_call_target="tpu_custom_call" | custom-call | tf_op jit(solution)/shard_map/choose/pallas_call | solution.py:315
  23.8 0.9 ready.1
  24.7 8.5 %all-to-all-done = bf16[64,16,128]{2,1,0:T(8,128)(2,1)S(1)} async-done(((bf16[64,16,128]{2,1,0:T(8,128)(2,1)}), bf16[64,16,128]{2,1,0:T(8,128)(2,1)S(1)}, u32[]{:S(2)}, u32[]{:S(2)}) %all-to-all-start) | async-done | bytes 262176 | tf_op jit(solution)/shard_map/all_to_all | solution.py:264
  33.2 5.4 %collective-permute-start = (bf16[64,8,128]{2,1,0:T(8,128)(2,1)S(1)}, bf16[64,8,128]{2,1,0:T(8,128)(2,1)S(1)}, u32[]{:S(2)}, u32[]{:S(2)}) collective-permute-start(bf16[64,8,128]{2,1,0:T(8,128)(2,1)S(1)} %get-tuple-element.54), channel_id=1, source_target_pairs={{0,4},{4,0},{8,12},{12,8},{16,20},{20,16},{24,28},{28,24},{32,36},... | collective-permute-start | bytes 393224 | tf_op jit(solution)/shard_map/ppermute | solution.py:274
  38.6 3.1 %choose.3.weights = bf16[4,512,128]{2,1,0:T(8,128)(2,1)} custom-call(s32[4]{0:T(128)} %bitcast.15, bf16[512,8,128]{2,1,0:T(8,128)(2,1)} %far.3), custom_call_target="tpu_custom_call" | custom-call | tf_op jit(solution)/shard_map/choose/pallas_call | solution.py:316
  41.7 0.8 gather.1
  42.6 0.0 copy-start.4
  42.6 13.3 %all_to_all.35.agg = bf16[4,512,128]{2,1,0:T(8,128)(2,1)S(1)} all-to-all(bf16[4,512,128]{2,1,0:T(8,128)(2,1)S(1)} %get-tuple-element.35), channel_id=1, replica_groups=mesh['dom'=128,'rep'=4] {'rep'}, dimensions={0} | all-to-all | bytes 1048576 | tf_op jit(solution)/shard_map/all_to_all | solution.py:270
  55.9 1.4 one.1
  57.3 10.9 %all_to_all.36.agg = bf16[4,512,128]{2,1,0:T(8,128)(2,1)S(1)} all-to-all(bf16[4,512,128]{2,1,0:T(8,128)(2,1)S(1)} %get-tuple-element.38), channel_id=1, replica_groups=mesh['dom'=128,'rep'=4] {'rep'}, dimensions={0} | all-to-all | bytes 1048576 | tf_op jit(solution)/shard_map/all_to_all | solution.py:270
  68.2 1.7 %two.1 = (bf16[512,128]{1,0:T(8,128)(2,1)}, bf16[512,128]{1,0:T(8,128)(2,1)S(1)}, bf16[4,512,128]{2,1,0:T(8,128)(2,1)}) custom-call(bf16[4,512,128]{2,1,0:T(8,128)(2,1)S(1)} %all_to_all.36.agg, bf16[4,512,128]{2,1,0:T(8,128)(2,1)S(1)} %copy-done.1, bf16[512,128]{1,0:T(8,128)(2,1)S(1)} %get-tuple-element.40.h_one, bf16[512,128]{1,0:T(8,128)(2,1)S(1)} %copy-done.4), custom_call_target="tpu_custom_call" | custom-call | tf_op jit(solution)/shard_map/two/pallas_call | solution.py:336
  69.8 3.5 %all-to-all-start.3 = ((bf16[4,512,128]{2,1,0:T(8,128)(2,1)}), bf16[4,512,128]{2,1,0:T(8,128)(2,1)S(1)}, u32[]{:S(2)}, u32[]{:S(2)}) async-start(bf16[4,512,128]{2,1,0:T(8,128)(2,1)} %get-tuple-element.43), calls=%async_computation.3 | async-start | bytes 1048576 | tf_op jit(solution)/shard_map/all_to_all | solution.py:270
  73.3 1.8 %grad_two.1 = (f32[256,1024]{1,0:T(8,128)S(1)}, bf16[256,1024]{1,0:T(8,128)(2,1)}) custom-call(s32[4]{0:T(128)S(1)} %bitcast.16, s32[1]{0:T(128)} %bitcast.1.core, bf16[4,512,128]{2,1,0:T(8,128)(2,1)S(1)} %all_to_all.36.agg, bf16[512,128]{1,0:T(8,128)(2,1)S(1)} %get-tuple-element.47.dz), custom_call_target="tpu_custom_call" | custom-call | tf_op jit(solution)/shard_map/grad_two/pallas_call | solution.py:342
  75.2 3.9 %collective-permute-start.2 = (bf16[256,1024]{1,0:T(8,128)(2,1)}, bf16[256,1024]{1,0:T(8,128)(2,1)}, u32[]{:S(2)}, u32[]{:S(2)}) collective-permute-start(bf16[256,1024]{1,0:T(8,128)(2,1)} %get-tuple-element.49), channel_id=1, source_target_pairs={{0,4},{4,0},{8,12},{12,8},{16,20},{20,16},{24,28},{28,24},{32,36},... | collective-permute-start | bytes 1572872 | tf_op jit(solution)/shard_map/ppermute | solution.py:274
  79.1 1.4 all-to-all-done.3.parts
  80.5 1.5 back.1
  81.9 5.2 %collective-permute-start.1 = (bf16[256,1024]{1,0:T(8,128)(2,1)S(1)}, bf16[256,1024]{1,0:T(8,128)(2,1)S(1)}, u32[]{:S(2)}, u32[]{:S(2)}) collective-permute-start(bf16[256,1024]{1,0:T(8,128)(2,1)S(1)} %get-tuple-element.46), channel_id=1, source_target_pairs={{0,4},{4,0},{8,12},{12,8},{16,20},{20,16},{24,28},{28,24},{32,36},... | collective-permute-start | bytes 1572872 | tf_op jit(solution)/shard_map/ppermute | solution.py:274
  87.1 1.2 add_convert_fusion
  88.3 0.3 collective-permute-done.1
  88.6 0.1 add_convert_fusion.1
  88.8 0.1 pad_maximum_fusion
  88.9 23.8 %all_to_all.37.parts = bf16[16,32,1024]{2,1,0:T(8,128)(2,1)S(1)} all-to-all(bf16[16,32,1024]{2,1,0:T(8,128)(2,1)S(1)} %pad_maximum_fusion), channel_id=1, replica_groups={{0,64,128,192,256,320,384,448,8,72,136,200,264,328,392,456},{16,80,144,..., dimensions={0} | all-to-all | bytes 2097152 | tf_op jit(solution)/shard_map/all_to_all | solution.py:264
  112.7 0.1 first_sum.1
  112.9 11.6 %all_to_all.38.parts = bf16[4,32,1024]{2,1,0:T(8,128)(2,1)S(1)} all-to-all(bf16[4,32,1024]{2,1,0:T(8,128)(2,1)S(1)} %first_sum.1), channel_id=1, replica_groups={{0,16,32,48},{8,24,40,56},{64,80,96,112},{72,88,104,120},{128,144,160,1..., dimensions={0} | all-to-all | bytes 524288 | tf_op jit(solution)/shard_map/all_to_all | solution.py:264
  124.5 0.2 second_sum.1
  124.7 24.1 %all_to_all.39.half = bf16[16,256,128]{2,1,0:T(8,128)(2,1)S(1)} all-to-all(bf16[16,256,128]{2,1,0:T(8,128)(2,1)S(1)} %second_sum.1), channel_id=1, replica_groups={{0,64,128,192,256,320,384,448,8,72,136,200,264,328,392,456},{16,80,144,..., dimensions={0} | all-to-all | bytes 2097152 | tf_op jit(solution)/shard_map/all_to_all | solution.py:264
  148.8 3.5 %collective-permute-start.3 = (bf16[16,256,128]{2,1,0:T(8,128)(2,1)S(1)}, bf16[16,256,128]{2,1,0:T(8,128)(2,1)S(1)}, u32[]{:S(2)}, u32[]{:S(2)}) collective-permute-start(bf16[16,256,128]{2,1,0:T(8,128)(2,1)S(1)} %all_to_all.39.half), channel_id=1, source_target_pairs={{0,4},{4,0},{8,12},{12,8},{16,20},{20,16},{24,28},{28,24},{32,36},... | collective-permute-start | bytes 3145736 | tf_op jit(solution)/shard_map/ppermute | solution.py:274
  152.3 1.4 widen_own.1
  153.7 0.8 collective-permute-done.3.half
  154.6 1.4 widen_other.1
  (18 shorter events, 0.1 us)
Async XLA Ops:
  0.6 23.1 %copy-start.2 = (bf16[512,128]{1,0:T(8,128)(2,1)S(1)}, bf16[512,128]{1,0:T(8,128)(2,1)}, u32[]{:S(2)}) copy-start(bf16[512,128]{1,0:T(8,128)(2,1)} %feats.3) | copy-start | bytes 393220
  0.6 23.1 %copy-start.3 = (bf16[512,128]{1,0:T(8,128)(2,1)S(1)}, bf16[512,128]{1,0:T(8,128)(2,1)}, u32[]{:S(2)}) copy-start(bf16[512,128]{1,0:T(8,128)(2,1)} %local.5) | copy-start | bytes 393220
  0.7 23.1 %copy-start.7 = (s32[1,4]{1,0:T(1,128)S(1)}, s32[1,4]{1,0:T(1,128)}, u32[]{:S(2)}) copy-start(s32[1,4]{1,0:T(1,128)} %param.15) | copy-start | bytes 52
  0.7 23.1 %copy-start.5 = (bf16[512,128]{1,0:T(8,128)(2,1)S(1)}, bf16[512,128]{1,0:T(8,128)(2,1)}, u32[]{:S(2)}) copy-start(bf16[512,128]{1,0:T(8,128)(2,1)} %halo_val.1) | copy-start | bytes 393220
  3.4 29.7 %all-to-all-start = ((bf16[64,16,128]{2,1,0:T(8,128)(2,1)}), bf16[64,16,128]{2,1,0:T(8,128)(2,1)S(1)}, u32[]{:S(2)}, u32[]{:S(2)}) async-start(bf16[64,16,128]{2,1,0:T(8,128)(2,1)} %pick.1), calls=%async_computation | async-start | bytes 524288 | tf_op jit(solution)/shard_map/all_to_all | solution.py:264
  33.2 22.7 %copy-start = (bf16[4,512,128]{2,1,0:T(8,128)(2,1)S(1)}, bf16[4,512,128]{2,1,0:T(8,128)(2,1)}, u32[]{:S(2)}) copy-start(bf16[4,512,128]{2,1,0:T(8,128)(2,1)} %choose.2.weights) | copy-start | bytes 1572868
  33.2 8.6 %collective-permute-start = (bf16[64,8,128]{2,1,0:T(8,128)(2,1)S(1)}, bf16[64,8,128]{2,1,0:T(8,128)(2,1)S(1)}, u32[]{:S(2)}, u32[]{:S(2)}) collective-permute-start(bf16[64,8,128]{2,1,0:T(8,128)(2,1)S(1)} %get-tuple-element.54), channel_id=1, source_target_pairs={{0,4},{4,0},{8,12},{12,8},{16,20},{20,16},{24,28},{28,24},{32,36},... | collective-permute-start | bytes 393224 | tf_op jit(solution)/shard_map/ppermute | solution.py:274
  42.6 25.6 %copy-start.1 = (bf16[4,512,128]{2,1,0:T(8,128)(2,1)S(1)}, bf16[4,512,128]{2,1,0:T(8,128)(2,1)}, u32[]{:S(2)}) copy-start(bf16[4,512,128]{2,1,0:T(8,128)(2,1)} %choose.3.weights) | copy-start | bytes 1572868
  42.6 25.6 %copy-start.4 = (bf16[512,128]{1,0:T(8,128)(2,1)S(1)}, bf16[512,128]{1,0:T(8,128)(2,1)}, u32[]{:S(2)}) copy-start(bf16[512,128]{1,0:T(8,128)(2,1)} %grad.3) | copy-start | bytes 393220
  57.3 16.1 %copy-start.6 = (s32[1,4]{1,0:T(1,128)S(1)}, s32[1,4]{1,0:T(1,128)}, u32[]{:S(2)}) copy-start(s32[1,4]{1,0:T(1,128)} %param.16) | copy-start | bytes 52
  69.8 10.6 %all-to-all-start.3 = ((bf16[4,512,128]{2,1,0:T(8,128)(2,1)}), bf16[4,512,128]{2,1,0:T(8,128)(2,1)S(1)}, u32[]{:S(2)}, u32[]{:S(2)}) async-start(bf16[4,512,128]{2,1,0:T(8,128)(2,1)} %get-tuple-element.43), calls=%async_computation.3 | async-start | bytes 1048576 | tf_op jit(solution)/shard_map/all_to_all | solution.py:270
  75.2 12.0 %collective-permute-start.2 = (bf16[256,1024]{1,0:T(8,128)(2,1)}, bf16[256,1024]{1,0:T(8,128)(2,1)}, u32[]{:S(2)}, u32[]{:S(2)}) collective-permute-start(bf16[256,1024]{1,0:T(8,128)(2,1)} %get-tuple-element.49), channel_id=1, source_target_pairs={{0,4},{4,0},{8,12},{12,8},{16,20},{20,16},{24,28},{28,24},{32,36},... | collective-permute-start | bytes 1572872 | tf_op jit(solution)/shard_map/ppermute | solution.py:274
  81.9 6.7 %collective-permute-start.1 = (bf16[256,1024]{1,0:T(8,128)(2,1)S(1)}, bf16[256,1024]{1,0:T(8,128)(2,1)S(1)}, u32[]{:S(2)}, u32[]{:S(2)}) collective-permute-start(bf16[256,1024]{1,0:T(8,128)(2,1)S(1)} %get-tuple-element.46), channel_id=1, source_target_pairs={{0,4},{4,0},{8,12},{12,8},{16,20},{20,16},{24,28},{28,24},{32,36},... | collective-permute-start | bytes 1572872 | tf_op jit(solution)/shard_map/ppermute | solution.py:274
  148.8 5.8 %collective-permute-start.3 = (bf16[16,256,128]{2,1,0:T(8,128)(2,1)S(1)}, bf16[16,256,128]{2,1,0:T(8,128)(2,1)S(1)}, u32[]{:S(2)}, u32[]{:S(2)}) collective-permute-start(bf16[16,256,128]{2,1,0:T(8,128)(2,1)S(1)} %all_to_all.39.half), channel_id=1, source_target_pairs={{0,4},{4,0},{8,12},{12,8},{16,20},{20,16},{24,28},{28,24},{32,36},... | collective-permute-start | bytes 3145736 | tf_op jit(solution)/shard_map/ppermute | solution.py:274

commit v9 on v7

--- a/solution.py
+++ b/solution.py
@@ -1,3 +1,5 @@
+import functools
+
 import jax
 import jax.numpy as jnp
 from jax import lax
@@ -20,12 +22,12 @@
 TILE = 128
 
 
-def call(body, name, ins, outs, scratch=(), params=PARAMS):
+def call(body, name, ins, outs, scratch=(), params=PARAMS, places=None):
     return pl.pallas_call(
         body,
         out_shape=tuple(jax.ShapeDtypeStruct(shape, kind) for shape, kind in outs),
         in_specs=list(ins),
-        out_specs=tuple(VMEM for _ in outs),
+        out_specs=places or tuple(VMEM for _ in outs),
         scratch_shapes=list(scratch),
         compiler_params=params,
         name=name,
@@ -58,10 +60,13 @@
     cap, parts = send.shape
     nodes, cols = feats_far.shape
     targets = (send, table.at[:, :cols], table.at[:, cols:])
-    for copy in fetch((send_far, feats_far, hist_far), targets, sems):
+    copies = fetch((send_far, feats_far, hist_far), targets, sems)
+    copies[0].wait()
+    spot = iota((nodes, parts), 0)
+    hits = [(spot == send[c : c + 1, :]).astype(F32).astype(BF) for c in range(cap)]
+    for copy in copies[1:]:
         copy.wait()
-    for c in range(cap):
-        hit = (iota((nodes, parts), 0) == send[c : c + 1, :]).astype(F32).astype(BF)
+    for c, hit in enumerate(hits):
         got = dot(hit, table[...], ((0,), (0,)))
         rows[:, c, :] = got[:, :cols]
         rows[:, cap + c, :] = got[:, cols:]
@@ -134,8 +139,9 @@
             copies[q, block(j), :] = mixed
 
 
-def two_body(agg, weights, h_one, grad, hidden, dz, back):
+def two_body(agg, weights, h_one, grad, hidden, dz, back, near, sems):
     cols = dz.shape[1]
+    copies = []
     for j in range(weights.shape[0]):
         act, bend = forward(agg, weights, j)
         hidden[block(j), :] = (h_one[block(j), :].astype(F32) + act).astype(BF)
@@ -143,13 +149,18 @@
         dz[block(j), :] = d
         term = dot(d, weights[j], ((1,), (1,))).astype(BF)
         for q in range(back.shape[0]):
-            back[q, block(j), :] = term[:, q * cols : (q + 1) * cols]
-
-
-def write_grad(types, core, agg, dz, keep, send):
+            near[q, block(j), :] = term[:, q * cols : (q + 1) * cols]
+        spot = (slice(None), pl.ds(j * TILE, TILE))
+        copies.append(pltpu.make_async_copy(near.at[spot], back.at[spot], sems.at[j]))
+        copies[-1].start()
+    for copy in copies:
+        copy.wait()
+
+
+def grad_rows(types, side, agg, dz, target):
     reps, _, cols = agg.shape
     rows = types.shape[0]
-    experts = keep.shape[1] // cols
+    experts = target.shape[1] // cols
     wide = []
     for e in range(experts):
         part = []
@@ -157,13 +168,21 @@
             part.append((dz[block(j), :].astype(F32) * (types[j] == e).astype(F32)).astype(BF))
         wide.append(jnp.concatenate(part, axis=0))
     wide = jnp.concatenate(wide, axis=1)
-    for target, side in ((send, 1 - core[0]), (keep, core[0])):
-        for i in range(reps // 2):
-            got = dot(agg[side * (reps // 2) + i], wide, ((0,), (0,)))
-            target[i * cols : (i + 1) * cols, :] = got.astype(target.dtype)
-
-
-def back_body(types, core, parts, local, grad, slope, agg, keep, send, dz):
+    for i in range(reps // 2):
+        got = dot(agg[side * (reps // 2) + i], wide, ((0,), (0,)))
+        target[i * cols : (i + 1) * cols, :] = got.astype(target.dtype)
+
+
+def both_body(types, core, agg, dz, keep, send):
+    grad_rows(types, 1 - core[0], agg, dz, send)
+    grad_rows(types, core[0], agg, dz, keep)
+
+
+def keep_body(types, core, agg, dz, keep):
+    grad_rows(types, core[0], agg, dz, keep)
+
+
+def back_body(types, core, parts, local, grad, slope, agg, dz, send):
     for j in range(types.shape[0]):
         total = parts[0, block(j), :].astype(F32)
         for q in range(1, parts.shape[0]):
@@ -172,7 +191,7 @@
             local[block(j), :], total.astype(BF), ((0,), (0,))
         )
         dz[block(j), :] = (dh * slope[block(j), :]).astype(BF)
-    write_grad(types, core, agg, dz, keep, send)
+    grad_rows(types, 1 - core[0], agg, dz, send)
 
 
 def add_up(parts):
@@ -198,35 +217,47 @@
         copies[i] = laid
 
 
-def widen_body(core, half, *refs):
-    one, two = refs[-2:]
-    step = pl.program_id(0)
-    length = half.shape[1] // 2
-    count = one.shape[0] // length
-    for i in range(count):
-        rows = half[step * count + i].astype(F32)
-        one[i * length : (i + 1) * length, :] = rows[:length]
-        two[i * length : (i + 1) * length, :] = rows[length:]
+def widen_body(own, core, half, *refs):
+    one, two, wide, sems = refs[-4:]
+    chunks, length, _ = half.shape
+    length = length // 2
+    side = core[0] if own else 1 - core[0]
+    start = pl.multiple_of(side * (chunks * length), chunks * length)
+    count = 2
+    copies = []
+    for i in range(chunks // count):
+        for k in range(count):
+            at = i * count + k
+            rows = half[at].astype(F32)
+            wide[0, at * length : (at + 1) * length, :] = rows[:length]
+            wide[1, at * length : (at + 1) * length, :] = rows[length:]
+        span = count * length
+        for layer, target in enumerate((one, two)):
+            copies.append(
+                pltpu.make_async_copy(
+                    wide.at[layer, pl.ds(i * span, span)],
+                    target.at[pl.ds(start + i * span, span)],
+                    sems.at[2 * i + layer],
+                )
+            )
+            copies[-1].start()
+    for copy in copies:
+        copy.wait()
 
 
 def widen(core, half, before=()):
     chunks, length, cols = half.shape
-    steps = 2
     own = not before
-    height = chunks // steps * (length // 2)
-    target = pl.BlockSpec(
-        (height, cols), lambda i, c: ((c[0] if own else 1 - c[0]) * steps + i, 0)
-    )
     shape = jax.ShapeDtypeStruct((chunks * length, cols), F32)
     return pl.pallas_call(
-        widen_body,
-        grid_spec=pltpu.PrefetchScalarGridSpec(
-            num_scalar_prefetch=1,
-            grid=(steps,),
-            in_specs=[VMEM] + [ANY] * len(before),
-            out_specs=(target, target),
-        ),
+        functools.partial(widen_body, own),
+        in_specs=[SMEM, VMEM] + [ANY] * len(before),
+        out_specs=(ANY, ANY),
         out_shape=(shape, shape),
+        scratch_shapes=[
+            pltpu.VMEM((2, chunks * length // 2, cols), F32),
+            pltpu.SemaphoreType.DMA((chunks,)),
+        ],
         input_output_aliases={} if own else {2: 0, 3: 1},
         compiler_params=PARAMS,
         name="widen_own" if own else "widen_other",
@@ -321,21 +352,25 @@
     )(agg_one, pick_one, feats, local_val, part)
     agg_two = across(copies)
     h_two, dz_two, back = call(
-        two_body, "two", [VMEM] * 4, [(flat, BF), (flat, BF), (copied, BF)]
+        two_body,
+        "two",
+        [VMEM] * 4,
+        [(flat, BF), (flat, BF), (copied, BF)],
+        [pltpu.VMEM(copied, BF), pltpu.SemaphoreType.DMA((rows,))],
+        places=(VMEM, VMEM, ANY),
     )(agg_two, pick_two, near, grad_out)
     back = across(back)
 
     half = (width // 2, experts * cols)
     keep_two, send_two = call(
-        write_grad, "grad_two", [SMEM] * 2 + [VMEM] * 2, [(half, F32), (half, BF)]
+        both_body, "grad_two", [SMEM] * 2 + [VMEM] * 2, [(half, F32), (half, BF)]
     )(types, core, agg_two, dz_two)
-    keep_one, send_one = call(
-        back_body,
-        "back",
-        [SMEM] * 2 + [VMEM] * 5,
-        [(half, F32), (half, BF)],
-        [pltpu.VMEM(flat, BF)],
+    dz_one, send_one = call(
+        back_body, "back", [SMEM] * 2 + [VMEM] * 5, [(flat, BF), (half, BF)]
     )(types, core, back, local_val, grad_out, slope, agg_one)
+    (keep_one,) = call(keep_body, "grad_one", [SMEM] * 2 + [VMEM] * 2, [(half, F32)])(
+        types, core, agg_one, dz_one
+    )
     pair_one = (keep_one + swap(send_one).astype(F32)).astype(BF)
     pair_two = (keep_two + swap(send_two).astype(F32)).astype(BF)
 

time: 151 us -> 152 us (level)
    pallas_call x5 -> x6, Pallas kernels: 7.76 us -> 9.17 us  [the longest x2 2.91 us: widen(): pl.pallas_call(functools.partial(widen_body, own), in_specs=[SMEM, VMEM]...]
  transfers between devices with their start and end apart: 5 -> 5, of which waited for: 3 -> 2; matrix products, arithmetic and copies ran while one was open for 1% -> 1% of each run, Pallas kernels for 6% -> 7%
where the time goes in v9:
time: 152 us
  blocking collectives  83.5 us (55%)
  starting transfers between devices  36.6 us (24%)
  Pallas kernels  18.6 us (12%)
  waiting for transfers between devices  7.12 us (5%)
  local copies, waits for them, and re-layouts  3.4 us (2%)
    all_to_all x3, blocking collectives, exchange(): lax.all_to_all(blocks, 'dom', split_axis=0, concat_axis=0, axis_index_gro...  63 us
    all_to_all x2, blocking collectives, across(): lax.all_to_all(blocks, 'rep', split_axis=0, concat_axis=0, tiled=True)  20.5 us
    all_to_all x1, starting transfers between devices, shards(): lax.all_to_all(rows_out, 'dom', split_axis=0, concat_axis=0, tiled=True)  18.4 us
    ppermute x3, starting transfers between devices, swap(): return lax.ppermute(rows, 'dom', [(p, p ^ 1) for p in range(128)])  14.7 us
    all_to_all x1, waiting for transfers between devices, shards(): lax.all_to_all(rows_out, 'dom', split_axis=0, concat_axis=0, tiled=True)  6.26 us
    pallas_call x1, Pallas kernels, shards(): call(choose_body, 'choose', [SMEM] + [FAR] * 2, [(chosen, BF)] * 2, [pltp...  3.68 us
    all_to_all x1, starting transfers between devices, across(): lax.all_to_all(blocks, 'rep', split_axis=0, concat_axis=0, tiled=True)  3.48 us
    unnamed x22, local copies, waits for them, and re-layouts  3.4 us
  transfers between devices with their start and end apart: 5, of which 2 were waited for; matrix products, arithmetic and copies ran while one was open for 1% of the time, Pallas kernels for 7%

profile of v9, /device:TPU:1, one launch (start us, length us, event | category | flops | bytes accessed | tf_op | source)
XLA Modules:
  0.0 151.6 jit_solution(15335660031586552320)
XLA Ops:
  0.6 2.3 %pick.1 = bf16[128,8,128]{2,1,0:T(8,128)(2,1)} custom-call(s32[4,128]{1,0:T(4,128)} %bitcast.22, bf16[512,128]{1,0:T(8,128)(2,1)} %feats.3, bf16[512,128]{1,0:T(8,128)(2,1)} %hist_far.1), custom_call_target="tpu_custom_call" | custom-call | tf_op jit(solution)/shard_map/pick/pallas_call | solution.py:313
  2.9 18.4 %all-to-all-start = ((bf16[128,8,128]{2,1,0:T(8,128)(2,1)}), bf16[128,8,128]{2,1,0:T(8,128)(2,1)S(1)}, u32[]{:S(2)}, u32[]{:S(2)}) async-start(bf16[128,8,128]{2,1,0:T(8,128)(2,1)} %pick.1), calls=%async_computation | async-start | bytes 524288 | tf_op jit(solution)/shard_map/all_to_all | solution.py:326
  21.4 0.9 copy-done
  22.3 0.9 copy-done.2
  23.2 0.9 copy-done.7
  24.1 0.7 copy-done.9
  24.8 0.9 ready.1
  25.7 3.7 %choose.1 = (bf16[4,512,128]{2,1,0:T(8,128)(2,1)}, bf16[4,512,128]{2,1,0:T(8,128)(2,1)}) custom-call(s32[4]{0:T(128)} %bitcast.12, bf16[512,8,128]{2,1,0:T(8,128)(2,1)} %w_one_far.1, bf16[512,8,128]{2,1,0:T(8,128)(2,1)} %w_two_far.1), custom_call_target="tpu_custom_call" | custom-call | tf_op jit(solution)/shard_map/choose/pallas_call | solution.py:330
  29.4 6.3 %all-to-all-done = bf16[128,8,128]{2,1,0:T(8,128)(2,1)S(1)} async-done(((bf16[128,8,128]{2,1,0:T(8,128)(2,1)}), bf16[128,8,128]{2,1,0:T(8,128)(2,1)S(1)}, u32[]{:S(2)}, u32[]{:S(2)}) %all-to-all-start) | async-done | bytes 262176 | tf_op jit(solution)/shard_map/all_to_all | solution.py:326
  35.6 0.8 gather.1
  36.5 11.1 %all_to_all.35.agg = bf16[4,512,128]{2,1,0:T(8,128)(2,1)S(1)} all-to-all(bf16[4,512,128]{2,1,0:T(8,128)(2,1)S(1)} %get-tuple-element.35), channel_id=1, replica_groups=mesh['dom'=128,'rep'=4] {'rep'}, dimensions={0} | all-to-all | bytes 1048576 | tf_op jit(solution)/shard_map/all_to_all | solution.py:293
  47.6 1.4 one.1
  49.0 9.5 %all_to_all.36.agg = bf16[4,512,128]{2,1,0:T(8,128)(2,1)S(1)} all-to-all(bf16[4,512,128]{2,1,0:T(8,128)(2,1)S(1)} %get-tuple-element.38), channel_id=1, replica_groups=mesh['dom'=128,'rep'=4] {'rep'}, dimensions={0} | all-to-all | bytes 1048576 | tf_op jit(solution)/shard_map/all_to_all | solution.py:293
  58.4 2.2 %two.1 = (bf16[512,128]{1,0:T(8,128)(2,1)}, bf16[512,128]{1,0:T(8,128)(2,1)S(1)}, bf16[4,512,128]{2,1,0:T(8,128)(2,1)}) custom-call(bf16[4,512,128]{2,1,0:T(8,128)(2,1)S(1)} %all_to_all.36.agg, bf16[4,512,128]{2,1,0:T(8,128)(2,1)S(1)} %copy-done.5, bf16[512,128]{1,0:T(8,128)(2,1)S(1)} %get-tuple-element.40.h_one, bf16[512,128]{1,0:T(8,128)(2,1)S(1)} %copy-done.6), custom_call_target="tpu_custom_call" | custom-call | tf_op jit(solution)/shard_map/two/pallas_call | solution.py:354
  60.7 3.5 %all-to-all-start.3 = ((bf16[4,512,128]{2,1,0:T(8,128)(2,1)}), bf16[4,512,128]{2,1,0:T(8,128)(2,1)S(1)}, u32[]{:S(2)}, u32[]{:S(2)}) async-start(bf16[4,512,128]{2,1,0:T(8,128)(2,1)} %get-tuple-element.43), calls=%async_computation.3 | async-start | bytes 1048576 | tf_op jit(solution)/shard_map/all_to_all | solution.py:293
  64.2 1.8 %grad_two.1 = (f32[256,1024]{1,0:T(8,128)S(1)}, bf16[256,1024]{1,0:T(8,128)(2,1)}) custom-call(s32[4]{0:T(128)S(1)} %bitcast.13, s32[1]{0:T(128)} %bitcast.5.core, bf16[4,512,128]{2,1,0:T(8,128)(2,1)S(1)} %all_to_all.36.agg, bf16[512,128]{1,0:T(8,128)(2,1)S(1)} %get-tuple-element.47.dz), custom_call_target="tpu_custom_call" | custom-call | tf_op jit(solution)/shard_map/grad_two/pallas_call | solution.py:365
  66.0 6.3 %collective-permute-start.1 = (bf16[256,1024]{1,0:T(8,128)(2,1)}, bf16[256,1024]{1,0:T(8,128)(2,1)}, u32[]{:S(2)}, u32[]{:S(2)}) collective-permute-start(bf16[256,1024]{1,0:T(8,128)(2,1)} %get-tuple-element.49), channel_id=1, source_target_pairs={{0,4},{4,0},{8,12},{12,8},{16,20},{20,16},{24,28},{28,24},{32,36},... | collective-permute-start | bytes 1572872 | tf_op jit(solution)/shard_map/ppermute | solution.py:297
  72.3 1.2 back.1
  73.6 6.2 %collective-permute-start = (bf16[256,1024]{1,0:T(8,128)(2,1)S(1)}, bf16[256,1024]{1,0:T(8,128)(2,1)S(1)}, u32[]{:S(2)}, u32[]{:S(2)}) collective-permute-start(bf16[256,1024]{1,0:T(8,128)(2,1)S(1)} %get-tuple-element.46), channel_id=1, source_target_pairs={{0,4},{4,0},{8,12},{12,8},{16,20},{20,16},{24,28},{28,24},{32,36},... | collective-permute-start | bytes 1572872 | tf_op jit(solution)/shard_map/ppermute | solution.py:297
  79.8 1.0 grad_one.1
  80.8 1.2 add_convert_fusion
  82.0 0.1 add_convert_fusion.1
  82.1 0.1 pad_maximum_fusion
  82.2 25.1 %all_to_all.37.parts = bf16[16,32,1024]{2,1,0:T(8,128)(2,1)S(1)} all-to-all(bf16[16,32,1024]{2,1,0:T(8,128)(2,1)S(1)} %pad_maximum_fusion), channel_id=1, replica_groups={{0,64,128,192,256,320,384,448,8,72,136,200,264,328,392,456},{16,80,144,..., dimensions={0} | all-to-all | bytes 2097152 | tf_op jit(solution)/shard_map/all_to_all | solution.py:287
  107.3 0.1 first_sum.1
  107.5 12.2 %all_to_all.38.parts = bf16[4,32,1024]{2,1,0:T(8,128)(2,1)S(1)} all-to-all(bf16[4,32,1024]{2,1,0:T(8,128)(2,1)S(1)} %first_sum.1), channel_id=1, replica_groups={{0,16,32,48},{8,24,40,56},{64,80,96,112},{72,88,104,120},{128,144,160,1..., dimensions={0} | all-to-all | bytes 524288 | tf_op jit(solution)/shard_map/all_to_all | solution.py:287
  119.7 0.2 second_sum.1
  119.9 25.7 %all_to_all.39.half = bf16[16,256,128]{2,1,0:T(8,128)(2,1)S(1)} all-to-all(bf16[16,256,128]{2,1,0:T(8,128)(2,1)S(1)} %second_sum.1), channel_id=1, replica_groups={{0,64,128,192,256,320,384,448,8,72,136,200,264,328,392,456},{16,80,144,..., dimensions={0} | all-to-all | bytes 2097152 | tf_op jit(solution)/shard_map/all_to_all | solution.py:287
  145.6 2.2 %collective-permute-start.2 = (bf16[16,256,128]{2,1,0:T(8,128)(2,1)S(1)}, bf16[16,256,128]{2,1,0:T(8,128)(2,1)S(1)}, u32[]{:S(2)}, u32[]{:S(2)}) collective-permute-start(bf16[16,256,128]{2,1,0:T(8,128)(2,1)S(1)} %all_to_all.39.half), channel_id=1, source_target_pairs={{0,4},{4,0},{8,12},{12,8},{16,20},{20,16},{24,28},{28,24},{32,36},... | collective-permute-start | bytes 3145736 | tf_op jit(solution)/shard_map/ppermute | solution.py:297
  147.8 1.5 widen_own.1
  149.3 0.9 collective-permute-done.2.half
  150.1 1.5 widen_other.1
  (21 shorter events, 0.1 us)
Async XLA Ops:
  0.6 35.0 %copy-start.10 = (s32[1,4]{1,0:T(1,128)S(1)}, s32[1,4]{1,0:T(1,128)}, u32[]{:S(2)}) copy-start(s32[1,4]{1,0:T(1,128)} %param.15) | copy-start | bytes 52
  2.9 32.7 %all-to-all-start = ((bf16[128,8,128]{2,1,0:T(8,128)(2,1)}), bf16[128,8,128]{2,1,0:T(8,128)(2,1)S(1)}, u32[]{:S(2)}, u32[]{:S(2)}) async-start(bf16[128,8,128]{2,1,0:T(8,128)(2,1)} %pick.1), calls=%async_computation | async-start | bytes 524288 | tf_op jit(solution)/shard_map/all_to_all | solution.py:326
  21.4 0.9 copy-start
  22.3 0.9 copy-start.2
  23.2 0.9 copy-start.7
  24.1 0.7 copy-start.9
  25.6 21.9 %copy-start.1 = (bf16[512,128]{1,0:T(8,128)(2,1)S(1)}, bf16[512,128]{1,0:T(8,128)(2,1)}, u32[]{:S(2)}) copy-start(bf16[512,128]{1,0:T(8,128)(2,1)} %feats.3) | copy-start | bytes 393220
  25.6 21.9 %copy-start.3 = (bf16[512,128]{1,0:T(8,128)(2,1)S(1)}, bf16[512,128]{1,0:T(8,128)(2,1)}, u32[]{:S(2)}) copy-start(bf16[512,128]{1,0:T(8,128)(2,1)} %local.5) | copy-start | bytes 393220
  29.3 18.2 %copy-start.4 = (bf16[4,512,128]{2,1,0:T(8,128)(2,1)S(1)}, bf16[4,512,128]{2,1,0:T(8,128)(2,1)}, u32[]{:S(2)}) copy-start(bf16[4,512,128]{2,1,0:T(8,128)(2,1)} %get-tuple-element.36.weights) | copy-start | bytes 1572868
  36.4 22.0 %copy-start.5 = (bf16[4,512,128]{2,1,0:T(8,128)(2,1)S(1)}, bf16[4,512,128]{2,1,0:T(8,128)(2,1)}, u32[]{:S(2)}) copy-start(bf16[4,512,128]{2,1,0:T(8,128)(2,1)} %get-tuple-element.39.weights) | copy-start | bytes 1572868
  36.5 22.0 %copy-start.6 = (bf16[512,128]{1,0:T(8,128)(2,1)S(1)}, bf16[512,128]{1,0:T(8,128)(2,1)}, u32[]{:S(2)}) copy-start(bf16[512,128]{1,0:T(8,128)(2,1)} %grad.3) | copy-start | bytes 393220
  49.0 15.2 %copy-start.8 = (s32[1,4]{1,0:T(1,128)S(1)}, s32[1,4]{1,0:T(1,128)}, u32[]{:S(2)}) copy-start(s32[1,4]{1,0:T(1,128)} %param.16) | copy-start | bytes 52
  60.7 11.7 %all-to-all-start.3 = ((bf16[4,512,128]{2,1,0:T(8,128)(2,1)}), bf16[4,512,128]{2,1,0:T(8,128)(2,1)S(1)}, u32[]{:S(2)}, u32[]{:S(2)}) async-start(bf16[4,512,128]{2,1,0:T(8,128)(2,1)} %get-tuple-element.43), calls=%async_computation.3 | async-start | bytes 1048576 | tf_op jit(solution)/shard_map/all_to_all | solution.py:293
  66.0 14.8 %collective-permute-start.1 = (bf16[256,1024]{1,0:T(8,128)(2,1)}, bf16[256,1024]{1,0:T(8,128)(2,1)}, u32[]{:S(2)}, u32[]{:S(2)}) collective-permute-start(bf16[256,1024]{1,0:T(8,128)(2,1)} %get-tuple-element.49), channel_id=1, source_target_pairs={{0,4},{4,0},{8,12},{12,8},{16,20},{20,16},{24,28},{28,24},{32,36},... | collective-permute-start | bytes 1572872 | tf_op jit(solution)/shard_map/ppermute | solution.py:297
  73.6 8.4 %collective-permute-start = (bf16[256,1024]{1,0:T(8,128)(2,1)S(1)}, bf16[256,1024]{1,0:T(8,128)(2,1)S(1)}, u32[]{:S(2)}, u32[]{:S(2)}) collective-permute-start(bf16[256,1024]{1,0:T(8,128)(2,1)S(1)} %get-tuple-element.46), channel_id=1, source_target_pairs={{0,4},{4,0},{8,12},{12,8},{16,20},{20,16},{24,28},{28,24},{32,36},... | collective-permute-start | bytes 1572872 | tf_op jit(solution)/shard_map/ppermute | solution.py:297
  145.6 4.5 %collective-permute-start.2 = (bf16[16,256,128]{2,1,0:T(8,128)(2,1)S(1)}, bf16[16,256,128]{2,1,0:T(8,128)(2,1)S(1)}, u32[]{:S(2)}, u32[]{:S(2)}) collective-permute-start(bf16[16,256,128]{2,1,0:T(8,128)(2,1)S(1)} %all_to_all.39.half), channel_id=1, source_target_pairs={{0,4},{4,0},{8,12},{12,8},{16,20},{20,16},{24,28},{28,24},{32,36},... | collective-permute-start | bytes 3145736 | tf_op jit(solution)/shard_map/ppermute | solution.py:297

commit v10 on v7

--- a/solution.py
+++ b/solution.py
@@ -107,40 +107,52 @@
 
 
 def gather_body(pick, landed, wide, base, copies, part):
-    for j in range(wide.shape[0]):
-        both = dot(wide[pick[j]], landed[pick[j]])
-        agg = (base[block(j), :] + both[:TILE]).astype(BF)
-        part[block(j), :] = both[TILE:]
+    rows = range(wide.shape[0])
+    both = [dot(wide[pick[j]], landed[pick[j]]) for j in rows]
+    for j in rows:
+        agg = (base[block(j), :] + both[j][:TILE]).astype(BF)
+        part[block(j), :] = both[j][TILE:]
         for q in range(copies.shape[0]):
             copies[q, block(j), :] = agg
 
 
-def forward(agg, weights, j):
-    rows = jnp.concatenate([agg[q, block(j), :] for q in range(agg.shape[0])], axis=1)
-    z = dot(rows, weights[j])
+def products(agg, weights):
+    out = []
+    for j in range(weights.shape[0]):
+        rows = jnp.concatenate([agg[q, block(j), :] for q in range(agg.shape[0])], axis=1)
+        out.append(dot(rows, weights[j]))
+    return out
+
+
+def activate(z):
     sig = jax.nn.sigmoid(z)
     return z * sig, sig * (1.0 + z * (1.0 - sig))
 
 
 def one_body(agg, weights, feats, local, part, hidden, near, slope, copies):
-    for j in range(weights.shape[0]):
-        act, bend = forward(agg, weights, j)
+    hs = []
+    for j, z in enumerate(products(agg, weights)):
+        act, bend = activate(z)
         slope[block(j), :] = bend
-        h = (feats[block(j), :].astype(F32) + act).astype(BF)
-        hidden[block(j), :] = h
-        near[block(j), :] = h
-        mixed = (dot(local[block(j), :], h) + part[block(j), :]).astype(BF)
+        hs.append((feats[block(j), :].astype(F32) + act).astype(BF))
+        hidden[block(j), :] = hs[j]
+        near[block(j), :] = hs[j]
+    mixed = [dot(local[block(j), :], h) for j, h in enumerate(hs)]
+    for j, term in enumerate(mixed):
+        term = (term + part[block(j), :]).astype(BF)
         for q in range(copies.shape[0]):
-            copies[q, block(j), :] = mixed
+            copies[q, block(j), :] = term
 
 
 def two_body(agg, weights, h_one, grad, hidden, dz, back):
     cols = dz.shape[1]
-    for j in range(weights.shape[0]):
-        act, bend = forward(agg, weights, j)
+    ds = []
+    for j, z in enumerate(products(agg, weights)):
+        act, bend = activate(z)
         hidden[block(j), :] = (h_one[block(j), :].astype(F32) + act).astype(BF)
-        d = (grad[block(j), :].astype(F32) * bend).astype(BF)
-        dz[block(j), :] = d
+        ds.append((grad[block(j), :].astype(F32) * bend).astype(BF))
+        dz[block(j), :] = ds[j]
+    for j, d in enumerate(ds):
         term = dot(d, weights[j], ((1,), (1,))).astype(BF)
         for q in range(back.shape[0]):
             back[q, block(j), :] = term[:, q * cols : (q + 1) * cols]
@@ -164,13 +176,16 @@
 
 
 def back_body(types, core, parts, local, grad, slope, agg, keep, send, dz):
-    for j in range(types.shape[0]):
+    rows = range(types.shape[0])
+    totals = []
+    for j in rows:
         total = parts[0, block(j), :].astype(F32)
         for q in range(1, parts.shape[0]):
             total = total + parts[q, block(j), :].astype(F32)
-        dh = grad[block(j), :].astype(F32) + dot(
-            local[block(j), :], total.astype(BF), ((0,), (0,))
-        )
+        totals.append(total.astype(BF))
+    terms = [dot(local[block(j), :], totals[j], ((0,), (0,))) for j in rows]
+    for j in rows:
+        dh = grad[block(j), :].astype(F32) + terms[j]
         dz[block(j), :] = (dh * slope[block(j), :]).astype(BF)
     write_grad(types, core, agg, dz, keep, send)
 

time: 151 us -> 150 us (level)
  no operation moved by 1% of the time
where the time goes in v10:
time: 150 us
  blocking collectives  82.7 us (55%)
  starting transfers between devices  37.6 us (25%)
  Pallas kernels  16.3 us (11%)
  waiting for transfers between devices  7.4 us (5%)
  local copies, waits for them, and re-layouts  3.4 us (2%)
    all_to_all x3, blocking collectives, exchange(): lax.all_to_all(blocks, 'dom', split_axis=0, concat_axis=0, axis_index_gro...  62.1 us
    all_to_all x2, blocking collectives, across(): lax.all_to_all(blocks, 'rep', split_axis=0, concat_axis=0, tiled=True)  20.5 us
    all_to_all x1, starting transfers between devices, shards(): lax.all_to_all(rows_out, 'dom', split_axis=0, concat_axis=0, tiled=True)  18.4 us
    ppermute x3, starting transfers between devices, swap(): return lax.ppermute(rows, 'dom', [(p, p ^ 1) for p in range(128)])  15.7 us
    all_to_all x1, waiting for transfers between devices, shards(): lax.all_to_all(rows_out, 'dom', split_axis=0, concat_axis=0, tiled=True)  6.25 us
    pallas_call x1, Pallas kernels, shards(): call(choose_body, 'choose', [SMEM] + [FAR] * 2, [(chosen, BF)] * 2, [pltp...  3.68 us
    all_to_all x1, starting transfers between devices, across(): lax.all_to_all(blocks, 'rep', split_axis=0, concat_axis=0, tiled=True)  3.47 us
    unnamed x22, local copies, waits for them, and re-layouts  3.4 us
  transfers between devices with their start and end apart: 5, of which 3 were waited for; matrix products, arithmetic and copies ran while one was open for 1% of the time, Pallas kernels for 6%

profile of v10, /device:TPU:1, one launch (start us, length us, event | category | flops | bytes accessed | tf_op | source)
XLA Modules:
  0.0 149.6 jit_solution(973544007901075520)
XLA Ops:
  0.6 2.3 %pick.1 = bf16[128,8,128]{2,1,0:T(8,128)(2,1)} custom-call(s32[4,128]{1,0:T(4,128)} %bitcast.21, bf16[512,128]{1,0:T(8,128)(2,1)} %feats.3, bf16[512,128]{1,0:T(8,128)(2,1)} %hist_far.1), custom_call_target="tpu_custom_call" | custom-call | tf_op jit(solution)/shard_map/pick/pallas_call | solution.py:297
  3.0 18.4 %all-to-all-start = ((bf16[128,8,128]{2,1,0:T(8,128)(2,1)}), bf16[128,8,128]{2,1,0:T(8,128)(2,1)S(1)}, u32[]{:S(2)}, u32[]{:S(2)}) async-start(bf16[128,8,128]{2,1,0:T(8,128)(2,1)} %pick.1), calls=%async_computation | async-start | bytes 524288 | tf_op jit(solution)/shard_map/all_to_all | solution.py:310
  21.4 0.9 copy-done
  22.3 0.9 copy-done.2
  23.2 0.9 copy-done.7
  24.1 0.7 copy-done.9
  24.8 0.9 ready.1
  25.7 3.7 %choose.1 = (bf16[4,512,128]{2,1,0:T(8,128)(2,1)}, bf16[4,512,128]{2,1,0:T(8,128)(2,1)}) custom-call(s32[4]{0:T(128)} %bitcast.12, bf16[512,8,128]{2,1,0:T(8,128)(2,1)} %w_one_far.1, bf16[512,8,128]{2,1,0:T(8,128)(2,1)} %w_two_far.1), custom_call_target="tpu_custom_call" | custom-call | tf_op jit(solution)/shard_map/choose/pallas_call | solution.py:314
  29.4 6.3 %all-to-all-done = bf16[128,8,128]{2,1,0:T(8,128)(2,1)S(1)} async-done(((bf16[128,8,128]{2,1,0:T(8,128)(2,1)}), bf16[128,8,128]{2,1,0:T(8,128)(2,1)S(1)}, u32[]{:S(2)}, u32[]{:S(2)}) %all-to-all-start) | async-done | bytes 262176 | tf_op jit(solution)/shard_map/all_to_all | solution.py:310
  35.6 0.8 gather.1
  36.5 11.1 %all_to_all.35.agg = bf16[4,512,128]{2,1,0:T(8,128)(2,1)S(1)} all-to-all(bf16[4,512,128]{2,1,0:T(8,128)(2,1)S(1)} %get-tuple-element.35), channel_id=1, replica_groups=mesh['dom'=128,'rep'=4] {'rep'}, dimensions={0} | all-to-all | bytes 1048576 | tf_op jit(solution)/shard_map/all_to_all | solution.py:277
  47.6 1.0 one.1
  48.5 9.5 %all_to_all.36.agg = bf16[4,512,128]{2,1,0:T(8,128)(2,1)S(1)} all-to-all(bf16[4,512,128]{2,1,0:T(8,128)(2,1)S(1)} %get-tuple-element.38), channel_id=1, replica_groups=mesh['dom'=128,'rep'=4] {'rep'}, dimensions={0} | all-to-all | bytes 1048576 | tf_op jit(solution)/shard_map/all_to_all | solution.py:277
  58.0 1.2 two.1
  59.2 3.5 %all-to-all-start.3 = ((bf16[4,512,128]{2,1,0:T(8,128)(2,1)}), bf16[4,512,128]{2,1,0:T(8,128)(2,1)S(1)}, u32[]{:S(2)}, u32[]{:S(2)}) async-start(bf16[4,512,128]{2,1,0:T(8,128)(2,1)} %get-tuple-element.43), calls=%async_computation.3 | async-start | bytes 1048576 | tf_op jit(solution)/shard_map/all_to_all | solution.py:277
  62.7 1.8 %grad_two.1 = (f32[256,1024]{1,0:T(8,128)S(1)}, bf16[256,1024]{1,0:T(8,128)(2,1)}) custom-call(s32[4]{0:T(128)S(1)} %bitcast.13, s32[1]{0:T(128)} %bitcast.5.core, bf16[4,512,128]{2,1,0:T(8,128)(2,1)S(1)} %all_to_all.36.agg, bf16[512,128]{1,0:T(8,128)(2,1)S(1)} %get-tuple-element.47.dz), custom_call_target="tpu_custom_call" | custom-call | tf_op jit(solution)/shard_map/grad_two/pallas_call | solution.py:344
  64.5 6.3 %collective-permute-start.1 = (bf16[256,1024]{1,0:T(8,128)(2,1)}, bf16[256,1024]{1,0:T(8,128)(2,1)}, u32[]{:S(2)}, u32[]{:S(2)}) collective-permute-start(bf16[256,1024]{1,0:T(8,128)(2,1)} %get-tuple-element.49), channel_id=1, source_target_pairs={{0,4},{4,0},{8,12},{12,8},{16,20},{20,16},{24,28},{28,24},{32,36},... | collective-permute-start | bytes 1572872 | tf_op jit(solution)/shard_map/ppermute | solution.py:281
  70.9 1.5 back.1
  72.4 6.2 %collective-permute-start = (bf16[256,1024]{1,0:T(8,128)(2,1)S(1)}, bf16[256,1024]{1,0:T(8,128)(2,1)S(1)}, u32[]{:S(2)}, u32[]{:S(2)}) collective-permute-start(bf16[256,1024]{1,0:T(8,128)(2,1)S(1)} %get-tuple-element.46), channel_id=1, source_target_pairs={{0,4},{4,0},{8,12},{12,8},{16,20},{20,16},{24,28},{28,24},{32,36},... | collective-permute-start | bytes 1572872 | tf_op jit(solution)/shard_map/ppermute | solution.py:281
  78.6 1.2 add_convert_fusion
  79.8 0.3 collective-permute-done
  80.1 0.1 add_convert_fusion.1
  80.2 0.1 pad_maximum_fusion
  80.3 25.5 %all_to_all.37.parts = bf16[16,32,1024]{2,1,0:T(8,128)(2,1)S(1)} all-to-all(bf16[16,32,1024]{2,1,0:T(8,128)(2,1)S(1)} %pad_maximum_fusion), channel_id=1, replica_groups={{0,64,128,192,256,320,384,448,8,72,136,200,264,328,392,456},{16,80,144,..., dimensions={0} | all-to-all | bytes 2097152 | tf_op jit(solution)/shard_map/all_to_all | solution.py:271
  105.8 0.1 first_sum.1
  105.9 11.6 %all_to_all.38.parts = bf16[4,32,1024]{2,1,0:T(8,128)(2,1)S(1)} all-to-all(bf16[4,32,1024]{2,1,0:T(8,128)(2,1)S(1)} %first_sum.1), channel_id=1, replica_groups={{0,16,32,48},{8,24,40,56},{64,80,96,112},{72,88,104,120},{128,144,160,1..., dimensions={0} | all-to-all | bytes 524288 | tf_op jit(solution)/shard_map/all_to_all | solution.py:271
  117.6 0.2 second_sum.1
  117.8 25.0 %all_to_all.39.half = bf16[16,256,128]{2,1,0:T(8,128)(2,1)S(1)} all-to-all(bf16[16,256,128]{2,1,0:T(8,128)(2,1)S(1)} %second_sum.1), channel_id=1, replica_groups={{0,64,128,192,256,320,384,448,8,72,136,200,264,328,392,456},{16,80,144,..., dimensions={0} | all-to-all | bytes 2097152 | tf_op jit(solution)/shard_map/all_to_all | solution.py:271
  142.8 3.2 %collective-permute-start.2 = (bf16[16,256,128]{2,1,0:T(8,128)(2,1)S(1)}, bf16[16,256,128]{2,1,0:T(8,128)(2,1)S(1)}, u32[]{:S(2)}, u32[]{:S(2)}) collective-permute-start(bf16[16,256,128]{2,1,0:T(8,128)(2,1)S(1)} %all_to_all.39.half), channel_id=1, source_target_pairs={{0,4},{4,0},{8,12},{12,8},{16,20},{20,16},{24,28},{28,24},{32,36},... | collective-permute-start | bytes 3145736 | tf_op jit(solution)/shard_map/ppermute | solution.py:281
  146.0 1.4 widen_own.1
  147.4 0.8 collective-permute-done.2.half
  148.3 1.4 widen_other.1
  (20 shorter events, 0.1 us)
Async XLA Ops:
  0.6 35.0 %copy-start.10 = (s32[1,4]{1,0:T(1,128)S(1)}, s32[1,4]{1,0:T(1,128)}, u32[]{:S(2)}) copy-start(s32[1,4]{1,0:T(1,128)} %param.15) | copy-start | bytes 52
  3.0 32.7 %all-to-all-start = ((bf16[128,8,128]{2,1,0:T(8,128)(2,1)}), bf16[128,8,128]{2,1,0:T(8,128)(2,1)S(1)}, u32[]{:S(2)}, u32[]{:S(2)}) async-start(bf16[128,8,128]{2,1,0:T(8,128)(2,1)} %pick.1), calls=%async_computation | async-start | bytes 524288 | tf_op jit(solution)/shard_map/all_to_all | solution.py:310
  21.4 0.9 copy-start
  22.3 0.9 copy-start.2
  23.2 0.9 copy-start.7
  24.1 0.7 copy-start.9
  25.6 21.9 %copy-start.1 = (bf16[512,128]{1,0:T(8,128)(2,1)S(1)}, bf16[512,128]{1,0:T(8,128)(2,1)}, u32[]{:S(2)}) copy-start(bf16[512,128]{1,0:T(8,128)(2,1)} %feats.3) | copy-start | bytes 393220
  25.7 21.9 %copy-start.3 = (bf16[512,128]{1,0:T(8,128)(2,1)S(1)}, bf16[512,128]{1,0:T(8,128)(2,1)}, u32[]{:S(2)}) copy-start(bf16[512,128]{1,0:T(8,128)(2,1)} %local.5) | copy-start | bytes 393220
  29.4 18.2 %copy-start.4 = (bf16[4,512,128]{2,1,0:T(8,128)(2,1)S(1)}, bf16[4,512,128]{2,1,0:T(8,128)(2,1)}, u32[]{:S(2)}) copy-start(bf16[4,512,128]{2,1,0:T(8,128)(2,1)} %get-tuple-element.36.weights) | copy-start | bytes 1572868
  36.5 21.5 %copy-start.5 = (bf16[4,512,128]{2,1,0:T(8,128)(2,1)S(1)}, bf16[4,512,128]{2,1,0:T(8,128)(2,1)}, u32[]{:S(2)}) copy-start(bf16[4,512,128]{2,1,0:T(8,128)(2,1)} %get-tuple-element.39.weights) | copy-start | bytes 1572868
  36.5 21.5 %copy-start.6 = (bf16[512,128]{1,0:T(8,128)(2,1)S(1)}, bf16[512,128]{1,0:T(8,128)(2,1)}, u32[]{:S(2)}) copy-start(bf16[512,128]{1,0:T(8,128)(2,1)} %grad.3) | copy-start | bytes 393220
  48.5 14.2 %copy-start.8 = (s32[1,4]{1,0:T(1,128)S(1)}, s32[1,4]{1,0:T(1,128)}, u32[]{:S(2)}) copy-start(s32[1,4]{1,0:T(1,128)} %param.16) | copy-start | bytes 52
  59.2 11.7 %all-to-all-start.3 = ((bf16[4,512,128]{2,1,0:T(8,128)(2,1)}), bf16[4,512,128]{2,1,0:T(8,128)(2,1)S(1)}, u32[]{:S(2)}, u32[]{:S(2)}) async-start(bf16[4,512,128]{2,1,0:T(8,128)(2,1)} %get-tuple-element.43), calls=%async_computation.3 | async-start | bytes 1048576 | tf_op jit(solution)/shard_map/all_to_all | solution.py:277
  64.5 14.0 %collective-permute-start.1 = (bf16[256,1024]{1,0:T(8,128)(2,1)}, bf16[256,1024]{1,0:T(8,128)(2,1)}, u32[]{:S(2)}, u32[]{:S(2)}) collective-permute-start(bf16[256,1024]{1,0:T(8,128)(2,1)} %get-tuple-element.49), channel_id=1, source_target_pairs={{0,4},{4,0},{8,12},{12,8},{16,20},{20,16},{24,28},{28,24},{32,36},... | collective-permute-start | bytes 1572872 | tf_op jit(solution)/shard_map/ppermute | solution.py:281
  72.4 7.7 %collective-permute-start = (bf16[256,1024]{1,0:T(8,128)(2,1)S(1)}, bf16[256,1024]{1,0:T(8,128)(2,1)S(1)}, u32[]{:S(2)}, u32[]{:S(2)}) collective-permute-start(bf16[256,1024]{1,0:T(8,128)(2,1)S(1)} %get-tuple-element.46), channel_id=1, source_target_pairs={{0,4},{4,0},{8,12},{12,8},{16,20},{20,16},{24,28},{28,24},{32,36},... | collective-permute-start | bytes 1572872 | tf_op jit(solution)/shard_map/ppermute | solution.py:281
  142.8 5.4 %collective-permute-start.2 = (bf16[16,256,128]{2,1,0:T(8,128)(2,1)S(1)}, bf16[16,256,128]{2,1,0:T(8,128)(2,1)S(1)}, u32[]{:S(2)}, u32[]{:S(2)}) collective-permute-start(bf16[16,256,128]{2,1,0:T(8,128)(2,1)S(1)} %all_to_all.39.half), channel_id=1, source_target_pairs={{0,4},{4,0},{8,12},{12,8},{16,20},{20,16},{24,28},{28,24},{32,36},... | collective-permute-start | bytes 3145736 | tf_op jit(solution)/shard_map/ppermute | solution.py:281

commit v11 on v10

--- a/solution.py
+++ b/solution.py
@@ -58,13 +58,17 @@
     cap, parts = send.shape
     nodes, cols = feats_far.shape
     targets = (send, table.at[:, :cols], table.at[:, cols:])
-    for copy in fetch((send_far, feats_far, hist_far), targets, sems):
+    copies = fetch((send_far, feats_far, hist_far), targets, sems)
+    copies[0].wait()
+    spot = iota((nodes, parts), 0)
+    hits = [(spot == send[c : c + 1, :]).astype(F32).astype(BF) for c in range(cap)]
+    hits = jnp.concatenate(hits, axis=1)
+    for copy in copies[1:]:
         copy.wait()
+    got = dot(hits, table[...], ((0,), (0,)))
     for c in range(cap):
-        hit = (iota((nodes, parts), 0) == send[c : c + 1, :]).astype(F32).astype(BF)
-        got = dot(hit, table[...], ((0,), (0,)))
-        rows[:, c, :] = got[:, :cols]
-        rows[:, cap + c, :] = got[:, cols:]
+        rows[:, c, :] = got[block(c), :cols]
+        rows[:, cap + c, :] = got[block(c), cols:]
     out[...] = rows[...].astype(BF)
 
 
@@ -129,13 +133,12 @@
     return z * sig, sig * (1.0 + z * (1.0 - sig))
 
 
-def one_body(agg, weights, feats, local, part, hidden, near, slope, copies):
+def one_body(agg, weights, feats, local, part, near, slope, copies):
     hs = []
     for j, z in enumerate(products(agg, weights)):
         act, bend = activate(z)
         slope[block(j), :] = bend
         hs.append((feats[block(j), :].astype(F32) + act).astype(BF))
-        hidden[block(j), :] = hs[j]
         near[block(j), :] = hs[j]
     mixed = [dot(local[block(j), :], h) for j, h in enumerate(hs)]
     for j, term in enumerate(mixed):
@@ -173,6 +176,12 @@
         for i in range(reps // 2):
             got = dot(agg[side * (reps // 2) + i], wide, ((0,), (0,)))
             target[i * cols : (i + 1) * cols, :] = got.astype(target.dtype)
+
+
+def two_grad_body(types, core, agg, dz, near_one, near_two, keep, send, h_one, h_two):
+    h_one[...] = near_one[...]
+    h_two[...] = near_two[...]
+    write_grad(types, core, agg, dz, keep, send)
 
 
 def back_body(types, core, parts, local, grad, slope, agg, keep, send, dz):
@@ -331,19 +340,22 @@
         pick, landed, wide, base
     )
     agg_one = across(copies)
-    h_one, near, slope, copies = call(
-        one_body, "one", [VMEM] * 5, [(flat, BF)] * 2 + [(flat, F32), (copied, BF)]
+    near_one, slope, copies = call(
+        one_body, "one", [VMEM] * 5, [(flat, BF), (flat, F32), (copied, BF)]
     )(agg_one, pick_one, feats, local_val, part)
     agg_two = across(copies)
-    h_two, dz_two, back = call(
+    near_two, dz_two, back = call(
         two_body, "two", [VMEM] * 4, [(flat, BF), (flat, BF), (copied, BF)]
-    )(agg_two, pick_two, near, grad_out)
+    )(agg_two, pick_two, near_one, grad_out)
     back = across(back)
 
     half = (width // 2, experts * cols)
-    keep_two, send_two = call(
-        write_grad, "grad_two", [SMEM] * 2 + [VMEM] * 2, [(half, F32), (half, BF)]
-    )(types, core, agg_two, dz_two)
+    keep_two, send_two, h_one, h_two = call(
+        two_grad_body,
+        "grad_two",
+        [SMEM] * 2 + [VMEM] * 4,
+        [(half, F32), (half, BF), (flat, BF), (flat, BF)],
+    )(types, core, agg_two, dz_two, near_one, near_two)
     keep_one, send_one = call(
         back_body,
         "back",

time: 150 us -> 150 us (level)
  no operation moved by 1% of the time
where the time goes in v11:
time: 150 us; the launch traced here: 149 us
  blocking collectives  82.6 us (55%)
  starting transfers between devices  37.5 us (25%)
  Pallas kernels  15.8 us (11%)
  waiting for transfers between devices  7.41 us (5%)
  local copies, waits for them, and re-layouts  3.41 us (2%)
    all_to_all x3, blocking collectives, exchange(): lax.all_to_all(blocks, 'dom', split_axis=0, concat_axis=0, axis_index_gro...  62.2 us
    all_to_all x2, blocking collectives, across(): lax.all_to_all(blocks, 'rep', split_axis=0, concat_axis=0, tiled=True)  20.4 us
    all_to_all x1, starting transfers between devices, shards(): lax.all_to_all(rows_out, 'dom', split_axis=0, concat_axis=0, tiled=True)  18.4 us
    ppermute x3, starting transfers between devices, swap(): return lax.ppermute(rows, 'dom', [(p, p ^ 1) for p in range(128)])  15.6 us
    all_to_all x1, waiting for transfers between devices, shards(): lax.all_to_all(rows_out, 'dom', split_axis=0, concat_axis=0, tiled=True)  6.26 us
    pallas_call x1, Pallas kernels, shards(): call(choose_body, 'choose', [SMEM] + [FAR] * 2, [(chosen, BF)] * 2, [pltp...  3.68 us
    all_to_all x1, starting transfers between devices, across(): lax.all_to_all(blocks, 'rep', split_axis=0, concat_axis=0, tiled=True)  3.47 us
    unnamed x22, local copies, waits for them, and re-layouts  3.41 us
  transfers between devices with their start and end apart: 5, of which 3 were waited for; matrix products, arithmetic and copies ran while one was open for 1% of the time, Pallas kernels for 6%

profile of v11, /device:TPU:1, one launch (start us, length us, event | category | flops | bytes accessed | tf_op | source)
XLA Modules:
  0.0 149.0 jit_solution(12466727127385447298)
XLA Ops:
  0.6 2.3 %pick.1 = bf16[128,8,128]{2,1,0:T(8,128)(2,1)} custom-call(s32[4,128]{1,0:T(4,128)} %bitcast.21, bf16[512,128]{1,0:T(8,128)(2,1)} %feats.3, bf16[512,128]{1,0:T(8,128)(2,1)} %hist_far.1), custom_call_target="tpu_custom_call" | custom-call | tf_op jit(solution)/shard_map/pick/pallas_call | solution.py:306
  2.9 18.4 %all-to-all-start = ((bf16[128,8,128]{2,1,0:T(8,128)(2,1)}), bf16[128,8,128]{2,1,0:T(8,128)(2,1)S(1)}, u32[]{:S(2)}, u32[]{:S(2)}) async-start(bf16[128,8,128]{2,1,0:T(8,128)(2,1)} %pick.1), calls=%async_computation | async-start | bytes 524288 | tf_op jit(solution)/shard_map/all_to_all | solution.py:319
  21.4 0.9 copy-done
  22.3 0.9 copy-done.2
  23.2 0.9 copy-done.7
  24.1 0.7 copy-done.9
  24.8 0.9 ready.1
  25.6 3.7 %choose.1 = (bf16[4,512,128]{2,1,0:T(8,128)(2,1)}, bf16[4,512,128]{2,1,0:T(8,128)(2,1)}) custom-call(s32[4]{0:T(128)} %bitcast.12, bf16[512,8,128]{2,1,0:T(8,128)(2,1)} %w_one_far.1, bf16[512,8,128]{2,1,0:T(8,128)(2,1)} %w_two_far.1), custom_call_target="tpu_custom_call" | custom-call | tf_op jit(solution)/shard_map/choose/pallas_call | solution.py:323
  29.4 6.3 %all-to-all-done = bf16[128,8,128]{2,1,0:T(8,128)(2,1)S(1)} async-done(((bf16[128,8,128]{2,1,0:T(8,128)(2,1)}), bf16[128,8,128]{2,1,0:T(8,128)(2,1)S(1)}, u32[]{:S(2)}, u32[]{:S(2)}) %all-to-all-start) | async-done | bytes 262176 | tf_op jit(solution)/shard_map/all_to_all | solution.py:319
  35.6 0.8 gather.1
  36.5 11.1 %all_to_all.35.agg = bf16[4,512,128]{2,1,0:T(8,128)(2,1)S(1)} all-to-all(bf16[4,512,128]{2,1,0:T(8,128)(2,1)S(1)} %get-tuple-element.36), channel_id=1, replica_groups=mesh['dom'=128,'rep'=4] {'rep'}, dimensions={0} | all-to-all | bytes 1048576 | tf_op jit(solution)/shard_map/all_to_all | solution.py:286
  47.6 0.4 one.1
  48.0 9.3 %all_to_all.36.agg = bf16[4,512,128]{2,1,0:T(8,128)(2,1)S(1)} all-to-all(bf16[4,512,128]{2,1,0:T(8,128)(2,1)S(1)} %get-tuple-element.39), channel_id=1, replica_groups=mesh['dom'=128,'rep'=4] {'rep'}, dimensions={0} | all-to-all | bytes 1048576 | tf_op jit(solution)/shard_map/all_to_all | solution.py:286
  57.4 1.2 two.1
  58.6 3.5 %all-to-all-start.3 = ((bf16[4,512,128]{2,1,0:T(8,128)(2,1)}), bf16[4,512,128]{2,1,0:T(8,128)(2,1)S(1)}, u32[]{:S(2)}, u32[]{:S(2)}) async-start(bf16[4,512,128]{2,1,0:T(8,128)(2,1)} %get-tuple-element.46), calls=%async_computation.3 | async-start | bytes 1048576 | tf_op jit(solution)/shard_map/all_to_all | solution.py:286
  62.1 1.9 %grad_two.1 = (f32[256,1024]{1,0:T(8,128)S(1)}, bf16[256,1024]{1,0:T(8,128)(2,1)}, bf16[512,128]{1,0:T(8,128)(2,1)}, bf16[512,128]{1,0:T(8,128)(2,1)}) custom-call(s32[4]{0:T(128)S(1)} %bitcast.13, s32[1]{0:T(128)} %bitcast.1.core, bf16[4,512,128]{2,1,0:T(8,128)(2,1)S(1)} %all_to_all.36.agg, bf16[512,128]{1,0:T(8,128)(2,1)S(1)} %get-tuple-element.42.dz, ...), custom_call_target="tpu_custom_call" | custom-call | tf_op jit(solution)/shard_map/grad_two/pallas_call | solution.py:353
  64.0 6.3 %collective-permute-start.1 = (bf16[256,1024]{1,0:T(8,128)(2,1)}, bf16[256,1024]{1,0:T(8,128)(2,1)}, u32[]{:S(2)}, u32[]{:S(2)}) collective-permute-start(bf16[256,1024]{1,0:T(8,128)(2,1)} %get-tuple-element.51), channel_id=1, source_target_pairs={{0,4},{4,0},{8,12},{12,8},{16,20},{20,16},{24,28},{28,24},{32,36},... | collective-permute-start | bytes 1572872 | tf_op jit(solution)/shard_map/ppermute | solution.py:290
  70.4 1.5 back.1
  71.9 6.1 %collective-permute-start = (bf16[256,1024]{1,0:T(8,128)(2,1)S(1)}, bf16[256,1024]{1,0:T(8,128)(2,1)S(1)}, u32[]{:S(2)}, u32[]{:S(2)}) collective-permute-start(bf16[256,1024]{1,0:T(8,128)(2,1)S(1)} %get-tuple-element.49), channel_id=1, source_target_pairs={{0,4},{4,0},{8,12},{12,8},{16,20},{20,16},{24,28},{28,24},{32,36},... | collective-permute-start | bytes 1572872 | tf_op jit(solution)/shard_map/ppermute | solution.py:290
  78.0 1.2 add_convert_fusion
  79.2 0.3 collective-permute-done
  79.5 0.1 add_convert_fusion.1
  79.6 0.1 pad_maximum_fusion
  79.7 25.5 %all_to_all.37.parts = bf16[16,32,1024]{2,1,0:T(8,128)(2,1)S(1)} all-to-all(bf16[16,32,1024]{2,1,0:T(8,128)(2,1)S(1)} %pad_maximum_fusion), channel_id=1, replica_groups={{0,64,128,192,256,320,384,448,8,72,136,200,264,328,392,456},{16,80,144,..., dimensions={0} | all-to-all | bytes 2097152 | tf_op jit(solution)/shard_map/all_to_all | solution.py:280
  105.2 0.1 first_sum.1
  105.3 11.6 %all_to_all.38.parts = bf16[4,32,1024]{2,1,0:T(8,128)(2,1)S(1)} all-to-all(bf16[4,32,1024]{2,1,0:T(8,128)(2,1)S(1)} %first_sum.1), channel_id=1, replica_groups={{0,16,32,48},{8,24,40,56},{64,80,96,112},{72,88,104,120},{128,144,160,1..., dimensions={0} | all-to-all | bytes 524288 | tf_op jit(solution)/shard_map/all_to_all | solution.py:280
  117.0 0.2 second_sum.1
  117.2 25.1 %all_to_all.39.half = bf16[16,256,128]{2,1,0:T(8,128)(2,1)S(1)} all-to-all(bf16[16,256,128]{2,1,0:T(8,128)(2,1)S(1)} %second_sum.1), channel_id=1, replica_groups={{0,64,128,192,256,320,384,448,8,72,136,200,264,328,392,456},{16,80,144,..., dimensions={0} | all-to-all | bytes 2097152 | tf_op jit(solution)/shard_map/all_to_all | solution.py:280
  142.2 3.1 %collective-permute-start.2 = (bf16[16,256,128]{2,1,0:T(8,128)(2,1)S(1)}, bf16[16,256,128]{2,1,0:T(8,128)(2,1)S(1)}, u32[]{:S(2)}, u32[]{:S(2)}) collective-permute-start(bf16[16,256,128]{2,1,0:T(8,128)(2,1)S(1)} %all_to_all.39.half), channel_id=1, source_target_pairs={{0,4},{4,0},{8,12},{12,8},{16,20},{20,16},{24,28},{28,24},{32,36},... | collective-permute-start | bytes 3145736 | tf_op jit(solution)/shard_map/ppermute | solution.py:290
  145.4 1.4 widen_own.1
  146.8 0.8 collective-permute-done.2.half
  147.7 1.4 widen_other.1
  (20 shorter events, 0.1 us)
Async XLA Ops:
  0.6 35.0 %copy-start.10 = (s32[1,4]{1,0:T(1,128)S(1)}, s32[1,4]{1,0:T(1,128)}, u32[]{:S(2)}) copy-start(s32[1,4]{1,0:T(1,128)} %param.15) | copy-start | bytes 52
  2.9 32.7 %all-to-all-start = ((bf16[128,8,128]{2,1,0:T(8,128)(2,1)}), bf16[128,8,128]{2,1,0:T(8,128)(2,1)S(1)}, u32[]{:S(2)}, u32[]{:S(2)}) async-start(bf16[128,8,128]{2,1,0:T(8,128)(2,1)} %pick.1), calls=%async_computation | async-start | bytes 524288 | tf_op jit(solution)/shard_map/all_to_all | solution.py:319
  21.4 0.9 copy-start
  22.3 0.9 copy-start.2
  23.2 0.9 copy-start.7
  24.1 0.7 copy-start.9
  25.6 21.9 %copy-start.1 = (bf16[512,128]{1,0:T(8,128)(2,1)S(1)}, bf16[512,128]{1,0:T(8,128)(2,1)}, u32[]{:S(2)}) copy-start(bf16[512,128]{1,0:T(8,128)(2,1)} %feats.3) | copy-start | bytes 393220
  25.6 21.9 %copy-start.3 = (bf16[512,128]{1,0:T(8,128)(2,1)S(1)}, bf16[512,128]{1,0:T(8,128)(2,1)}, u32[]{:S(2)}) copy-start(bf16[512,128]{1,0:T(8,128)(2,1)} %local.5) | copy-start | bytes 393220
  29.3 18.2 %copy-start.4 = (bf16[4,512,128]{2,1,0:T(8,128)(2,1)S(1)}, bf16[4,512,128]{2,1,0:T(8,128)(2,1)}, u32[]{:S(2)}) copy-start(bf16[4,512,128]{2,1,0:T(8,128)(2,1)} %get-tuple-element.37.weights) | copy-start | bytes 1572868
  36.4 20.9 %copy-start.5 = (bf16[4,512,128]{2,1,0:T(8,128)(2,1)S(1)}, bf16[4,512,128]{2,1,0:T(8,128)(2,1)}, u32[]{:S(2)}) copy-start(bf16[4,512,128]{2,1,0:T(8,128)(2,1)} %get-tuple-element.40.weights) | copy-start | bytes 1572868
  36.5 20.9 %copy-start.6 = (bf16[512,128]{1,0:T(8,128)(2,1)S(1)}, bf16[512,128]{1,0:T(8,128)(2,1)}, u32[]{:S(2)}) copy-start(bf16[512,128]{1,0:T(8,128)(2,1)} %grad.3) | copy-start | bytes 393220
  48.0 14.1 %copy-start.8 = (s32[1,4]{1,0:T(1,128)S(1)}, s32[1,4]{1,0:T(1,128)}, u32[]{:S(2)}) copy-start(s32[1,4]{1,0:T(1,128)} %param.16) | copy-start | bytes 52
  58.6 11.8 %all-to-all-start.3 = ((bf16[4,512,128]{2,1,0:T(8,128)(2,1)}), bf16[4,512,128]{2,1,0:T(8,128)(2,1)S(1)}, u32[]{:S(2)}, u32[]{:S(2)}) async-start(bf16[4,512,128]{2,1,0:T(8,128)(2,1)} %get-tuple-element.46), calls=%async_computation.3 | async-start | bytes 1048576 | tf_op jit(solution)/shard_map/all_to_all | solution.py:286
  64.0 14.0 %collective-permute-start.1 = (bf16[256,1024]{1,0:T(8,128)(2,1)}, bf16[256,1024]{1,0:T(8,128)(2,1)}, u32[]{:S(2)}, u32[]{:S(2)}) collective-permute-start(bf16[256,1024]{1,0:T(8,128)(2,1)} %get-tuple-element.51), channel_id=1, source_target_pairs={{0,4},{4,0},{8,12},{12,8},{16,20},{20,16},{24,28},{28,24},{32,36},... | collective-permute-start | bytes 1572872 | tf_op jit(solution)/shard_map/ppermute | solution.py:290
  71.9 7.6 %collective-permute-start = (bf16[256,1024]{1,0:T(8,128)(2,1)S(1)}, bf16[256,1024]{1,0:T(8,128)(2,1)S(1)}, u32[]{:S(2)}, u32[]{:S(2)}) collective-permute-start(bf16[256,1024]{1,0:T(8,128)(2,1)S(1)} %get-tuple-element.49), channel_id=1, source_target_pairs={{0,4},{4,0},{8,12},{12,8},{16,20},{20,16},{24,28},{28,24},{32,36},... | collective-permute-start | bytes 1572872 | tf_op jit(solution)/shard_map/ppermute | solution.py:290
  142.2 5.4 %collective-permute-start.2 = (bf16[16,256,128]{2,1,0:T(8,128)(2,1)S(1)}, bf16[16,256,128]{2,1,0:T(8,128)(2,1)S(1)}, u32[]{:S(2)}, u32[]{:S(2)}) collective-permute-start(bf16[16,256,128]{2,1,0:T(8,128)(2,1)S(1)} %all_to_all.39.half), channel_id=1, source_target_pairs={{0,4},{4,0},{8,12},{12,8},{16,20},{20,16},{24,28},{28,24},{32,36},... | collective-permute-start | bytes 3145736 | tf_op jit(solution)/shard_map/ppermute | solution.py:290

commit v12 on v11

--- a/solution.py
+++ b/solution.py
@@ -161,27 +161,34 @@
             back[q, block(j), :] = term[:, q * cols : (q + 1) * cols]
 
 
-def write_grad(types, core, agg, dz, keep, send):
-    reps, _, cols = agg.shape
+def write_grad(types, core, agg, dz, keep, send, dims):
+    reps = agg.shape[0]
+    cols = dz.shape[1]
     rows = types.shape[0]
+    zero = jnp.zeros((TILE, cols), BF)
     experts = keep.shape[1] // cols
     wide = []
     for e in range(experts):
         part = []
         for j in range(rows):
-            part.append((dz[block(j), :].astype(F32) * (types[j] == e).astype(F32)).astype(BF))
+            part.append(lax.select(types[j] == e, dz[block(j), :], zero))
         wide.append(jnp.concatenate(part, axis=0))
     wide = jnp.concatenate(wide, axis=1)
     for target, side in ((send, 1 - core[0]), (keep, core[0])):
         for i in range(reps // 2):
-            got = dot(agg[side * (reps // 2) + i], wide, ((0,), (0,)))
+            got = dot(agg[side * (reps // 2) + i], wide, dims)
             target[i * cols : (i + 1) * cols, :] = got.astype(target.dtype)
 
 
 def two_grad_body(types, core, agg, dz, near_one, near_two, keep, send, h_one, h_two):
     h_one[...] = near_one[...]
     h_two[...] = near_two[...]
-    write_grad(types, core, agg, dz, keep, send)
+    write_grad(types, core, agg, dz, keep, send, ((0,), (0,)))
+
+
+def turn_body(agg, turned):
+    for q in range(agg.shape[0]):
+        turned[q] = jnp.transpose(agg[q])
 
 
 def back_body(types, core, parts, local, grad, slope, agg, keep, send, dz):
@@ -196,7 +203,7 @@
     for j in rows:
         dh = grad[block(j), :].astype(F32) + terms[j]
         dz[block(j), :] = (dh * slope[block(j), :]).astype(BF)
-    write_grad(types, core, agg, dz, keep, send)
+    write_grad(types, core, agg, dz, keep, send, ((1,), (0,)))
 
 
 def add_up(parts):
@@ -356,13 +363,15 @@
         [SMEM] * 2 + [VMEM] * 4,
         [(half, F32), (half, BF), (flat, BF), (flat, BF)],
     )(types, core, agg_two, dz_two, near_one, near_two)
+    agg_one, keep_two = lax.optimization_barrier((agg_one, keep_two))
+    (turned,) = call(turn_body, "turn", [VMEM], [((REPS, cols, nodes), BF)])(agg_one)
     keep_one, send_one = call(
         back_body,
         "back",
         [SMEM] * 2 + [VMEM] * 5,
         [(half, F32), (half, BF)],
         [pltpu.VMEM(flat, BF)],
-    )(types, core, back, local_val, grad_out, slope, agg_one)
+    )(types, core, back, local_val, grad_out, slope, turned)
     pair_one = (keep_one + swap(send_one).astype(F32)).astype(BF)
     pair_two = (keep_two + swap(send_two).astype(F32)).astype(BF)
 

time: 150 us -> 150 us (level)
  no operation moved by 1% of the time
where the time goes in v12:
time: 150 us; the launch traced here: 149 us
  blocking collectives  82.6 us (55%)
  starting transfers between devices  37.3 us (25%)
  Pallas kernels  16.1 us (11%)
  waiting for transfers between devices  7.41 us (5%)
  local copies, waits for them, and re-layouts  3.41 us (2%)
    all_to_all x3, blocking collectives, exchange(): lax.all_to_all(blocks, 'dom', split_axis=0, concat_axis=0, axis_index_gro...  62.2 us
    all_to_all x2, blocking collectives, across(): lax.all_to_all(blocks, 'rep', split_axis=0, concat_axis=0, tiled=True)  20.4 us
    all_to_all x1, starting transfers between devices, shards(): lax.all_to_all(rows_out, 'dom', split_axis=0, concat_axis=0, tiled=True)  18.4 us
    ppermute x3, starting transfers between devices, swap(): return lax.ppermute(rows, 'dom', [(p, p ^ 1) for p in range(128)])  15.4 us
    all_to_all x1, waiting for transfers between devices, shards(): lax.all_to_all(rows_out, 'dom', split_axis=0, concat_axis=0, tiled=True)  6.26 us
    pallas_call x1, Pallas kernels, shards(): call(choose_body, 'choose', [SMEM] + [FAR] * 2, [(chosen, BF)] * 2, [pltp...  3.68 us
    all_to_all x1, starting transfers between devices, across(): lax.all_to_all(blocks, 'rep', split_axis=0, concat_axis=0, tiled=True)  3.47 us
    unnamed x22, local copies, waits for them, and re-layouts  3.41 us
  transfers between devices with their start and end apart: 5, of which 3 were waited for; matrix products, arithmetic and copies ran while one was open for 1% of the time, Pallas kernels for 6%

profile of v12, /device:TPU:1, one launch (start us, length us, event | category | flops | bytes accessed | tf_op | source)
XLA Modules:
  0.0 149.1 jit_solution(15265640789248788799)
XLA Ops:
  0.6 2.3 %pick.1 = bf16[128,8,128]{2,1,0:T(8,128)(2,1)} custom-call(s32[4,128]{1,0:T(4,128)} %bitcast.21, bf16[512,128]{1,0:T(8,128)(2,1)} %feats.3, bf16[512,128]{1,0:T(8,128)(2,1)} %hist_far.1), custom_call_target="tpu_custom_call" | custom-call | tf_op jit(solution)/shard_map/pick/pallas_call | solution.py:313
  2.9 18.4 %all-to-all-start = ((bf16[128,8,128]{2,1,0:T(8,128)(2,1)}), bf16[128,8,128]{2,1,0:T(8,128)(2,1)S(1)}, u32[]{:S(2)}, u32[]{:S(2)}) async-start(bf16[128,8,128]{2,1,0:T(8,128)(2,1)} %pick.1), calls=%async_computation | async-start | bytes 524288 | tf_op jit(solution)/shard_map/all_to_all | solution.py:326
  21.4 0.9 copy-done
  22.3 0.9 copy-done.2
  23.2 0.9 copy-done.7
  24.1 0.7 copy-done.9
  24.8 0.9 ready.1
  25.6 3.7 %choose.1 = (bf16[4,512,128]{2,1,0:T(8,128)(2,1)}, bf16[4,512,128]{2,1,0:T(8,128)(2,1)}) custom-call(s32[4]{0:T(128)} %bitcast.12, bf16[512,8,128]{2,1,0:T(8,128)(2,1)} %w_one_far.1, bf16[512,8,128]{2,1,0:T(8,128)(2,1)} %w_two_far.1), custom_call_target="tpu_custom_call" | custom-call | tf_op jit(solution)/shard_map/choose/pallas_call | solution.py:330
  29.4 6.3 %all-to-all-done = bf16[128,8,128]{2,1,0:T(8,128)(2,1)S(1)} async-done(((bf16[128,8,128]{2,1,0:T(8,128)(2,1)}), bf16[128,8,128]{2,1,0:T(8,128)(2,1)S(1)}, u32[]{:S(2)}, u32[]{:S(2)}) %all-to-all-start) | async-done | bytes 262176 | tf_op jit(solution)/shard_map/all_to_all | solution.py:326
  35.6 0.8 gather.1
  36.5 11.1 %all_to_all.35.agg = bf16[4,512,128]{2,1,0:T(8,128)(2,1)S(1)} all-to-all(bf16[4,512,128]{2,1,0:T(8,128)(2,1)S(1)} %get-tuple-element.38), channel_id=1, replica_groups=mesh['dom'=128,'rep'=4] {'rep'}, dimensions={0} | all-to-all | bytes 1048576 | tf_op jit(solution)/shard_map/all_to_all | solution.py:293
  47.6 0.4 one.1
  48.0 9.3 %all_to_all.36.agg = bf16[4,512,128]{2,1,0:T(8,128)(2,1)S(1)} all-to-all(bf16[4,512,128]{2,1,0:T(8,128)(2,1)S(1)} %get-tuple-element.41), channel_id=1, replica_groups=mesh['dom'=128,'rep'=4] {'rep'}, dimensions={0} | all-to-all | bytes 1048576 | tf_op jit(solution)/shard_map/all_to_all | solution.py:293
  57.4 1.2 two.1
  58.6 3.5 %all-to-all-start.3 = ((bf16[4,512,128]{2,1,0:T(8,128)(2,1)}), bf16[4,512,128]{2,1,0:T(8,128)(2,1)S(1)}, u32[]{:S(2)}, u32[]{:S(2)}) async-start(bf16[4,512,128]{2,1,0:T(8,128)(2,1)} %get-tuple-element.48), calls=%async_computation.3 | async-start | bytes 1048576 | tf_op jit(solution)/shard_map/all_to_all | solution.py:293
  62.1 1.9 %grad_two.1 = (f32[256,1024]{1,0:T(8,128)S(1)}, bf16[256,1024]{1,0:T(8,128)(2,1)}, bf16[512,128]{1,0:T(8,128)(2,1)}, bf16[512,128]{1,0:T(8,128)(2,1)}) custom-call(s32[4]{0:T(128)S(1)} %bitcast.13, s32[1]{0:T(128)} %bitcast.1.core, bf16[4,512,128]{2,1,0:T(8,128)(2,1)S(1)} %all_to_all.36.agg, bf16[512,128]{1,0:T(8,128)(2,1)S(1)} %get-tuple-element.44.dz, ...), custom_call_target="tpu_custom_call" | custom-call | tf_op jit(solution)/shard_map/grad_two/pallas_call | solution.py:360
  64.0 6.3 %collective-permute-start.1 = (bf16[256,1024]{1,0:T(8,128)(2,1)}, bf16[256,1024]{1,0:T(8,128)(2,1)}, u32[]{:S(2)}, u32[]{:S(2)}) collective-permute-start(bf16[256,1024]{1,0:T(8,128)(2,1)} %get-tuple-element.55), channel_id=1, source_target_pairs={{0,4},{4,0},{8,12},{12,8},{16,20},{20,16},{24,28},{28,24},{32,36},... | collective-permute-start | bytes 1572872 | tf_op jit(solution)/shard_map/ppermute | solution.py:297
  70.4 0.2 turn.1.agg
  70.6 1.5 %back.1 = (f32[256,1024]{1,0:T(8,128)S(1)}, bf16[256,1024]{1,0:T(8,128)(2,1)S(1)}) custom-call(s32[4]{0:T(128)S(1)} %bitcast.14, s32[1]{0:T(128)} %bitcast.1.core, bf16[4,512,128]{2,1,0:T(8,128)(2,1)S(1)} %all-to-all-done.3.parts, bf16[512,128]{1,0:T(8,128)(2,1)S(1)} %copy-done.3, bf16[512,128]{1,0:T(8,128)(2,1)S(1)} %copy-done.6, ...), custom_call_target="tpu_custom_call" | custom-call | tf_op jit(solution)/shard_map/back/pallas_call | solution.py:368
  72.1 5.9 %collective-permute-start = (bf16[256,1024]{1,0:T(8,128)(2,1)S(1)}, bf16[256,1024]{1,0:T(8,128)(2,1)S(1)}, u32[]{:S(2)}, u32[]{:S(2)}) collective-permute-start(bf16[256,1024]{1,0:T(8,128)(2,1)S(1)} %get-tuple-element.53), channel_id=1, source_target_pairs={{0,4},{4,0},{8,12},{12,8},{16,20},{20,16},{24,28},{28,24},{32,36},... | collective-permute-start | bytes 1572872 | tf_op jit(solution)/shard_map/ppermute | solution.py:297
  78.0 1.2 add_convert_fusion
  79.2 0.3 collective-permute-done
  79.5 0.1 add_convert_fusion.1
  79.8 25.4 %all_to_all.37.parts = bf16[16,32,1024]{2,1,0:T(8,128)(2,1)S(1)} all-to-all(bf16[16,32,1024]{2,1,0:T(8,128)(2,1)S(1)} %pad_maximum_fusion), channel_id=1, replica_groups={{0,64,128,192,256,320,384,448,8,72,136,200,264,328,392,456},{16,80,144,..., dimensions={0} | all-to-all | bytes 2097152 | tf_op jit(solution)/shard_map/all_to_all | solution.py:287
  105.2 0.1 first_sum.1
  105.3 11.6 %all_to_all.38.parts = bf16[4,32,1024]{2,1,0:T(8,128)(2,1)S(1)} all-to-all(bf16[4,32,1024]{2,1,0:T(8,128)(2,1)S(1)} %first_sum.1), channel_id=1, replica_groups={{0,16,32,48},{8,24,40,56},{64,80,96,112},{72,88,104,120},{128,144,160,1..., dimensions={0} | all-to-all | bytes 524288 | tf_op jit(solution)/shard_map/all_to_all | solution.py:287
  117.0 0.2 second_sum.1
  117.2 25.1 %all_to_all.39.half = bf16[16,256,128]{2,1,0:T(8,128)(2,1)S(1)} all-to-all(bf16[16,256,128]{2,1,0:T(8,128)(2,1)S(1)} %second_sum.1), channel_id=1, replica_groups={{0,64,128,192,256,320,384,448,8,72,136,200,264,328,392,456},{16,80,144,..., dimensions={0} | all-to-all | bytes 2097152 | tf_op jit(solution)/shard_map/all_to_all | solution.py:287
  142.3 3.1 %collective-permute-start.2 = (bf16[16,256,128]{2,1,0:T(8,128)(2,1)S(1)}, bf16[16,256,128]{2,1,0:T(8,128)(2,1)S(1)}, u32[]{:S(2)}, u32[]{:S(2)}) collective-permute-start(bf16[16,256,128]{2,1,0:T(8,128)(2,1)S(1)} %all_to_all.39.half), channel_id=1, source_target_pairs={{0,4},{4,0},{8,12},{12,8},{16,20},{20,16},{24,28},{28,24},{32,36},... | collective-permute-start | bytes 3145736 | tf_op jit(solution)/shard_map/ppermute | solution.py:297
  145.4 1.4 widen_own.1
  146.8 0.8 collective-permute-done.2.half
  147.7 1.4 widen_other.1
  (21 shorter events, 0.1 us)
Async XLA Ops:
  0.6 35.0 %copy-start.10 = (s32[1,4]{1,0:T(1,128)S(1)}, s32[1,4]{1,0:T(1,128)}, u32[]{:S(2)}) copy-start(s32[1,4]{1,0:T(1,128)} %param.15) | copy-start | bytes 52
  2.9 32.7 %all-to-all-start = ((bf16[128,8,128]{2,1,0:T(8,128)(2,1)}), bf16[128,8,128]{2,1,0:T(8,128)(2,1)S(1)}, u32[]{:S(2)}, u32[]{:S(2)}) async-start(bf16[128,8,128]{2,1,0:T(8,128)(2,1)} %pick.1), calls=%async_computation | async-start | bytes 524288 | tf_op jit(solution)/shard_map/all_to_all | solution.py:326
  21.4 0.9 copy-start
  22.3 0.9 copy-start.2
  23.2 0.9 copy-start.7
  24.1 0.7 copy-start.9
  25.6 21.9 %copy-start.1 = (bf16[512,128]{1,0:T(8,128)(2,1)S(1)}, bf16[512,128]{1,0:T(8,128)(2,1)}, u32[]{:S(2)}) copy-start(bf16[512,128]{1,0:T(8,128)(2,1)} %feats.3) | copy-start | bytes 393220
  25.6 21.9 %copy-start.3 = (bf16[512,128]{1,0:T(8,128)(2,1)S(1)}, bf16[512,128]{1,0:T(8,128)(2,1)}, u32[]{:S(2)}) copy-start(bf16[512,128]{1,0:T(8,128)(2,1)} %local.5) | copy-start | bytes 393220
  29.3 18.2 %copy-start.4 = (bf16[4,512,128]{2,1,0:T(8,128)(2,1)S(1)}, bf16[4,512,128]{2,1,0:T(8,128)(2,1)}, u32[]{:S(2)}) copy-start(bf16[4,512,128]{2,1,0:T(8,128)(2,1)} %get-tuple-element.39.weights) | copy-start | bytes 1572868
  36.4 20.9 %copy-start.5 = (bf16[4,512,128]{2,1,0:T(8,128)(2,1)S(1)}, bf16[4,512,128]{2,1,0:T(8,128)(2,1)}, u32[]{:S(2)}) copy-start(bf16[4,512,128]{2,1,0:T(8,128)(2,1)} %get-tuple-element.42.weights) | copy-start | bytes 1572868
  36.5 20.9 %copy-start.6 = (bf16[512,128]{1,0:T(8,128)(2,1)S(1)}, bf16[512,128]{1,0:T(8,128)(2,1)}, u32[]{:S(2)}) copy-start(bf16[512,128]{1,0:T(8,128)(2,1)} %grad.3) | copy-start | bytes 393220
  48.0 14.1 %copy-start.8 = (s32[1,4]{1,0:T(1,128)S(1)}, s32[1,4]{1,0:T(1,128)}, u32[]{:S(2)}) copy-start(s32[1,4]{1,0:T(1,128)} %param.16) | copy-start | bytes 52
  58.6 11.9 %all-to-all-start.3 = ((bf16[4,512,128]{2,1,0:T(8,128)(2,1)}), bf16[4,512,128]{2,1,0:T(8,128)(2,1)S(1)}, u32[]{:S(2)}, u32[]{:S(2)}) async-start(bf16[4,512,128]{2,1,0:T(8,128)(2,1)} %get-tuple-element.48), calls=%async_computation.3 | async-start | bytes 1048576 | tf_op jit(solution)/shard_map/all_to_all | solution.py:293
  64.0 14.0 %collective-permute-start.1 = (bf16[256,1024]{1,0:T(8,128)(2,1)}, bf16[256,1024]{1,0:T(8,128)(2,1)}, u32[]{:S(2)}, u32[]{:S(2)}) collective-permute-start(bf16[256,1024]{1,0:T(8,128)(2,1)} %get-tuple-element.55), channel_id=1, source_target_pairs={{0,4},{4,0},{8,12},{12,8},{16,20},{20,16},{24,28},{28,24},{32,36},... | collective-permute-start | bytes 1572872 | tf_op jit(solution)/shard_map/ppermute | solution.py:297
  72.1 7.4 %collective-permute-start = (bf16[256,1024]{1,0:T(8,128)(2,1)S(1)}, bf16[256,1024]{1,0:T(8,128)(2,1)S(1)}, u32[]{:S(2)}, u32[]{:S(2)}) collective-permute-start(bf16[256,1024]{1,0:T(8,128)(2,1)S(1)} %get-tuple-element.53), channel_id=1, source_target_pairs={{0,4},{4,0},{8,12},{12,8},{16,20},{20,16},{24,28},{28,24},{32,36},... | collective-permute-start | bytes 1572872 | tf_op jit(solution)/shard_map/ppermute | solution.py:297
  142.3 5.4 %collective-permute-start.2 = (bf16[16,256,128]{2,1,0:T(8,128)(2,1)S(1)}, bf16[16,256,128]{2,1,0:T(8,128)(2,1)S(1)}, u32[]{:S(2)}, u32[]{:S(2)}) collective-permute-start(bf16[16,256,128]{2,1,0:T(8,128)(2,1)S(1)} %all_to_all.39.half), channel_id=1, source_target_pairs={{0,4},{4,0},{8,12},{12,8},{16,20},{20,16},{24,28},{28,24},{32,36},... | collective-permute-start | bytes 3145736 | tf_op jit(solution)/shard_map/ppermute | solution.py:297

commit v13 on v12

--- a/solution.py
+++ b/solution.py
@@ -174,10 +174,12 @@
             part.append(lax.select(types[j] == e, dz[block(j), :], zero))
         wide.append(jnp.concatenate(part, axis=0))
     wide = jnp.concatenate(wide, axis=1)
-    for target, side in ((send, 1 - core[0]), (keep, core[0])):
-        for i in range(reps // 2):
-            got = dot(agg[side * (reps // 2) + i], wide, dims)
-            target[i * cols : (i + 1) * cols, :] = got.astype(target.dtype)
+    sides = (1 - core[0], core[0])
+    order = [agg[side * (reps // 2) + i] for side in sides for i in range(reps // 2)]
+    got = dot(jnp.concatenate(order, axis=1 - dims[0][0]), wide, dims)
+    middle = send.shape[0]
+    send[...] = got[:middle].astype(send.dtype)
+    keep[...] = got[middle:]
 
 
 def two_grad_body(types, core, agg, dz, near_one, near_two, keep, send, h_one, h_two):

time: 150 us -> 150 us (level)
  no operation moved by 1% of the time
where the time goes in v13:
time: 150 us; the launch traced here: 149 us
  blocking collectives  82.6 us (55%)
  starting transfers between devices  37.1 us (25%)
  Pallas kernels  16.2 us (11%)
  waiting for transfers between devices  7.41 us (5%)
  local copies, waits for them, and re-layouts  3.41 us (2%)
    all_to_all x3, blocking collectives, exchange(): lax.all_to_all(blocks, 'dom', split_axis=0, concat_axis=0, axis_index_gro...  62.2 us
    all_to_all x2, blocking collectives, across(): lax.all_to_all(blocks, 'rep', split_axis=0, concat_axis=0, tiled=True)  20.4 us
    all_to_all x1, starting transfers between devices, shards(): lax.all_to_all(rows_out, 'dom', split_axis=0, concat_axis=0, tiled=True)  18.4 us
    ppermute x3, starting transfers between devices, swap(): return lax.ppermute(rows, 'dom', [(p, p ^ 1) for p in range(128)])  15.2 us
    all_to_all x1, waiting for transfers between devices, shards(): lax.all_to_all(rows_out, 'dom', split_axis=0, concat_axis=0, tiled=True)  6.26 us
    pallas_call x1, Pallas kernels, shards(): call(choose_body, 'choose', [SMEM] + [FAR] * 2, [(chosen, BF)] * 2, [pltp...  3.68 us
    all_to_all x1, starting transfers between devices, across(): lax.all_to_all(blocks, 'rep', split_axis=0, concat_axis=0, tiled=True)  3.47 us
    unnamed x22, local copies, waits for them, and re-layouts  3.41 us
  transfers between devices with their start and end apart: 5, of which 3 were waited for; matrix products, arithmetic and copies ran while one was open for 1% of the time, Pallas kernels for 6%

profile of v13, /device:TPU:1, one launch (start us, length us, event | category | flops | bytes accessed | tf_op | source)
XLA Modules:
  0.0 149.0 jit_solution(5558060349822418642)
XLA Ops:
  0.6 2.3 %pick.1 = bf16[128,8,128]{2,1,0:T(8,128)(2,1)} custom-call(s32[4,128]{1,0:T(4,128)} %bitcast.21, bf16[512,128]{1,0:T(8,128)(2,1)} %feats.3, bf16[512,128]{1,0:T(8,128)(2,1)} %hist_far.1), custom_call_target="tpu_custom_call" | custom-call | tf_op jit(solution)/shard_map/pick/pallas_call | solution.py:315
  2.9 18.4 %all-to-all-start = ((bf16[128,8,128]{2,1,0:T(8,128)(2,1)}), bf16[128,8,128]{2,1,0:T(8,128)(2,1)S(1)}, u32[]{:S(2)}, u32[]{:S(2)}) async-start(bf16[128,8,128]{2,1,0:T(8,128)(2,1)} %pick.1), calls=%async_computation | async-start | bytes 524288 | tf_op jit(solution)/shard_map/all_to_all | solution.py:328
  21.4 0.9 copy-done
  22.3 0.9 copy-done.2
  23.2 0.9 copy-done.7
  24.1 0.7 copy-done.9
  24.8 0.9 ready.1
  25.6 3.7 %choose.1 = (bf16[4,512,128]{2,1,0:T(8,128)(2,1)}, bf16[4,512,128]{2,1,0:T(8,128)(2,1)}) custom-call(s32[4]{0:T(128)} %bitcast.12, bf16[512,8,128]{2,1,0:T(8,128)(2,1)} %w_one_far.1, bf16[512,8,128]{2,1,0:T(8,128)(2,1)} %w_two_far.1), custom_call_target="tpu_custom_call" | custom-call | tf_op jit(solution)/shard_map/choose/pallas_call | solution.py:332
  29.4 6.3 %all-to-all-done = bf16[128,8,128]{2,1,0:T(8,128)(2,1)S(1)} async-done(((bf16[128,8,128]{2,1,0:T(8,128)(2,1)}), bf16[128,8,128]{2,1,0:T(8,128)(2,1)S(1)}, u32[]{:S(2)}, u32[]{:S(2)}) %all-to-all-start) | async-done | bytes 262176 | tf_op jit(solution)/shard_map/all_to_all | solution.py:328
  35.6 0.8 gather.1
  36.5 11.1 %all_to_all.35.agg = bf16[4,512,128]{2,1,0:T(8,128)(2,1)S(1)} all-to-all(bf16[4,512,128]{2,1,0:T(8,128)(2,1)S(1)} %get-tuple-element.38), channel_id=1, replica_groups=mesh['dom'=128,'rep'=4] {'rep'}, dimensions={0} | all-to-all | bytes 1048576 | tf_op jit(solution)/shard_map/all_to_all | solution.py:295
  47.6 0.4 one.1
  48.0 9.3 %all_to_all.36.agg = bf16[4,512,128]{2,1,0:T(8,128)(2,1)S(1)} all-to-all(bf16[4,512,128]{2,1,0:T(8,128)(2,1)S(1)} %get-tuple-element.41), channel_id=1, replica_groups=mesh['dom'=128,'rep'=4] {'rep'}, dimensions={0} | all-to-all | bytes 1048576 | tf_op jit(solution)/shard_map/all_to_all | solution.py:295
  57.4 1.2 two.1
  58.6 3.5 %all-to-all-start.3 = ((bf16[4,512,128]{2,1,0:T(8,128)(2,1)}), bf16[4,512,128]{2,1,0:T(8,128)(2,1)S(1)}, u32[]{:S(2)}, u32[]{:S(2)}) async-start(bf16[4,512,128]{2,1,0:T(8,128)(2,1)} %get-tuple-element.48), calls=%async_computation.3 | async-start | bytes 1048576 | tf_op jit(solution)/shard_map/all_to_all | solution.py:295
  62.1 2.1 %grad_two.1 = (f32[256,1024]{1,0:T(8,128)S(1)}, bf16[256,1024]{1,0:T(8,128)(2,1)}, bf16[512,128]{1,0:T(8,128)(2,1)}, bf16[512,128]{1,0:T(8,128)(2,1)}) custom-call(s32[4]{0:T(128)S(1)} %bitcast.13, s32[1]{0:T(128)} %bitcast.1.core, bf16[4,512,128]{2,1,0:T(8,128)(2,1)S(1)} %all_to_all.36.agg, bf16[512,128]{1,0:T(8,128)(2,1)S(1)} %get-tuple-element.44.dz, ...), custom_call_target="tpu_custom_call" | custom-call | tf_op jit(solution)/shard_map/grad_two/pallas_call | solution.py:362
  64.2 6.3 %collective-permute-start.1 = (bf16[256,1024]{1,0:T(8,128)(2,1)}, bf16[256,1024]{1,0:T(8,128)(2,1)}, u32[]{:S(2)}, u32[]{:S(2)}) collective-permute-start(bf16[256,1024]{1,0:T(8,128)(2,1)} %get-tuple-element.55), channel_id=1, source_target_pairs={{0,4},{4,0},{8,12},{12,8},{16,20},{20,16},{24,28},{28,24},{32,36},... | collective-permute-start | bytes 1572872 | tf_op jit(solution)/shard_map/ppermute | solution.py:299
  70.5 0.2 turn.1.agg
  70.7 1.5 back.1
  72.2 5.8 %collective-permute-start = (bf16[256,1024]{1,0:T(8,128)(2,1)S(1)}, bf16[256,1024]{1,0:T(8,128)(2,1)S(1)}, u32[]{:S(2)}, u32[]{:S(2)}) collective-permute-start(bf16[256,1024]{1,0:T(8,128)(2,1)S(1)} %get-tuple-element.53), channel_id=1, source_target_pairs={{0,4},{4,0},{8,12},{12,8},{16,20},{20,16},{24,28},{28,24},{32,36},... | collective-permute-start | bytes 1572872 | tf_op jit(solution)/shard_map/ppermute | solution.py:299
  78.0 1.2 add_convert_fusion
  79.2 0.3 collective-permute-done
  79.5 0.1 add_convert_fusion.1
  79.7 25.4 %all_to_all.37.parts = bf16[16,32,1024]{2,1,0:T(8,128)(2,1)S(1)} all-to-all(bf16[16,32,1024]{2,1,0:T(8,128)(2,1)S(1)} %pad_maximum_fusion), channel_id=1, replica_groups={{0,64,128,192,256,320,384,448,8,72,136,200,264,328,392,456},{16,80,144,..., dimensions={0} | all-to-all | bytes 2097152 | tf_op jit(solution)/shard_map/all_to_all | solution.py:289
  105.2 0.1 first_sum.1
  105.3 11.6 %all_to_all.38.parts = bf16[4,32,1024]{2,1,0:T(8,128)(2,1)S(1)} all-to-all(bf16[4,32,1024]{2,1,0:T(8,128)(2,1)S(1)} %first_sum.1), channel_id=1, replica_groups={{0,16,32,48},{8,24,40,56},{64,80,96,112},{72,88,104,120},{128,144,160,1..., dimensions={0} | all-to-all | bytes 524288 | tf_op jit(solution)/shard_map/all_to_all | solution.py:289
  116.9 0.2 second_sum.1
  117.1 25.1 %all_to_all.39.half = bf16[16,256,128]{2,1,0:T(8,128)(2,1)S(1)} all-to-all(bf16[16,256,128]{2,1,0:T(8,128)(2,1)S(1)} %second_sum.1), channel_id=1, replica_groups={{0,64,128,192,256,320,384,448,8,72,136,200,264,328,392,456},{16,80,144,..., dimensions={0} | all-to-all | bytes 2097152 | tf_op jit(solution)/shard_map/all_to_all | solution.py:289
  142.2 3.1 %collective-permute-start.2 = (bf16[16,256,128]{2,1,0:T(8,128)(2,1)S(1)}, bf16[16,256,128]{2,1,0:T(8,128)(2,1)S(1)}, u32[]{:S(2)}, u32[]{:S(2)}) collective-permute-start(bf16[16,256,128]{2,1,0:T(8,128)(2,1)S(1)} %all_to_all.39.half), channel_id=1, source_target_pairs={{0,4},{4,0},{8,12},{12,8},{16,20},{20,16},{24,28},{28,24},{32,36},... | collective-permute-start | bytes 3145736 | tf_op jit(solution)/shard_map/ppermute | solution.py:299
  145.4 1.4 widen_own.1
  146.8 0.8 collective-permute-done.2.half
  147.6 1.4 widen_other.1
  (21 shorter events, 0.1 us)
Async XLA Ops:
  0.6 35.0 %copy-start.10 = (s32[1,4]{1,0:T(1,128)S(1)}, s32[1,4]{1,0:T(1,128)}, u32[]{:S(2)}) copy-start(s32[1,4]{1,0:T(1,128)} %param.15) | copy-start | bytes 52
  2.9 32.7 %all-to-all-start = ((bf16[128,8,128]{2,1,0:T(8,128)(2,1)}), bf16[128,8,128]{2,1,0:T(8,128)(2,1)S(1)}, u32[]{:S(2)}, u32[]{:S(2)}) async-start(bf16[128,8,128]{2,1,0:T(8,128)(2,1)} %pick.1), calls=%async_computation | async-start | bytes 524288 | tf_op jit(solution)/shard_map/all_to_all | solution.py:328
  21.4 0.9 copy-start
  22.3 0.9 copy-start.2
  23.2 0.9 copy-start.7
  24.1 0.7 copy-start.9
  25.6 21.9 %copy-start.1 = (bf16[512,128]{1,0:T(8,128)(2,1)S(1)}, bf16[512,128]{1,0:T(8,128)(2,1)}, u32[]{:S(2)}) copy-start(bf16[512,128]{1,0:T(8,128)(2,1)} %feats.3) | copy-start | bytes 393220
  25.6 21.9 %copy-start.3 = (bf16[512,128]{1,0:T(8,128)(2,1)S(1)}, bf16[512,128]{1,0:T(8,128)(2,1)}, u32[]{:S(2)}) copy-start(bf16[512,128]{1,0:T(8,128)(2,1)} %local.5) | copy-start | bytes 393220
  29.3 18.2 %copy-start.4 = (bf16[4,512,128]{2,1,0:T(8,128)(2,1)S(1)}, bf16[4,512,128]{2,1,0:T(8,128)(2,1)}, u32[]{:S(2)}) copy-start(bf16[4,512,128]{2,1,0:T(8,128)(2,1)} %get-tuple-element.39.weights) | copy-start | bytes 1572868
  36.4 20.9 %copy-start.5 = (bf16[4,512,128]{2,1,0:T(8,128)(2,1)S(1)}, bf16[4,512,128]{2,1,0:T(8,128)(2,1)}, u32[]{:S(2)}) copy-start(bf16[4,512,128]{2,1,0:T(8,128)(2,1)} %get-tuple-element.42.weights) | copy-start | bytes 1572868
  36.5 20.9 %copy-start.6 = (bf16[512,128]{1,0:T(8,128)(2,1)S(1)}, bf16[512,128]{1,0:T(8,128)(2,1)}, u32[]{:S(2)}) copy-start(bf16[512,128]{1,0:T(8,128)(2,1)} %grad.3) | copy-start | bytes 393220
  48.0 14.1 %copy-start.8 = (s32[1,4]{1,0:T(1,128)S(1)}, s32[1,4]{1,0:T(1,128)}, u32[]{:S(2)}) copy-start(s32[1,4]{1,0:T(1,128)} %param.16) | copy-start | bytes 52
  58.6 12.1 %all-to-all-start.3 = ((bf16[4,512,128]{2,1,0:T(8,128)(2,1)}), bf16[4,512,128]{2,1,0:T(8,128)(2,1)S(1)}, u32[]{:S(2)}, u32[]{:S(2)}) async-start(bf16[4,512,128]{2,1,0:T(8,128)(2,1)} %get-tuple-element.48), calls=%async_computation.3 | async-start | bytes 1048576 | tf_op jit(solution)/shard_map/all_to_all | solution.py:295
  64.2 13.8 %collective-permute-start.1 = (bf16[256,1024]{1,0:T(8,128)(2,1)}, bf16[256,1024]{1,0:T(8,128)(2,1)}, u32[]{:S(2)}, u32[]{:S(2)}) collective-permute-start(bf16[256,1024]{1,0:T(8,128)(2,1)} %get-tuple-element.55), channel_id=1, source_target_pairs={{0,4},{4,0},{8,12},{12,8},{16,20},{20,16},{24,28},{28,24},{32,36},... | collective-permute-start | bytes 1572872 | tf_op jit(solution)/shard_map/ppermute | solution.py:299
  72.2 7.3 %collective-permute-start = (bf16[256,1024]{1,0:T(8,128)(2,1)S(1)}, bf16[256,1024]{1,0:T(8,128)(2,1)S(1)}, u32[]{:S(2)}, u32[]{:S(2)}) collective-permute-start(bf16[256,1024]{1,0:T(8,128)(2,1)S(1)} %get-tuple-element.53), channel_id=1, source_target_pairs={{0,4},{4,0},{8,12},{12,8},{16,20},{20,16},{24,28},{28,24},{32,36},... | collective-permute-start | bytes 1572872 | tf_op jit(solution)/shard_map/ppermute | solution.py:299
  142.2 5.4 %collective-permute-start.2 = (bf16[16,256,128]{2,1,0:T(8,128)(2,1)S(1)}, bf16[16,256,128]{2,1,0:T(8,128)(2,1)S(1)}, u32[]{:S(2)}, u32[]{:S(2)}) collective-permute-start(bf16[16,256,128]{2,1,0:T(8,128)(2,1)S(1)} %all_to_all.39.half), channel_id=1, source_target_pairs={{0,4},{4,0},{8,12},{12,8},{16,20},{20,16},{24,28},{28,24},{32,36},... | collective-permute-start | bytes 3145736 | tf_op jit(solution)/shard_map/ppermute | solution.py:299

commit v14 on v11

--- a/solution.py
+++ b/solution.py
@@ -263,7 +263,7 @@
         return (y * 8 + z) * 2 + core
 
     first = [
-        [device(core, line, pair * PAIR + i) for i in range(PAIR) for line in range(8)]
+        [device(core, line, pair * PAIR + i) for line in range(8) for i in range(PAIR)]
         for core in range(2)
         for pair in range(8 // PAIR)
     ]

time: 150 us -> 150 us (level)
  no operation moved by 1% of the time
where the time goes in v14:
time: 150 us
  blocking collectives  83.4 us (56%)
  starting transfers between devices  37.4 us (25%)
  Pallas kernels  15.8 us (11%)
  waiting for transfers between devices  7.41 us (5%)
  local copies, waits for them, and re-layouts  3.41 us (2%)
    all_to_all x3, blocking collectives, exchange(): lax.all_to_all(blocks, 'dom', split_axis=0, concat_axis=0, axis_index_gro...  62.9 us
    all_to_all x2, blocking collectives, across(): lax.all_to_all(blocks, 'rep', split_axis=0, concat_axis=0, tiled=True)  20.4 us
    all_to_all x1, starting transfers between devices, shards(): lax.all_to_all(rows_out, 'dom', split_axis=0, concat_axis=0, tiled=True)  18.4 us
    ppermute x3, starting transfers between devices, swap(): return lax.ppermute(rows, 'dom', [(p, p ^ 1) for p in range(128)])  15.5 us
    all_to_all x1, waiting for transfers between devices, shards(): lax.all_to_all(rows_out, 'dom', split_axis=0, concat_axis=0, tiled=True)  6.26 us
    pallas_call x1, Pallas kernels, shards(): call(choose_body, 'choose', [SMEM] + [FAR] * 2, [(chosen, BF)] * 2, [pltp...  3.68 us
    all_to_all x1, starting transfers between devices, across(): lax.all_to_all(blocks, 'rep', split_axis=0, concat_axis=0, tiled=True)  3.47 us
    unnamed x22, local copies, waits for them, and re-layouts  3.41 us
  transfers between devices with their start and end apart: 5, of which 3 were waited for; matrix products, arithmetic and copies ran while one was open for 1% of the time, Pallas kernels for 6%

profile of v14, /device:TPU:1, one launch (start us, length us, event | category | flops | bytes accessed | tf_op | source)
XLA Modules:
  0.0 149.8 jit_solution(11046540367110058860)
XLA Ops:
  0.6 2.3 %pick.1 = bf16[128,8,128]{2,1,0:T(8,128)(2,1)} custom-call(s32[4,128]{1,0:T(4,128)} %bitcast.21, bf16[512,128]{1,0:T(8,128)(2,1)} %feats.3, bf16[512,128]{1,0:T(8,128)(2,1)} %hist_far.1), custom_call_target="tpu_custom_call" | custom-call | tf_op jit(solution)/shard_map/pick/pallas_call | solution.py:306
  2.9 18.4 %all-to-all-start = ((bf16[128,8,128]{2,1,0:T(8,128)(2,1)}), bf16[128,8,128]{2,1,0:T(8,128)(2,1)S(1)}, u32[]{:S(2)}, u32[]{:S(2)}) async-start(bf16[128,8,128]{2,1,0:T(8,128)(2,1)} %pick.1), calls=%async_computation | async-start | bytes 524288 | tf_op jit(solution)/shard_map/all_to_all | solution.py:319
  21.4 0.9 copy-done
  22.3 0.9 copy-done.2
  23.2 0.9 copy-done.7
  24.1 0.7 copy-done.9
  24.8 0.9 ready.1
  25.6 3.7 %choose.1 = (bf16[4,512,128]{2,1,0:T(8,128)(2,1)}, bf16[4,512,128]{2,1,0:T(8,128)(2,1)}) custom-call(s32[4]{0:T(128)} %bitcast.12, bf16[512,8,128]{2,1,0:T(8,128)(2,1)} %w_one_far.1, bf16[512,8,128]{2,1,0:T(8,128)(2,1)} %w_two_far.1), custom_call_target="tpu_custom_call" | custom-call | tf_op jit(solution)/shard_map/choose/pallas_call | solution.py:323
  29.4 6.3 %all-to-all-done = bf16[128,8,128]{2,1,0:T(8,128)(2,1)S(1)} async-done(((bf16[128,8,128]{2,1,0:T(8,128)(2,1)}), bf16[128,8,128]{2,1,0:T(8,128)(2,1)S(1)}, u32[]{:S(2)}, u32[]{:S(2)}) %all-to-all-start) | async-done | bytes 262176 | tf_op jit(solution)/shard_map/all_to_all | solution.py:319
  35.6 0.8 gather.1
  36.5 11.1 %all_to_all.35.agg = bf16[4,512,128]{2,1,0:T(8,128)(2,1)S(1)} all-to-all(bf16[4,512,128]{2,1,0:T(8,128)(2,1)S(1)} %get-tuple-element.36), channel_id=1, replica_groups=mesh['dom'=128,'rep'=4] {'rep'}, dimensions={0} | all-to-all | bytes 1048576 | tf_op jit(solution)/shard_map/all_to_all | solution.py:286
  47.6 0.4 one.1
  48.0 9.3 %all_to_all.36.agg = bf16[4,512,128]{2,1,0:T(8,128)(2,1)S(1)} all-to-all(bf16[4,512,128]{2,1,0:T(8,128)(2,1)S(1)} %get-tuple-element.39), channel_id=1, replica_groups=mesh['dom'=128,'rep'=4] {'rep'}, dimensions={0} | all-to-all | bytes 1048576 | tf_op jit(solution)/shard_map/all_to_all | solution.py:286
  57.4 1.2 two.1
  58.6 3.5 %all-to-all-start.3 = ((bf16[4,512,128]{2,1,0:T(8,128)(2,1)}), bf16[4,512,128]{2,1,0:T(8,128)(2,1)S(1)}, u32[]{:S(2)}, u32[]{:S(2)}) async-start(bf16[4,512,128]{2,1,0:T(8,128)(2,1)} %get-tuple-element.46), calls=%async_computation.3 | async-start | bytes 1048576 | tf_op jit(solution)/shard_map/all_to_all | solution.py:286
  62.1 1.9 %grad_two.1 = (f32[256,1024]{1,0:T(8,128)S(1)}, bf16[256,1024]{1,0:T(8,128)(2,1)}, bf16[512,128]{1,0:T(8,128)(2,1)}, bf16[512,128]{1,0:T(8,128)(2,1)}) custom-call(s32[4]{0:T(128)S(1)} %bitcast.13, s32[1]{0:T(128)} %bitcast.1.core, bf16[4,512,128]{2,1,0:T(8,128)(2,1)S(1)} %all_to_all.36.agg, bf16[512,128]{1,0:T(8,128)(2,1)S(1)} %get-tuple-element.42.dz, ...), custom_call_target="tpu_custom_call" | custom-call | tf_op jit(solution)/shard_map/grad_two/pallas_call | solution.py:353
  64.0 6.3 %collective-permute-start.1 = (bf16[256,1024]{1,0:T(8,128)(2,1)}, bf16[256,1024]{1,0:T(8,128)(2,1)}, u32[]{:S(2)}, u32[]{:S(2)}) collective-permute-start(bf16[256,1024]{1,0:T(8,128)(2,1)} %get-tuple-element.51), channel_id=1, source_target_pairs={{0,4},{4,0},{8,12},{12,8},{16,20},{20,16},{24,28},{28,24},{32,36},... | collective-permute-start | bytes 1572872 | tf_op jit(solution)/shard_map/ppermute | solution.py:290
  70.4 1.5 back.1
  71.9 6.1 %collective-permute-start = (bf16[256,1024]{1,0:T(8,128)(2,1)S(1)}, bf16[256,1024]{1,0:T(8,128)(2,1)S(1)}, u32[]{:S(2)}, u32[]{:S(2)}) collective-permute-start(bf16[256,1024]{1,0:T(8,128)(2,1)S(1)} %get-tuple-element.49), channel_id=1, source_target_pairs={{0,4},{4,0},{8,12},{12,8},{16,20},{20,16},{24,28},{28,24},{32,36},... | collective-permute-start | bytes 1572872 | tf_op jit(solution)/shard_map/ppermute | solution.py:290
  78.0 1.2 add_convert_fusion
  79.2 0.3 collective-permute-done
  79.5 0.1 add_convert_fusion.1
  79.6 0.1 pad_maximum_fusion
  79.7 25.0 %all_to_all.37.parts = bf16[16,32,1024]{2,1,0:T(8,128)(2,1)S(1)} all-to-all(bf16[16,32,1024]{2,1,0:T(8,128)(2,1)S(1)} %pad_maximum_fusion), channel_id=1, replica_groups={{0,8,64,72,128,136,192,200,256,264,320,328,384,392,448,456},{16,24,80,8..., dimensions={0} | all-to-all | bytes 2097152 | tf_op jit(solution)/shard_map/all_to_all | solution.py:280
  104.7 0.1 first_sum.1
  104.9 14.4 %all_to_all.38.parts = bf16[4,32,1024]{2,1,0:T(8,128)(2,1)S(1)} all-to-all(bf16[4,32,1024]{2,1,0:T(8,128)(2,1)S(1)} %first_sum.1), channel_id=1, replica_groups={{0,16,32,48},{8,24,40,56},{64,80,96,112},{72,88,104,120},{128,144,160,1..., dimensions={0} | all-to-all | bytes 524288 | tf_op jit(solution)/shard_map/all_to_all | solution.py:280
  119.3 0.2 second_sum.1
  119.5 23.5 %all_to_all.39.half = bf16[16,256,128]{2,1,0:T(8,128)(2,1)S(1)} all-to-all(bf16[16,256,128]{2,1,0:T(8,128)(2,1)S(1)} %second_sum.1), channel_id=1, replica_groups={{0,8,64,72,128,136,192,200,256,264,320,328,384,392,448,456},{16,24,80,8..., dimensions={0} | all-to-all | bytes 2097152 | tf_op jit(solution)/shard_map/all_to_all | solution.py:280
  143.0 3.1 %collective-permute-start.2 = (bf16[16,256,128]{2,1,0:T(8,128)(2,1)S(1)}, bf16[16,256,128]{2,1,0:T(8,128)(2,1)S(1)}, u32[]{:S(2)}, u32[]{:S(2)}) collective-permute-start(bf16[16,256,128]{2,1,0:T(8,128)(2,1)S(1)} %all_to_all.39.half), channel_id=1, source_target_pairs={{0,4},{4,0},{8,12},{12,8},{16,20},{20,16},{24,28},{28,24},{32,36},... | collective-permute-start | bytes 3145736 | tf_op jit(solution)/shard_map/ppermute | solution.py:290
  146.1 1.4 widen_own.1
  147.5 0.8 collective-permute-done.2.half
  148.4 1.4 widen_other.1
  (20 shorter events, 0.1 us)
Async XLA Ops:
  0.6 35.0 %copy-start.10 = (s32[1,4]{1,0:T(1,128)S(1)}, s32[1,4]{1,0:T(1,128)}, u32[]{:S(2)}) copy-start(s32[1,4]{1,0:T(1,128)} %param.15) | copy-start | bytes 52
  2.9 32.7 %all-to-all-start = ((bf16[128,8,128]{2,1,0:T(8,128)(2,1)}), bf16[128,8,128]{2,1,0:T(8,128)(2,1)S(1)}, u32[]{:S(2)}, u32[]{:S(2)}) async-start(bf16[128,8,128]{2,1,0:T(8,128)(2,1)} %pick.1), calls=%async_computation | async-start | bytes 524288 | tf_op jit(solution)/shard_map/all_to_all | solution.py:319
  21.4 0.9 copy-start
  22.3 0.9 copy-start.2
  23.2 0.9 copy-start.7
  24.1 0.7 copy-start.9
  25.6 21.9 %copy-start.1 = (bf16[512,128]{1,0:T(8,128)(2,1)S(1)}, bf16[512,128]{1,0:T(8,128)(2,1)}, u32[]{:S(2)}) copy-start(bf16[512,128]{1,0:T(8,128)(2,1)} %feats.3) | copy-start | bytes 393220
  25.6 21.9 %copy-start.3 = (bf16[512,128]{1,0:T(8,128)(2,1)S(1)}, bf16[512,128]{1,0:T(8,128)(2,1)}, u32[]{:S(2)}) copy-start(bf16[512,128]{1,0:T(8,128)(2,1)} %local.5) | copy-start | bytes 393220
  29.3 18.2 %copy-start.4 = (bf16[4,512,128]{2,1,0:T(8,128)(2,1)S(1)}, bf16[4,512,128]{2,1,0:T(8,128)(2,1)}, u32[]{:S(2)}) copy-start(bf16[4,512,128]{2,1,0:T(8,128)(2,1)} %get-tuple-element.37.weights) | copy-start | bytes 1572868
  36.4 20.9 %copy-start.5 = (bf16[4,512,128]{2,1,0:T(8,128)(2,1)S(1)}, bf16[4,512,128]{2,1,0:T(8,128)(2,1)}, u32[]{:S(2)}) copy-start(bf16[4,512,128]{2,1,0:T(8,128)(2,1)} %get-tuple-element.40.weights) | copy-start | bytes 1572868
  36.5 20.9 %copy-start.6 = (bf16[512,128]{1,0:T(8,128)(2,1)S(1)}, bf16[512,128]{1,0:T(8,128)(2,1)}, u32[]{:S(2)}) copy-start(bf16[512,128]{1,0:T(8,128)(2,1)} %grad.3) | copy-start | bytes 393220
  48.0 14.1 %copy-start.8 = (s32[1,4]{1,0:T(1,128)S(1)}, s32[1,4]{1,0:T(1,128)}, u32[]{:S(2)}) copy-start(s32[1,4]{1,0:T(1,128)} %param.16) | copy-start | bytes 52
  58.6 11.8 %all-to-all-start.3 = ((bf16[4,512,128]{2,1,0:T(8,128)(2,1)}), bf16[4,512,128]{2,1,0:T(8,128)(2,1)S(1)}, u32[]{:S(2)}, u32[]{:S(2)}) async-start(bf16[4,512,128]{2,1,0:T(8,128)(2,1)} %get-tuple-element.46), calls=%async_computation.3 | async-start | bytes 1048576 | tf_op jit(solution)/shard_map/all_to_all | solution.py:286
  64.0 14.0 %collective-permute-start.1 = (bf16[256,1024]{1,0:T(8,128)(2,1)}, bf16[256,1024]{1,0:T(8,128)(2,1)}, u32[]{:S(2)}, u32[]{:S(2)}) collective-permute-start(bf16[256,1024]{1,0:T(8,128)(2,1)} %get-tuple-element.51), channel_id=1, source_target_pairs={{0,4},{4,0},{8,12},{12,8},{16,20},{20,16},{24,28},{28,24},{32,36},... | collective-permute-start | bytes 1572872 | tf_op jit(solution)/shard_map/ppermute | solution.py:290
  71.9 7.6 %collective-permute-start = (bf16[256,1024]{1,0:T(8,128)(2,1)S(1)}, bf16[256,1024]{1,0:T(8,128)(2,1)S(1)}, u32[]{:S(2)}, u32[]{:S(2)}) collective-permute-start(bf16[256,1024]{1,0:T(8,128)(2,1)S(1)} %get-tuple-element.49), channel_id=1, source_target_pairs={{0,4},{4,0},{8,12},{12,8},{16,20},{20,16},{24,28},{28,24},{32,36},... | collective-permute-start | bytes 1572872 | tf_op jit(solution)/shard_map/ppermute | solution.py:290
  143.0 5.4 %collective-permute-start.2 = (bf16[16,256,128]{2,1,0:T(8,128)(2,1)S(1)}, bf16[16,256,128]{2,1,0:T(8,128)(2,1)S(1)}, u32[]{:S(2)}, u32[]{:S(2)}) collective-permute-start(bf16[16,256,128]{2,1,0:T(8,128)(2,1)S(1)} %all_to_all.39.half), channel_id=1, source_target_pairs={{0,4},{4,0},{8,12},{12,8},{16,20},{20,16},{24,28},{28,24},{32,36},... | collective-permute-start | bytes 3145736 | tf_op jit(solution)/shard_map/ppermute | solution.py:290

commit v15 on v12

--- a/solution.py
+++ b/solution.py
@@ -186,11 +186,6 @@
     write_grad(types, core, agg, dz, keep, send, ((0,), (0,)))
 
 
-def turn_body(agg, turned):
-    for q in range(agg.shape[0]):
-        turned[q] = jnp.transpose(agg[q])
-
-
 def back_body(types, core, parts, local, grad, slope, agg, keep, send, dz):
     rows = range(types.shape[0])
     totals = []
@@ -203,7 +198,7 @@
     for j in rows:
         dh = grad[block(j), :].astype(F32) + terms[j]
         dz[block(j), :] = (dh * slope[block(j), :]).astype(BF)
-    write_grad(types, core, agg, dz, keep, send, ((1,), (0,)))
+    write_grad(types, core, agg, dz, keep, send, ((0,), (0,)))
 
 
 def add_up(parts):
@@ -363,15 +358,13 @@
         [SMEM] * 2 + [VMEM] * 4,
         [(half, F32), (half, BF), (flat, BF), (flat, BF)],
     )(types, core, agg_two, dz_two, near_one, near_two)
-    agg_one, keep_two = lax.optimization_barrier((agg_one, keep_two))
-    (turned,) = call(turn_body, "turn", [VMEM], [((REPS, cols, nodes), BF)])(agg_one)
     keep_one, send_one = call(
         back_body,
         "back",
         [SMEM] * 2 + [VMEM] * 5,
         [(half, F32), (half, BF)],
         [pltpu.VMEM(flat, BF)],
-    )(types, core, back, local_val, grad_out, slope, turned)
+    )(types, core, back, local_val, grad_out, slope, agg_one)
     pair_one = (keep_one + swap(send_one).astype(F32)).astype(BF)
     pair_two = (keep_two + swap(send_two).astype(F32)).astype(BF)
 

time: 150 us -> 150 us (level)
  no operation moved by 1% of the time
where the time goes in v15:
time: 150 us; the launch traced here: 149 us
  blocking collectives  82.6 us (55%)
  starting transfers between devices  37.5 us (25%)
  Pallas kernels  15.8 us (11%)
  waiting for transfers between devices  7.41 us (5%)
  local copies, waits for them, and re-layouts  3.41 us (2%)
    all_to_all x3, blocking collectives, exchange(): lax.all_to_all(blocks, 'dom', split_axis=0, concat_axis=0, axis_index_gro...  62.2 us
    all_to_all x2, blocking collectives, across(): lax.all_to_all(blocks, 'rep', split_axis=0, concat_axis=0, tiled=True)  20.4 us
    all_to_all x1, starting transfers between devices, shards(): lax.all_to_all(rows_out, 'dom', split_axis=0, concat_axis=0, tiled=True)  18.4 us
    ppermute x3, starting transfers between devices, swap(): return lax.ppermute(rows, 'dom', [(p, p ^ 1) for p in range(128)])  15.6 us
    all_to_all x1, waiting for transfers between devices, shards(): lax.all_to_all(rows_out, 'dom', split_axis=0, concat_axis=0, tiled=True)  6.26 us
    pallas_call x1, Pallas kernels, shards(): call(choose_body, 'choose', [SMEM] + [FAR] * 2, [(chosen, BF)] * 2, [pltp...  3.68 us
    all_to_all x1, starting transfers between devices, across(): lax.all_to_all(blocks, 'rep', split_axis=0, concat_axis=0, tiled=True)  3.47 us
    unnamed x22, local copies, waits for them, and re-layouts  3.41 us
  transfers between devices with their start and end apart: 5, of which 3 were waited for; matrix products, arithmetic and copies ran while one was open for 1% of the time, Pallas kernels for 6%

profile of v15, /device:TPU:1, one launch (start us, length us, event | category | flops | bytes accessed | tf_op | source)
XLA Modules:
  0.0 149.0 jit_solution(13743689950786959758)
XLA Ops:
  0.6 2.3 %pick.1 = bf16[128,8,128]{2,1,0:T(8,128)(2,1)} custom-call(s32[4,128]{1,0:T(4,128)} %bitcast.21, bf16[512,128]{1,0:T(8,128)(2,1)} %feats.3, bf16[512,128]{1,0:T(8,128)(2,1)} %hist_far.1), custom_call_target="tpu_custom_call" | custom-call | tf_op jit(solution)/shard_map/pick/pallas_call | solution.py:308
  2.9 18.4 %all-to-all-start = ((bf16[128,8,128]{2,1,0:T(8,128)(2,1)}), bf16[128,8,128]{2,1,0:T(8,128)(2,1)S(1)}, u32[]{:S(2)}, u32[]{:S(2)}) async-start(bf16[128,8,128]{2,1,0:T(8,128)(2,1)} %pick.1), calls=%async_computation | async-start | bytes 524288 | tf_op jit(solution)/shard_map/all_to_all | solution.py:321
  21.4 0.9 copy-done
  22.3 0.9 copy-done.2
  23.2 0.9 copy-done.7
  24.1 0.7 copy-done.9
  24.8 0.9 ready.1
  25.6 3.7 %choose.1 = (bf16[4,512,128]{2,1,0:T(8,128)(2,1)}, bf16[4,512,128]{2,1,0:T(8,128)(2,1)}) custom-call(s32[4]{0:T(128)} %bitcast.12, bf16[512,8,128]{2,1,0:T(8,128)(2,1)} %w_one_far.1, bf16[512,8,128]{2,1,0:T(8,128)(2,1)} %w_two_far.1), custom_call_target="tpu_custom_call" | custom-call | tf_op jit(solution)/shard_map/choose/pallas_call | solution.py:325
  29.4 6.3 %all-to-all-done = bf16[128,8,128]{2,1,0:T(8,128)(2,1)S(1)} async-done(((bf16[128,8,128]{2,1,0:T(8,128)(2,1)}), bf16[128,8,128]{2,1,0:T(8,128)(2,1)S(1)}, u32[]{:S(2)}, u32[]{:S(2)}) %all-to-all-start) | async-done | bytes 262176 | tf_op jit(solution)/shard_map/all_to_all | solution.py:321
  35.6 0.8 gather.1
  36.5 11.1 %all_to_all.35.agg = bf16[4,512,128]{2,1,0:T(8,128)(2,1)S(1)} all-to-all(bf16[4,512,128]{2,1,0:T(8,128)(2,1)S(1)} %get-tuple-element.36), channel_id=1, replica_groups=mesh['dom'=128,'rep'=4] {'rep'}, dimensions={0} | all-to-all | bytes 1048576 | tf_op jit(solution)/shard_map/all_to_all | solution.py:288
  47.6 0.4 one.1
  48.0 9.3 %all_to_all.36.agg = bf16[4,512,128]{2,1,0:T(8,128)(2,1)S(1)} all-to-all(bf16[4,512,128]{2,1,0:T(8,128)(2,1)S(1)} %get-tuple-element.39), channel_id=1, replica_groups=mesh['dom'=128,'rep'=4] {'rep'}, dimensions={0} | all-to-all | bytes 1048576 | tf_op jit(solution)/shard_map/all_to_all | solution.py:288
  57.4 1.2 two.1
  58.6 3.5 %all-to-all-start.3 = ((bf16[4,512,128]{2,1,0:T(8,128)(2,1)}), bf16[4,512,128]{2,1,0:T(8,128)(2,1)S(1)}, u32[]{:S(2)}, u32[]{:S(2)}) async-start(bf16[4,512,128]{2,1,0:T(8,128)(2,1)} %get-tuple-element.46), calls=%async_computation.3 | async-start | bytes 1048576 | tf_op jit(solution)/shard_map/all_to_all | solution.py:288
  62.1 1.9 %grad_two.1 = (f32[256,1024]{1,0:T(8,128)S(1)}, bf16[256,1024]{1,0:T(8,128)(2,1)}, bf16[512,128]{1,0:T(8,128)(2,1)}, bf16[512,128]{1,0:T(8,128)(2,1)}) custom-call(s32[4]{0:T(128)S(1)} %bitcast.13, s32[1]{0:T(128)} %bitcast.1.core, bf16[4,512,128]{2,1,0:T(8,128)(2,1)S(1)} %all_to_all.36.agg, bf16[512,128]{1,0:T(8,128)(2,1)S(1)} %get-tuple-element.42.dz, ...), custom_call_target="tpu_custom_call" | custom-call | tf_op jit(solution)/shard_map/grad_two/pallas_call | solution.py:355
  64.0 6.3 %collective-permute-start.1 = (bf16[256,1024]{1,0:T(8,128)(2,1)}, bf16[256,1024]{1,0:T(8,128)(2,1)}, u32[]{:S(2)}, u32[]{:S(2)}) collective-permute-start(bf16[256,1024]{1,0:T(8,128)(2,1)} %get-tuple-element.51), channel_id=1, source_target_pairs={{0,4},{4,0},{8,12},{12,8},{16,20},{20,16},{24,28},{28,24},{32,36},... | collective-permute-start | bytes 1572872 | tf_op jit(solution)/shard_map/ppermute | solution.py:292
  70.4 1.5 back.1
  71.8 6.1 %collective-permute-start = (bf16[256,1024]{1,0:T(8,128)(2,1)S(1)}, bf16[256,1024]{1,0:T(8,128)(2,1)S(1)}, u32[]{:S(2)}, u32[]{:S(2)}) collective-permute-start(bf16[256,1024]{1,0:T(8,128)(2,1)S(1)} %get-tuple-element.49), channel_id=1, source_target_pairs={{0,4},{4,0},{8,12},{12,8},{16,20},{20,16},{24,28},{28,24},{32,36},... | collective-permute-start | bytes 1572872 | tf_op jit(solution)/shard_map/ppermute | solution.py:292
  78.0 1.2 add_convert_fusion
  79.2 0.3 collective-permute-done
  79.5 0.1 add_convert_fusion.1
  79.6 0.1 pad_maximum_fusion
  79.7 25.5 %all_to_all.37.parts = bf16[16,32,1024]{2,1,0:T(8,128)(2,1)S(1)} all-to-all(bf16[16,32,1024]{2,1,0:T(8,128)(2,1)S(1)} %pad_maximum_fusion), channel_id=1, replica_groups={{0,64,128,192,256,320,384,448,8,72,136,200,264,328,392,456},{16,80,144,..., dimensions={0} | all-to-all | bytes 2097152 | tf_op jit(solution)/shard_map/all_to_all | solution.py:282
  105.2 0.1 first_sum.1
  105.3 11.6 %all_to_all.38.parts = bf16[4,32,1024]{2,1,0:T(8,128)(2,1)S(1)} all-to-all(bf16[4,32,1024]{2,1,0:T(8,128)(2,1)S(1)} %first_sum.1), channel_id=1, replica_groups={{0,16,32,48},{8,24,40,56},{64,80,96,112},{72,88,104,120},{128,144,160,1..., dimensions={0} | all-to-all | bytes 524288 | tf_op jit(solution)/shard_map/all_to_all | solution.py:282
  117.0 0.2 second_sum.1
  117.2 25.1 %all_to_all.39.half = bf16[16,256,128]{2,1,0:T(8,128)(2,1)S(1)} all-to-all(bf16[16,256,128]{2,1,0:T(8,128)(2,1)S(1)} %second_sum.1), channel_id=1, replica_groups={{0,64,128,192,256,320,384,448,8,72,136,200,264,328,392,456},{16,80,144,..., dimensions={0} | all-to-all | bytes 2097152 | tf_op jit(solution)/shard_map/all_to_all | solution.py:282
  142.2 3.1 %collective-permute-start.2 = (bf16[16,256,128]{2,1,0:T(8,128)(2,1)S(1)}, bf16[16,256,128]{2,1,0:T(8,128)(2,1)S(1)}, u32[]{:S(2)}, u32[]{:S(2)}) collective-permute-start(bf16[16,256,128]{2,1,0:T(8,128)(2,1)S(1)} %all_to_all.39.half), channel_id=1, source_target_pairs={{0,4},{4,0},{8,12},{12,8},{16,20},{20,16},{24,28},{28,24},{32,36},... | collective-permute-start | bytes 3145736 | tf_op jit(solution)/shard_map/ppermute | solution.py:292
  145.4 1.4 widen_own.1
  146.8 0.8 collective-permute-done.2.half
  147.6 1.4 widen_other.1
  (20 shorter events, 0.1 us)
Async XLA Ops:
  0.6 35.0 %copy-start.10 = (s32[1,4]{1,0:T(1,128)S(1)}, s32[1,4]{1,0:T(1,128)}, u32[]{:S(2)}) copy-start(s32[1,4]{1,0:T(1,128)} %param.15) | copy-start | bytes 52
  2.9 32.7 %all-to-all-start = ((bf16[128,8,128]{2,1,0:T(8,128)(2,1)}), bf16[128,8,128]{2,1,0:T(8,128)(2,1)S(1)}, u32[]{:S(2)}, u32[]{:S(2)}) async-start(bf16[128,8,128]{2,1,0:T(8,128)(2,1)} %pick.1), calls=%async_computation | async-start | bytes 524288 | tf_op jit(solution)/shard_map/all_to_all | solution.py:321
  21.4 0.9 copy-start
  22.3 0.9 copy-start.2
  23.2 0.9 copy-start.7
  24.1 0.7 copy-start.9
  25.6 21.9 %copy-start.1 = (bf16[512,128]{1,0:T(8,128)(2,1)S(1)}, bf16[512,128]{1,0:T(8,128)(2,1)}, u32[]{:S(2)}) copy-start(bf16[512,128]{1,0:T(8,128)(2,1)} %feats.3) | copy-start | bytes 393220
  25.6 21.9 %copy-start.3 = (bf16[512,128]{1,0:T(8,128)(2,1)S(1)}, bf16[512,128]{1,0:T(8,128)(2,1)}, u32[]{:S(2)}) copy-start(bf16[512,128]{1,0:T(8,128)(2,1)} %local.5) | copy-start | bytes 393220
  29.3 18.2 %copy-start.4 = (bf16[4,512,128]{2,1,0:T(8,128)(2,1)S(1)}, bf16[4,512,128]{2,1,0:T(8,128)(2,1)}, u32[]{:S(2)}) copy-start(bf16[4,512,128]{2,1,0:T(8,128)(2,1)} %get-tuple-element.37.weights) | copy-start | bytes 1572868
  36.4 20.9 %copy-start.5 = (bf16[4,512,128]{2,1,0:T(8,128)(2,1)S(1)}, bf16[4,512,128]{2,1,0:T(8,128)(2,1)}, u32[]{:S(2)}) copy-start(bf16[4,512,128]{2,1,0:T(8,128)(2,1)} %get-tuple-element.40.weights) | copy-start | bytes 1572868
  36.5 20.9 %copy-start.6 = (bf16[512,128]{1,0:T(8,128)(2,1)S(1)}, bf16[512,128]{1,0:T(8,128)(2,1)}, u32[]{:S(2)}) copy-start(bf16[512,128]{1,0:T(8,128)(2,1)} %grad.3) | copy-start | bytes 393220
  48.0 14.1 %copy-start.8 = (s32[1,4]{1,0:T(1,128)S(1)}, s32[1,4]{1,0:T(1,128)}, u32[]{:S(2)}) copy-start(s32[1,4]{1,0:T(1,128)} %param.16) | copy-start | bytes 52
  58.6 11.8 %all-to-all-start.3 = ((bf16[4,512,128]{2,1,0:T(8,128)(2,1)}), bf16[4,512,128]{2,1,0:T(8,128)(2,1)S(1)}, u32[]{:S(2)}, u32[]{:S(2)}) async-start(bf16[4,512,128]{2,1,0:T(8,128)(2,1)} %get-tuple-element.46), calls=%async_computation.3 | async-start | bytes 1048576 | tf_op jit(solution)/shard_map/all_to_all | solution.py:288
  64.0 13.9 %collective-permute-start.1 = (bf16[256,1024]{1,0:T(8,128)(2,1)}, bf16[256,1024]{1,0:T(8,128)(2,1)}, u32[]{:S(2)}, u32[]{:S(2)}) collective-permute-start(bf16[256,1024]{1,0:T(8,128)(2,1)} %get-tuple-element.51), channel_id=1, source_target_pairs={{0,4},{4,0},{8,12},{12,8},{16,20},{20,16},{24,28},{28,24},{32,36},... | collective-permute-start | bytes 1572872 | tf_op jit(solution)/shard_map/ppermute | solution.py:292
  71.8 7.6 %collective-permute-start = (bf16[256,1024]{1,0:T(8,128)(2,1)S(1)}, bf16[256,1024]{1,0:T(8,128)(2,1)S(1)}, u32[]{:S(2)}, u32[]{:S(2)}) collective-permute-start(bf16[256,1024]{1,0:T(8,128)(2,1)S(1)} %get-tuple-element.49), channel_id=1, source_target_pairs={{0,4},{4,0},{8,12},{12,8},{16,20},{20,16},{24,28},{28,24},{32,36},... | collective-permute-start | bytes 1572872 | tf_op jit(solution)/shard_map/ppermute | solution.py:292
  142.2 5.4 %collective-permute-start.2 = (bf16[16,256,128]{2,1,0:T(8,128)(2,1)S(1)}, bf16[16,256,128]{2,1,0:T(8,128)(2,1)S(1)}, u32[]{:S(2)}, u32[]{:S(2)}) collective-permute-start(bf16[16,256,128]{2,1,0:T(8,128)(2,1)S(1)} %all_to_all.39.half), channel_id=1, source_target_pairs={{0,4},{4,0},{8,12},{12,8},{16,20},{20,16},{24,28},{28,24},{32,36},... | collective-permute-start | bytes 3145736 | tf_op jit(solution)/shard_map/ppermute | solution.py:292
